TPU v7x, 32 devices: a whole 2x2x4 slice. The times are simulated.
32 devices in a mesh: dp: 8 (over y, x, core), tensor: 4 (over z).
Axes of the slice: x: 2, y: 2, z: 4, core: 2. Of those that a mesh axis runs over, the one named last changes fastest.
Arguments:
- tokens: bfloat16 [16384, 768], P(('dp', 'tensor')), may hold values from -6 to 6
- cotangent: bfloat16 [16384, 768], P(('dp', 'tensor')), may hold values from -6 to 6
- deal: int32 [16384], P(('dp', 'tensor')), may hold values from 0 to 7, as said below
- lengths: int32 [8, 8], P('dp'), may hold values from 1 to 1024, 2048 in all within a row
- routes: int32 [16384, 2], P('dp'), may hold values from 0 to 11, all different within a row; in each aligned block of 2048 rows (0 to 2047, 2048 to 4095, ...) at most 512 rows name the same one
- gate_residual: float32 [16384, 12], P(('dp', 'tensor')), may hold values from -4 to 4
- w_qkv: bfloat16 [768, 3, 768], P('dp', None, 'tensor'), may hold values from -0.21875 to 0.21875
- w_out: bfloat16 [768, 768], P('dp', 'tensor'), may hold values from -1.25 to 1.25
- w_gate_up: bfloat16 [768, 8, 2, 2048], P('dp', None, None, 'tensor'), may hold values from -0.21875 to 0.21875
- w_down: bfloat16 [768, 8, 2048], P('dp', None, 'tensor'), may hold values from -0.25 to 0.25
- norm_gain_attn: float32 [768], replicated, may hold values from 0.1 to 1.9
- norm_gain_moe: float32 [768], replicated, may hold values from 0.1 to 1.9
- w_router: float32 [768, 12], replicated, may hold values from -0.15625 to 0.15625
- w_const: float32 [2, 768, 2], replicated, may hold values from -0.21875 to 0.21875
- v_const: float32 [2, 768], replicated, may hold values from -5 to 5
Outputs:
- output: bfloat16 [16384, 768], P(('dp', 'tensor'))
- grad_tokens: bfloat16 [16384, 768], P(('dp', 'tensor'))
- grad_residual: float32 [16384, 12], P(('dp', 'tensor'))
- grad_qkv: float32 [768, 3, 768], P('dp', None, 'tensor')
- grad_out: float32 [768, 768], P('dp', 'tensor')
- grad_gate_up: float32 [768, 8, 2, 2048], P('dp', None, None, 'tensor')
- grad_down: float32 [768, 8, 2048], P('dp', None, 'tensor')
- grad_gain_attn: float32 [768], replicated
- grad_gain_moe: float32 [768], replicated
- grad_router: float32 [768, 12], replicated
- grad_const: float32 [2, 768, 2], replicated
- grad_vconst: float32 [2, 768], replicated
Inputs may be any that keep to these rules, and one draw needn't show every extreme that they name: `deal`: every device deals exactly 64 of its tokens to each index of dp. Each row of a group's lengths sums to 2048; its largest is 1024. `routes`: A row names two different experts: 0 to 7 feed-forward, 8 zero, 9 copy, 10 and 11 constant. In the 2048 rows of one token group no expert is named by more than 512 rows, a bound that some block reaches.
All inputs are finite; a program needn't handle non-finite values.
Results may differ from a plain program's by a relative error of at most 0.02.
Values may be sent and summed in bfloat16 or wider, within the bound.
A program may use at most 256 MiB of HBM per device.

v0:
```python
import math

import jax
import jax.numpy as jnp
from jax import lax
from jax.sharding import PartitionSpec as P

D = 768
HEAD_DIM = 64
EXPERTS = 8


PRECISE = lax.Precision.HIGHEST
EPSILON = 1e-06
MASKED_SCORE = -1e30


def rms_norm(values, gain):
    return values * lax.rsqrt(jnp.mean(values * values, axis=-1, keepdims=True) + EPSILON) * gain


def rotate(values, cosine, sine):
    half_dim = values.shape[-1] // 2
    turned = jnp.concatenate([-values[..., half_dim:], values[..., :half_dim]], axis=-1)
    return values * cosine + turned * sine


def rotate_back(grad_in, cosine, sine):
    half_dim = grad_in.shape[-1] // 2
    scaled = grad_in * sine
    return grad_in * cosine + jnp.concatenate(
        [scaled[..., half_dim:], -scaled[..., :half_dim]], axis=-1
    )


def positions(seq_lengths, total_rows):
    finish = jnp.cumsum(seq_lengths)
    row_ids = jnp.arange(total_rows, dtype=jnp.int32)
    segment = jnp.sum((row_ids[:, None] >= finish[None, :]).astype(jnp.int32), axis=1)
    begins = finish - seq_lengths
    select = segment[:, None] == jnp.arange(seq_lengths.shape[0], dtype=jnp.int32)[None, :]
    opening = jnp.sum(jnp.where(select, begins[None, :], 0), axis=1)
    return (segment, row_ids - opening)


def rope_tables(place):
    half_dim = HEAD_DIM // 2
    rates = jnp.exp(jnp.arange(half_dim, dtype=jnp.float32) * (-2.0 * math.log(10000.0) / HEAD_DIM))
    angles = place.astype(jnp.float32)[:, None] * rates[None, :]
    cosine = jnp.concatenate([jnp.cos(angles), jnp.cos(angles)], axis=-1)[:, None, :]
    sine = jnp.concatenate([jnp.sin(angles), jnp.sin(angles)], axis=-1)[:, None, :]
    return (cosine, sine)


def expert_tables(route, expert_count, capacity):
    flat_ids = route.reshape(-1)
    entries = flat_ids.shape[0]
    hit_table = (flat_ids[:, None] == jnp.arange(expert_count, dtype=jnp.int32)[None, :]).astype(
        jnp.int32
    )
    rank_in = jnp.cumsum(hit_table, axis=0) - 1
    slot_in = jnp.sum(hit_table * rank_in, axis=1)
    routed = jnp.sum(hit_table, axis=1) > 0
    entry_slot = jnp.where(routed, flat_ids * capacity + slot_in, expert_count * capacity)
    slot_owner = (
        jnp.zeros((expert_count * capacity + 1,), jnp.int32)
        .at[entry_slot]
        .set(jnp.arange(entries, dtype=jnp.int32))[:-1]
    )
    filled = jnp.zeros((expert_count * capacity + 1,), jnp.float32).at[entry_slot].set(1.0)[:-1]
    return (entry_slot, slot_owner, filled)


def router(normed, residual, router_weight, route):
    logits = jnp.dot(normed, router_weight, precision=PRECISE) + residual
    choose = route[:, :, None] == jnp.arange(router_weight.shape[1], dtype=jnp.int32)[None, None, :]
    picked = jnp.sum(jnp.where(choose, logits[:, None, :], 0.0), axis=-1)
    return jax.nn.softmax(picked, axis=-1)


def local_experts(normed, gates, route, const_weight, const_vector):
    mixing = jax.nn.softmax(
        jnp.einsum("nd,cdj->ncj", normed, const_weight, precision=PRECISE), axis=-1
    )
    constant = mixing[:, :, 0:1] * normed[:, None, :] + mixing[:, :, 1:2] * const_vector[None, :, :]
    copy_weight = jnp.sum(jnp.where(route == EXPERTS + 1, gates, 0.0), axis=1)
    const_first = jnp.sum(jnp.where(route == EXPERTS + 2, gates, 0.0), axis=1)
    const_second = jnp.sum(jnp.where(route == EXPERTS + 3, gates, 0.0), axis=1)
    return (
        copy_weight[:, None] * normed
        + const_first[:, None] * constant[:, 0]
        + const_second[:, None] * constant[:, 1]
    )


def body(
    tokens,
    cotangent,
    deal,
    lengths,
    routes,
    gate_residual,
    w_qkv,
    w_out,
    w_gate_up,
    w_down,
    norm_gain_attn,
    norm_gain_moe,
    w_router,
    w_const,
    v_const,
):
    tok_rows = tokens.shape[0]
    group = tok_rows * lax.axis_size("tensor")
    capacity = group // 4
    local_ids = jnp.arange(tok_rows, dtype=jnp.int32)
    order = jnp.argsort(deal * tok_rows + local_ids)
    arrived, incoming = (
        lax.all_to_all(tokens[order], "dp", split_axis=0, concat_axis=0, tiled=True),
        lax.all_to_all(cotangent[order], "dp", split_axis=0, concat_axis=0, tiled=True),
    )
    wqkv, wout, wgu, wdown = (
        lax.all_gather(w_qkv, "dp", axis=0, tiled=True),
        lax.all_gather(w_out, "dp", axis=0, tiled=True),
        lax.all_gather(w_gate_up, "dp", axis=0, tiled=True),
        lax.all_gather(w_down, "dp", axis=0, tiled=True),
    )
    heads_here = wqkv.shape[2] // HEAD_DIM
    width_here = heads_here * HEAD_DIM
    segment, place = positions(lengths[0], group)
    cosine, sine = rope_tables(place)
    scale = HEAD_DIM ** (-0.5)
    x_start = arrived.astype(jnp.float32)
    normed_attn = rms_norm(x_start, norm_gain_attn).astype(jnp.bfloat16)
    all_normed = lax.all_gather(normed_attn, "tensor", axis=0, tiled=True)
    qkv = jnp.einsum("nd,dcm->ncm", all_normed, wqkv, preferred_element_type=jnp.float32)
    split = qkv.reshape(group, 3, heads_here, HEAD_DIM)
    query = rotate(split[:, 0], cosine, sine).astype(jnp.bfloat16)
    keys = rotate(split[:, 1], cosine, sine).astype(jnp.bfloat16)
    values = split[:, 2].astype(jnp.bfloat16)
    block = min(512, group)
    row_ids = jnp.arange(group, dtype=jnp.int32)
    starts = jnp.arange(group // block, dtype=jnp.int32) * block

    def scores(start):
        query_rows = lax.dynamic_slice_in_dim(query, start, block, 0)
        seg_rows = lax.dynamic_slice_in_dim(segment, start, block, 0)
        row_here = start + jnp.arange(block, dtype=jnp.int32)
        score = (
            jnp.einsum("qhd,khd->hqk", query_rows, keys, preferred_element_type=jnp.float32) * scale
        )
        allowed = (seg_rows[:, None] == segment[None, :]) & (row_ids[None, :] <= row_here[:, None])
        return (query_rows, jnp.where(allowed[None], score, MASKED_SCORE), allowed)

    def forward_block(start):
        query_rows, score, allowed = scores(start)
        top_score = jnp.max(score, axis=-1, keepdims=True)
        raised = jnp.exp(score - top_score)
        total = jnp.sum(raised, axis=-1, keepdims=True)
        weight = (raised / total).astype(jnp.bfloat16)
        mixed_rows = jnp.einsum("hqk,khd->qhd", weight, values, preferred_element_type=jnp.float32)
        return (mixed_rows, (top_score + jnp.log(total))[..., 0])

    mixed, log_totals = lax.map(forward_block, starts)
    mixed = mixed.reshape(group, width_here).astype(jnp.bfloat16)
    rows_here = mixed
    attended = lax.psum_scatter(
        lax.dot_general(
            rows_here, wout, (((1,), (1,)), ((), ())), preferred_element_type=jnp.float32
        ).astype(jnp.bfloat16),
        "tensor",
        scatter_dimension=0,
        tiled=True,
    ).astype(jnp.float32)
    x_mid = x_start + attended
    normed_moe = rms_norm(x_mid, norm_gain_moe).astype(jnp.bfloat16)
    normed_f = normed_moe.astype(jnp.float32)
    mine = lax.dynamic_slice_in_dim(routes, lax.axis_index("tensor") * tok_rows, tok_rows, 0)
    gates_f = router(normed_f, gate_residual, w_router, mine)
    gates_b = gates_f.astype(jnp.bfloat16)
    gates_r = gates_b.astype(jnp.float32)
    local = local_experts(normed_f, gates_r, mine, w_const, v_const)
    all_moe, all_gates, all_grad = (
        lax.all_gather(normed_moe, "tensor", axis=0, tiled=True),
        lax.all_gather(gates_b, "tensor", axis=0, tiled=True),
        lax.all_gather(incoming, "tensor", axis=0, tiled=True),
    )
    entry_slot, slot_owner, filled = expert_tables(routes, EXPERTS, capacity)
    slot_rows = slot_owner // 2
    inputs = all_moe[slot_rows].reshape(EXPERTS, capacity, D)
    projected = jnp.einsum("ecd,dejf->ecjf", inputs, wgu, preferred_element_type=jnp.float32)
    gate_part = projected[:, :, 0]
    up_part = projected[:, :, 1]
    activated = (jax.nn.silu(gate_part) * up_part).astype(jnp.bfloat16)
    produced = jnp.einsum("ecf,def->ecd", activated, wdown, preferred_element_type=jnp.float32)
    flat_produced = produced.reshape(EXPERTS * capacity, D)
    table = jnp.concatenate([flat_produced, jnp.zeros((1, D), jnp.float32)], axis=0)
    gate_entries = all_gates.reshape(-1).astype(jnp.float32)
    routed_part = jnp.sum((table[entry_slot] * gate_entries[:, None]).reshape(group, 2, D), axis=1)
    routed = lax.psum_scatter(
        routed_part.astype(jnp.bfloat16), "tensor", scatter_dimension=0, tiled=True
    ).astype(jnp.float32)
    result = (x_mid + routed + local).astype(jnp.bfloat16)
    grad_rows = incoming.astype(jnp.float32)
    slot_grad = all_grad[slot_rows].astype(jnp.float32)
    slot_gate = gate_entries[slot_owner] * filled
    d_produced = (slot_grad * slot_gate[:, None]).astype(jnp.bfloat16).reshape(EXPERTS, capacity, D)
    gate_slot_grad = jnp.sum(slot_grad * flat_produced, axis=-1) * filled
    d_activated = jnp.einsum("ecd,def->ecf", d_produced, wdown, preferred_element_type=jnp.float32)
    grad_down = jnp.einsum(
        "ecf,ecd->def", activated, d_produced, preferred_element_type=jnp.float32
    )
    sigmoid_gate = jax.nn.sigmoid(gate_part)
    d_gate = d_activated * up_part * sigmoid_gate * (1.0 + gate_part * (1.0 - sigmoid_gate))
    d_up = d_activated * gate_part * sigmoid_gate
    d_projected = jnp.stack([d_gate, d_up], axis=2).astype(jnp.bfloat16)
    d_inputs = jnp.einsum("ecjf,dejf->ecd", d_projected, wgu, preferred_element_type=jnp.float32)
    grad_gate_up = jnp.einsum(
        "ecd,ecjf->dejf", inputs, d_projected, preferred_element_type=jnp.float32
    )
    d_table = jnp.concatenate(
        [d_inputs.reshape(EXPERTS * capacity, D), jnp.zeros((1, D), jnp.float32)], axis=0
    )
    d_normed_part = jnp.sum(d_table[entry_slot].reshape(group, 2, D), axis=1)
    gate_grad_part = jnp.concatenate([gate_slot_grad, jnp.zeros((1,), jnp.float32)], axis=0)[
        entry_slot
    ].reshape(group, 2)
    d_normed_ff, d_gates_ff = (
        lax.psum_scatter(
            d_normed_part.astype(jnp.bfloat16), "tensor", scatter_dimension=0, tiled=True
        ).astype(jnp.float32),
        lax.psum_scatter(
            gate_grad_part.astype(jnp.bfloat16), "tensor", scatter_dimension=0, tiled=True
        ).astype(jnp.float32),
    )
    _, local_back = jax.vjp(
        lambda normed_in, gates_in, weight_in, vector_in: local_experts(
            normed_in, gates_in, mine, weight_in, vector_in
        ),
        normed_f,
        gates_r,
        w_const,
        v_const,
    )
    d_normed_local, d_gates_local, grad_const, grad_vconst = local_back(grad_rows)
    _, router_back = jax.vjp(
        lambda normed_in, residual_in, weight_in: router(normed_in, residual_in, weight_in, mine),
        normed_f,
        gate_residual,
        w_router,
    )
    d_normed_router, grad_residual, grad_router = router_back(d_gates_ff + d_gates_local)
    d_normed_moe = d_normed_ff + d_normed_local + d_normed_router
    _, norm_moe_back = jax.vjp(rms_norm, x_mid, norm_gain_moe)
    d_mid_norm, grad_gain_moe = norm_moe_back(d_normed_moe)
    d_mid = grad_rows + d_mid_norm
    all_d_mid = lax.all_gather(d_mid.astype(jnp.bfloat16), "tensor", axis=0, tiled=True)
    d_mixed = (
        jnp.dot(all_d_mid, wout, preferred_element_type=jnp.float32)
        .astype(jnp.bfloat16)
        .reshape(group, heads_here, HEAD_DIM)
    )
    grad_out = lax.dot_general(
        all_d_mid, mixed, (((0,), (0,)), ((), ())), preferred_element_type=jnp.float32
    )

    def backward_block(carry, item):
        d_keys, d_values = carry
        start, log_total = item
        query_rows, score, allowed = scores(start)
        prob = jnp.where(allowed[None], jnp.exp(score - log_total[..., None]), 0.0)
        d_rows = lax.dynamic_slice_in_dim(d_mixed, start, block, 0)
        d_prob = jnp.einsum("qhd,khd->hqk", d_rows, values, preferred_element_type=jnp.float32)
        inner = jnp.sum(prob * d_prob, axis=-1, keepdims=True)
        d_score = (prob * (d_prob - inner)).astype(jnp.bfloat16)
        d_query_rows = (
            jnp.einsum("hqk,khd->qhd", d_score, keys, preferred_element_type=jnp.float32) * scale
        )
        d_keys = (
            d_keys
            + jnp.einsum("hqk,qhd->khd", d_score, query_rows, preferred_element_type=jnp.float32)
            * scale
        )
        d_values = d_values + jnp.einsum(
            "hqk,qhd->khd", prob.astype(jnp.bfloat16), d_rows, preferred_element_type=jnp.float32
        )
        return ((d_keys, d_values), d_query_rows)

    zero_heads = jnp.zeros((group, heads_here, HEAD_DIM), jnp.float32)
    (d_keys, d_values), d_query = lax.scan(
        backward_block, (zero_heads, zero_heads), (starts, log_totals)
    )
    d_query = d_query.reshape(group, heads_here, HEAD_DIM)
    d_qkv = jnp.stack(
        [rotate_back(d_query, cosine, sine), rotate_back(d_keys, cosine, sine), d_values], axis=1
    )
    d_qkv = d_qkv.reshape(group, 3, width_here).astype(jnp.bfloat16)
    grad_qkv = jnp.einsum("nd,ncm->dcm", all_normed, d_qkv, preferred_element_type=jnp.float32)
    rows_here = d_qkv
    d_normed_attn = lax.psum_scatter(
        jnp.einsum("ncm,dcm->nd", rows_here, wqkv, preferred_element_type=jnp.float32).astype(
            jnp.bfloat16
        ),
        "tensor",
        scatter_dimension=0,
        tiled=True,
    ).astype(jnp.float32)
    _, norm_attn_back = jax.vjp(rms_norm, x_start, norm_gain_attn)
    d_start_norm, grad_gain_attn = norm_attn_back(d_normed_attn)
    d_start = (d_mid + d_start_norm).astype(jnp.bfloat16)
    qkv_shard, out_shard, gate_up_shard, down_shard = (
        lax.psum_scatter(grad_qkv, "dp", scatter_dimension=0, tiled=True),
        lax.psum_scatter(grad_out, "dp", scatter_dimension=0, tiled=True),
        lax.psum_scatter(grad_gate_up, "dp", scatter_dimension=0, tiled=True),
        lax.psum_scatter(grad_down, "dp", scatter_dimension=0, tiled=True),
    )
    small_sums = lax.psum(
        (grad_gain_attn, grad_gain_moe, grad_router, grad_const, grad_vconst), ("dp", "tensor")
    )
    back_out, back_grad = (
        lax.all_to_all(result, "dp", split_axis=0, concat_axis=0, tiled=True),
        lax.all_to_all(d_start, "dp", split_axis=0, concat_axis=0, tiled=True),
    )
    restore = jnp.argsort(order)
    return (
        back_out[restore],
        back_grad[restore],
        grad_residual,
        qkv_shard,
        out_shard,
        gate_up_shard,
        down_shard,
        small_sums[0],
        small_sums[1],
        small_sums[2],
        small_sums[3],
        small_sums[4],
    )


def solution(mesh):
    return jax.shard_map(
        body,
        mesh=mesh,
        in_specs=(
            P(("dp", "tensor"), None),
            P(("dp", "tensor"), None),
            P(("dp", "tensor")),
            P("dp", None),
            P("dp", None),
            P(("dp", "tensor"), None),
            P("dp", None, "tensor"),
            P("dp", "tensor"),
            P("dp", None, None, "tensor"),
            P("dp", None, "tensor"),
            P(),
            P(),
            P(),
            P(),
            P(),
        ),
        out_specs=(
            P(("dp", "tensor"), None),
            P(("dp", "tensor"), None),
            P(("dp", "tensor"), None),
            P("dp", None, "tensor"),
            P("dp", "tensor"),
            P("dp", None, None, "tensor"),
            P("dp", None, "tensor"),
            P(),
            P(),
            P(),
            P(),
            P(),
        ),
        check_vma=False,
    )
```

profile of v0, /device:TPU:0, one launch (start us, length us, event | category | flops | bytes accessed | tf_op | source)
XLA Modules:
  0.0 1494.0 jit_solution(10483238684854223833)
XLA Ops:
  15.0 17.6 %all_to_all.45 = bf16[8,64,768]{2,1,0:T(8,128)(2,1)S(1)} all-to-all(bf16[8,64,768]{2,1,0:T(8,128)(2,1)S(1)} %bitcast.298), channel_id=1, replica_groups=mesh['dp'=8,'tensor'=4] {'dp'}, dimensions={0} | all-to-all | bytes 1572864 | tf_op jit(solution)/shard_map/all_to_all | solution.py:119
  59.7 37.4 %all-gather.7.cloned.1.call-done = bf16[2048,768]{1,0:T(8,128)(2,1)} async-done(((bf16[512,768]{1,0:T(8,128)(2,1)}), bf16[2048,768]{1,0:T(8,128)(2,1)}) %all-gather.7.cloned.1.call-update) | async-done | bytes 3145744 | tf_op jit(solution)/shard_map/all_gather | solution.py:135
  102.9 102.8 %while.28 = (s32[]{:T(128)}, bf16[4,512,3,64]{1,3,2,0:T(8,128)(2,1)}, f32[4,3,512]{2,1,0:T(4,128)}, s32[4]{0:T(128)S(1)}, s32[2048]{0:T(1024)S(1)}, /*index=5*/b...) while((s32[]{:T(128)}, ...), condition=%wide.region_8.9_spmd.clone, body=%wide.region_5.8_spmd.clone.sunk | while | flops 846199808 | bytes 50471652 | solution.py:164
  230.3 41.0 %reduce-scatter.12.cloned.1.call-done = bf16[512,768]{1,0:T(8,128)(2,1)} async-done(((bf16[2048,768]{1,0:T(8,128)(2,1)}), bf16[512,768]{1,0:T(8,128)(2,1)}) %reduce-scatter.12.cloned.1.call-update) | async-done | bytes 786448 | tf_op jit(solution)/shard_map/reduce_scatter | solution.py:167
  316.4 19.8 %all-gather.15.cloned.1.call-done = bf16[2048,768]{1,0:T(8,128)(2,1)} async-done(((bf16[512,768]{1,0:T(8,128)(2,1)}), bf16[2048,768]{1,0:T(8,128)(2,1)}) %all-gather.15.cloned.1.call-update) | async-done | bytes 3145744 | tf_op jit(solution)/shard_map/all_gather | solution.py:186
  336.2 21.5 %gather_fusion.5 = bf16[4096,768]{1,0:T(8,128)(2,1)} fusion(bf16[2048,768]{1,0:T(8,128)(2,1)} %all-gather.15.cloned.1.call-done, s32[4096]{0:T(1024)S(1)} %get-tuple-element.337), kind=kCustom, calls=%fused_computation.5 | custom fusion | bytes 12599296 | tf_op jit(solution)/shard_map/gather | solution.py:205
  372.5 23.0 %gather_fusion.6 = f32[4096]{0:T(1024)S(1)} fusion(f32[4096]{0:T(1024)S(1)} %reshape.533, s32[4096]{0:T(1024)S(1)} %get-tuple-element.336), kind=kCustom, calls=%fused_computation.6 | custom fusion | bytes 49152 | tf_op jit(solution)/shard_map/gather | solution.py:206
  400.4 21.4 %gather_fusion.1 = bf16[4096,768]{1,0:T(8,128)(2,1)} fusion(bf16[2048,768]{1,0:T(8,128)(2,1)} %all-gather.9.cloned.1.call-done, s32[4096]{0:T(1024)S(1)} %get-tuple-element.337), kind=kCustom, calls=%fused_computation.1 | custom fusion | bytes 12599296 | tf_op jit(solution)/shard_map/gather | solution.py:190
  421.9 51.5 %all-gather.11.cloned.1.call-done = bf16[768,8,2,512]{3,0,2,1:T(8,128)(2,1)} async-done(((bf16[96,8,2,512]{3,0,2,1:T(8,128)(2,1)}), bf16[768,8,2,512]{3,0,2,1:T(8,128)(2,1)}) %all-gather.11.cloned.1.call-update) | async-done | bytes 12582928 | tf_op jit(solution)/shard_map/all_gather | solution.py:125
  489.0 32.1 %all-gather.13.cloned.1.call-done = bf16[768,8,512]{2,0,1:T(8,128)(2,1)} async-done(((bf16[96,8,512]{2,0,1:T(8,128)(2,1)}), bf16[768,8,512]{2,0,1:T(8,128)(2,1)}) %all-gather.13.cloned.1.call-update) | async-done | bytes 6291472 | tf_op jit(solution)/shard_map/all_gather | solution.py:126
  558.1 24.9 %gather_fusion.2 = f32[4096,768]{1,0:T(8,128)} fusion(f32[4097,768]{1,0:T(8,128)} %concatenate.40, s32[4096]{0:T(1024)S(1)} %broadcast_clamp_fusion), kind=kCustom, calls=%fused_computation.2 | custom fusion | bytes 25182208 | tf_op jit(solution)/shard_map/gather | solution.py:199
  598.2 26.0 %gather_fusion.8 = bf16[4096]{0:T(1024)(128)(2,1)S(1)} fusion(bf16[4097]{0:T(1024)(128)(2,1)S(1)} %pad_maximum_fusion.7, s32[4096]{0:T(1024)S(1)} %broadcast_clamp_fusion), kind=kCustom, calls=%fused_computation.8 | custom fusion | bytes 32768 | tf_op jit(solution)/shard_map/gather | solution.py:225
  626.2 19.9 %multiply_reduce_fusion.1 = bf16[2048,768]{1,0:T(8,128)(2,1)} fusion(f32[2048,2,768]{2,1,0:T(2,128)} %gather.35, f32[2048,2]{1,0:T(8,128)S(1)} %copy-done.21), kind=kLoop, calls=%fused_computation.63 | loop fusion | flops 4718592 | bytes 15745024 | tf_op jit(solution)/shard_map/reduce_sum | solution.py:199
  669.8 24.9 %gather_fusion.7 = f32[4096,768]{1,0:T(8,128)} fusion(f32[4097,768]{1,0:T(8,128)} %concatenate.41, s32[4096]{0:T(1024)S(1)} %broadcast_clamp_fusion), kind=kCustom, calls=%fused_computation.7 | custom fusion | bytes 25182208 | tf_op jit(solution)/shard_map/gather | solution.py:224
  709.8 35.9 %reduce_sum.305 = bf16[2048,768]{1,0:T(8,128)(2,1)} reduce(f32[2048,2,768]{2,1,0:T(2,128)} %reshape.525, f32[]{:T(128)} %constant.40.clone.1), dimensions={1}, to_apply=%region_28.29 | reduce | flops 1572864 | bytes 15728644 | tf_op jit(solution)/shard_map/reduce_sum | solution.py:224
  761.5 44.7 %reduce-scatter.16.cloned.1.call-done = bf16[512,768]{1,0:T(8,128)(2,1)} async-done(((bf16[2048,768]{1,0:T(8,128)(2,1)}), bf16[512,768]{1,0:T(8,128)(2,1)}) %reduce-scatter.16.cloned.1.call-update) | async-done | bytes 786448 | tf_op jit(solution)/shard_map/reduce_scatter | solution.py:229
  813.9 63.4 %all-gather.17.cloned.1.call-done = bf16[2048,768]{1,0:T(8,128)(2,1)} async-done(((bf16[512,768]{1,0:T(8,128)(2,1)}), bf16[2048,768]{1,0:T(8,128)(2,1)}) %all-gather.17.cloned.1.call-update) | async-done | bytes 3145744 | tf_op jit(solution)/shard_map/all_gather | solution.py:257
  881.4 184.4 %while.29 = (s32[]{:T(128)}, f32[2048,3,64]{0,2,1:T(8,128)S(1)}, f32[2048,3,64]{0,2,1:T(8,128)}, f32[4,512,3,64]{1,0,3,2:T(4,128)}, s32[4]{0:T(128)S(1)}, /*inde...) while((s32[]{:T(128)}, f32[2048,3,64]{0,2,1:T(8,128)S(1)}, ...), condition=%wide.region_44.45_spmd.clone, body=%wide.region_42.44_spmd.clone.sunk | while | flops 2049932288 | bytes 133087480 | solution.py:290
  1111.1 25.0 %copy.123 = f32[768,8,2,512]{3,1,2,0:T(8,128)} copy(f32[768,8,2,512]{0,3,2,1:T(8,128)} %convolution_bitcast_fusion) | data formatting | bytes 50331648 | tf_op jit(solution)/shard_map/ecd,ecjf->dejf/transpose | solution.py:218
  1174.5 49.1 %all-reduce.6 = (f32[768]{0:T(1024)}, f32[768]{0:T(1024)}, f32[768,12]{0,1:T(8,128)}, f32[2,768,2]{1,2,0:T(2,128)}, f32[2,768]{1,0:T(2,128)}) all-reduce(f32[768]{0:T(1024)S(1)} %get-tuple-element.257, f32[768]{0:T(1024)S(1)} %copy-done.89, f32[768,12]{0,1:T(8,128)S(1)} %fusion.111, ...), channel_id=1, replica_groups=mesh['dp'=8,'tensor'=4] {'dp','tensor'}, use_global_device_ids=true, to_apply=%region_52.53 | all-reduce | flops 15360 | bytes 122880 | tf_op jit(solution)/shard_map/psum | solution.py:317
  1226.3 16.2 %reduce-scatter.26.cloned.1.call-done = f32[96,8,512]{2,0,1:T(8,128)} async-done(((f32[768,8,512]{2,0,1:T(8,128)}), f32[96,8,512]{2,0,1:T(8,128)}) %reduce-scatter.26.cloned.1.call-update) | async-done | bytes 1572880 | tf_op jit(solution)/shard_map/reduce_scatter | solution.py:315
  1246.1 156.4 %reduce-scatter.24.cloned.1.call-done = f32[96,8,2,512]{3,1,2,0:T(8,128)} async-done(((f32[768,8,2,512]{3,1,2,0:T(8,128)}), f32[96,8,2,512]{3,1,2,0:T(8,128)}) %reduce-scatter.24.cloned.1.call-update) | async-done | bytes 3145744 | tf_op jit(solution)/shard_map/reduce_scatter | solution.py:314
  1409.0 32.0 %reduce-scatter.22.cloned.1.call-done = f32[96,192]{1,0:T(8,128)} async-done(((f32[768,192]{1,0:T(8,128)}), f32[96,192]{1,0:T(8,128)}) %reduce-scatter.22.cloned.1.call-update) | async-done | bytes 73744 | tf_op jit(solution)/shard_map/reduce_scatter | solution.py:313
  1441.1 46.1 %reduce-scatter.20.cloned.1.call-done = f32[96,3,192]{2,0,1:T(8,128)} async-done(((f32[768,3,192]{2,0,1:T(8,128)}), f32[96,3,192]{2,0,1:T(8,128)}) %reduce-scatter.20.cloned.1.call-update) | async-done | bytes 221200 | tf_op jit(solution)/shard_map/reduce_scatter | solution.py:312
  (477 shorter events, 631.7 us)
Async XLA Ops:
  7.2 89.9 %all-gather.7.cloned.1.call-start = ((), (), s32[]{:S(2)}) async-start(), calls=%async_computation.13 | async-start | bytes 3932160 | tf_op jit(solution)/shard_map/all_gather | solution.py:135
  34.1 237.1 %reduce-scatter.12.cloned.1.call-start = ((), (), s32[]{:S(2)}) async-start(), calls=%async_computation.14 | async-start | bytes 3932160 | tf_op jit(solution)/shard_map/reduce_scatter | solution.py:167
  212.0 124.2 %all-gather.15.cloned.1.call-start = ((), (), s32[]{:S(2)}) async-start(), calls=%async_computation.19 | async-start | bytes 3932160 | tf_op jit(solution)/shard_map/all_gather | solution.py:186
  214.1 59.7 %copy-start.50 = (f32[768]{0:T(1024)S(1)}, f32[768]{0:T(1024)}, u32[]{:S(2)}) copy-start(f32[768]{0:T(1024)} %param.30) | copy-start | bytes 9220
  230.2 170.2 %all-gather.9.cloned.1.call-start = ((), (), s32[]{:S(2)}) async-start(), calls=%async_computation.15 | async-start | bytes 3932160 | tf_op jit(solution)/shard_map/all_gather | solution.py:184
  276.2 197.2 %all-gather.11.cloned.1.call-start = ((), (), s32[]{:S(2)}) async-start(), calls=%async_computation.16 | async-start | bytes 14155776 | tf_op jit(solution)/shard_map/all_gather | solution.py:125
  278.3 242.8 %all-gather.13.cloned.1.call-start = ((), (), s32[]{:S(2)}) async-start(), calls=%async_computation.17 | async-start | bytes 7077888 | tf_op jit(solution)/shard_map/all_gather | solution.py:126
  279.5 476.2 %reduce-scatter.28.cloned.1.call-start = ((), (), s32[]{:S(2)}) async-start(), calls=%async_computation.27 | async-start | bytes 655360
  395.6 125.6 %copy-start.55 = (f32[8,512]{1,0:T(8,128)}, f32[8,512]{1,0:T(8,128)S(1)}, u32[]{:S(2)}) copy-start(f32[8,512]{1,0:T(8,128)S(1)} %mul.541) | copy-start | bytes 49156
  626.1 130.5 %reduce-scatter.14.cloned.1.call-start = ((), (), s32[]{:S(2)}) async-start(), calls=%async_computation.18 | async-start | bytes 3932160 | tf_op jit(solution)/shard_map/reduce_scatter | solution.py:200
  646.1 160.2 %reduce-scatter.16.cloned.1.call-start = ((), (), s32[]{:S(2)}) async-start(), calls=%async_computation.20 | async-start | bytes 3932160 | tf_op jit(solution)/shard_map/reduce_scatter | solution.py:229
  745.8 131.6 %all-gather.17.cloned.1.call-start = ((), (), s32[]{:S(2)}) async-start(), calls=%async_computation.21 | async-start | bytes 3932160 | tf_op jit(solution)/shard_map/all_gather | solution.py:257
  813.8 67.6 %copy-start.12 = (bf16[2048,3,64]{0,2,1:T(8,128)(2,1)S(1)}, bf16[2048,3,64]{0,2,1:T(8,128)(2,1)}, u32[]{:S(2)}) copy-start(bf16[2048,3,64]{0,2,1:T(8,128)(2,1)} %copy-done.11) | copy-start | bytes 2359300
  813.8 67.6 %copy-start.16 = (bf16[2048,3,64]{0,2,1:T(8,128)(2,1)S(1)}, bf16[2048,3,64]{0,2,1:T(8,128)(2,1)}, u32[]{:S(2)}) copy-start(bf16[2048,3,64]{0,2,1:T(8,128)(2,1)} %copy-done.15) | copy-start | bytes 2359300
  813.8 67.6 %copy-start.32 = (s32[2048]{0:T(1024)S(1)}, s32[2048]{0:T(1024)}, u32[]{:S(2)}) copy-start(s32[2048]{0:T(1024)} %copy-done.31) | copy-start | bytes 24580
  813.8 67.6 %copy-start.97 = (s32[4]{0:T(128)S(1)}, s32[4]{0:T(128)}, u32[]{:S(2)}) copy-start(s32[4]{0:T(128)} %copy-done.96) | copy-start | bytes 52
  813.8 340.9 %reduce-scatter.18.cloned.1.call-start = ((), (), s32[]{:S(2)}) async-start(), calls=%async_computation.22 | async-start | bytes 3932160 | tf_op jit(solution)/shard_map/reduce_scatter | solution.py:300
  1082.4 160.1 %reduce-scatter.26.cloned.1.call-start = ((), (), s32[]{:S(2)}) async-start(), calls=%async_computation.26 | async-start | bytes 14155776 | tf_op jit(solution)/shard_map/reduce_scatter | solution.py:315
  1095.2 307.4 %reduce-scatter.24.cloned.1.call-start = ((), (), s32[]{:S(2)}) async-start(), calls=%async_computation.25 | async-start | bytes 28311552 | tf_op jit(solution)/shard_map/reduce_scatter | solution.py:314
  1136.2 304.9 %reduce-scatter.22.cloned.1.call-start = ((), (), s32[]{:S(2)}) async-start(), calls=%async_computation.24 | async-start | bytes 884736 | tf_op jit(solution)/shard_map/reduce_scatter | solution.py:313
  1141.1 346.1 %reduce-scatter.20.cloned.1.call-start = ((), (), s32[]{:S(2)}) async-start(), calls=%async_computation.23 | async-start | bytes 2654208 | tf_op jit(solution)/shard_map/reduce_scatter | solution.py:312
  1151.0 16.2 %all-to-all-start.1 = ((bf16[8,64,768]{2,1,0:T(8,128)(2,1)}), bf16[8,64,768]{2,1,0:T(8,128)(2,1)S(1)}, u32[]{:S(2)}, u32[]{:S(2)}) async-start(bf16[8,64,768]{2,1,0:T(8,128)(2,1)} %bitcast.25), calls=%async_computation.3 | async-start | bytes 1572864 | tf_op jit(solution)/shard_map/all_to_all | solution.py:321
  1167.3 56.4 %all-to-all-start.3 = ((bf16[8,64,768]{2,1,0:T(8,128)(2,1)}), bf16[8,64,768]{2,1,0:T(8,128)(2,1)S(1)}, u32[]{:S(2)}, u32[]{:S(2)}) async-start(bf16[8,64,768]{2,1,0:T(8,128)(2,1)} %bitcast.296), calls=%async_computation.7 | async-start | bytes 1572864 | tf_op jit(solution)/shard_map/all_to_all | solution.py:322
  1242.6 244.7 %copy-start.1 = (bf16[512,768]{1,0:T(8,128)(2,1)S(1)}, bf16[512,768]{1,0:T(8,128)(2,1)}, u32[]{:S(2)}) copy-start(bf16[512,768]{1,0:T(8,128)(2,1)} %param.19) | copy-start | bytes 2359300
  (100 other events, 1042.9 us)
Sparse Core Ops, SparseCore 0:
  34.3 62.7 all-gather.6
  212.2 59.0 reduce-scatter.11
  272.8 63.3 all-gather.14
  338.2 62.2 all-gather.8
  402.8 70.5 all-gather.10
  475.7 45.3 all-gather.12
  626.3 21.8 reduce-scatter.27
  650.4 58.6 reduce-scatter.13
  745.9 60.3 reduce-scatter.15
  814.0 63.3 all-gather.16
  1082.5 59.0 reduce-scatter.17
  1145.0 97.5 reduce-scatter.25
  1246.2 156.2 reduce-scatter.23
  1406.1 34.9 reduce-scatter.21
  1444.8 42.3 reduce-scatter.19
where the time goes:
time: 1500 us; the launch traced here: 1490 us
  waiting for transfers between devices  551 us (37%)
  local copies, waits for them, and re-layouts  348 us (23%)
  matrix products  273 us (18%)
  other arithmetic  164 us (11%)
  blocking collectives  117 us (8%)
  loops' own time  16.7 us (1%)
  between operations  15.6 us (1%)
    reduce_scatter x1, waiting for transfers between devices, body(): lax.psum_scatter(grad_gate_up, 'dp', scatter_dimension=0, tiled=True)  156 us
    all_gather x1, waiting for transfers between devices, body(): lax.all_gather(d_mid.astype(jnp.bfloat16), 'tensor', axis=0, tiled=True)  63.4 us
    dot_general x8, matrix products, scores(): jnp.einsum('qhd,khd->hqk', query_rows, keys, preferred_element_type=jnp.f...  60.3 us
    all_gather x1, waiting for transfers between devices, body(): lax.all_gather(w_gate_up, 'dp', axis=0, tiled=True)  51.5 us
    psum x1, blocking collectives, body(): lax.psum((grad_gain_attn, grad_gain_moe, grad_router, grad_const, grad_vc...  49.1 us
    reduce_scatter x1, waiting for transfers between devices, body(): lax.psum_scatter(grad_qkv, 'dp', scatter_dimension=0, tiled=True)  46.1 us
    reduce_scatter x1, waiting for transfers between devices, body(): lax.psum_scatter(d_normed_part.astype(jnp.bfloat16), 'tensor', scatter_di...  44.7 us
    reduce_scatter x1, waiting for transfers between devices, body(): lax.psum_scatter(lax.dot_general(rows_here, wout, (((1,), (1,)), ((), ())...  41 us
  transfers between devices with their start and end apart: 17, of which 13 were waited for; matrix products, arithmetic and copies ran while one was open for 24% of the time, Pallas kernels for 0%

commit v1 on v0

v1 whole, which is shorter than its diff:
```python
import functools
import math

import jax
import jax.numpy as jnp
from jax import lax
from jax.experimental import pallas as pl
from jax.experimental.pallas import tpu as pltpu
from jax.sharding import PartitionSpec as P

D = 768
HEAD_DIM = 64
HEADS = 12
EXPERTS = 8
LONGEST = 1024
EPSILON = 1e-6
MASKED = -1e30
F32, BF16, I32 = jnp.float32, jnp.bfloat16, jnp.int32
NN = (((1,), (0,)), ((), ()))
NT = (((1,), (1,)), ((), ()))
TN = (((0,), (0,)), ((), ()))
SCORE_SCALE = HEAD_DIM**-0.5
LOG2E = 1.4426950408889634
TILE = 160
ROWS = 256
SPARE = 16
VMEM_CAP = 66_000_000


def mm(a, b, dims):
    return lax.dot_general(a, b, dims, preferred_element_type=F32)


def iota(shape, axis):
    return lax.broadcasted_iota(I32, shape, axis)


def pick(cond):
    return jnp.where(cond, 1.0, 0.0).astype(BF16)


def split2(v):
    high = v.astype(BF16)
    return high, (v - high.astype(F32)).astype(BF16)


def split3(v):
    high = v.astype(BF16)
    rest = v - high.astype(F32)
    mid = rest.astype(BF16)
    return high, mid, (rest - mid.astype(F32)).astype(BF16)


def vmem():
    return pl.BlockSpec(memory_space=pltpu.VMEM)


def smem():
    return pl.BlockSpec(memory_space=pltpu.SMEM)


def call(body, name, outs, operands, scalars=0, scratch=()):
    return pl.pallas_call(
        body,
        name=name,
        out_shape=[jax.ShapeDtypeStruct(*o) for o in outs],
        in_specs=[smem()] * scalars + [vmem()] * (len(operands) - scalars),
        out_specs=[vmem()] * len(outs),
        scratch_shapes=list(scratch),
        compiler_params=pltpu.CompilerParams(vmem_limit_bytes=VMEM_CAP),
    )(*operands)


def deal_body(n_dp, t_ref, deal_ref, tok_ref, cot_ref, routes_ref, xs_ref, gs_ref, pos_ref, slot_ref, cnt_ref):
    rows = tok_ref.shape[0]
    first, second = iota((rows, rows), 0), iota((rows, rows), 1)
    before = pick(first < second)
    deal = deal_ref[...]
    hit = iota((n_dp, rows), 0) == deal
    rank = mm(pick(hit), before, NN)
    rank = jnp.sum(jnp.where(hit, rank, 0.0), axis=0, keepdims=True).astype(I32)
    pos = deal * (rows // n_dp) + rank
    pos_ref[...] = pos
    place = pick(first == pos)
    xs_ref[...] = mm(place, tok_ref[...], NN).astype(BF16)
    gs_ref[...] = mm(place, cot_ref[...], NN).astype(BF16)
    expert = iota((EXPERTS, rows), 0)
    for j in range(routes_ref.shape[0]):
        route = routes_ref[t_ref[0] ^ j]
        named = (expert == route[0:1]) | (expert == route[1:2])
        ahead = mm(pick(named), before, NN).astype(I32)
        slot_ref[j] = jnp.where(named, ahead, -1)
        total = jnp.sum(jnp.where(named, 1.0, 0.0), axis=1, keepdims=True).astype(I32)
        cnt_ref[j] = jnp.broadcast_to(total, (EXPERTS, 128))


def restore_body(pos_ref, a_ref, b_ref, oa_ref, ob_ref):
    rows = a_ref.shape[0]
    place = pick(iota((rows, rows), 0) == pos_ref[...])
    oa_ref[...] = mm(place, a_ref[...], TN).astype(BF16)
    ob_ref[...] = mm(place, b_ref[...], TN).astype(BF16)


def turn(u):
    low = (iota((1, u.shape[1]), 1) % HEAD_DIM) < HEAD_DIM // 2
    half = HEAD_DIM // 2
    return jnp.where(low, pltpu.roll(u, u.shape[1] - half, 1), pltpu.roll(u, half, 1))


def wide(table):
    return jnp.concatenate([table] * (D // 128), axis=1)


def key_bias(start, block, first_row, base):
    window = LONGEST + block
    key = iota((window, block), 0) + first_row
    row = iota((1, block), 1) + (base + first_row)
    return jnp.where((key >= start) & (key <= row), 0.0, MASKED)


def attention_body(x0_ref, x1_ref, x2_ref, w_ref, gain_ref, cos_ref, sin_ref, start_ref,
                   h_ref, q_ref, k_ref, v_ref, o_ref, lse_ref, bias_ref):
    rows = x0_ref.shape[0]
    step = 256
    gain = gain_ref[...]
    for c, x_ref in enumerate((x2_ref, x1_ref, x0_ref)):
        def project(i, _, c=c, x_ref=x_ref):
            at = pl.multiple_of(i * step, step)
            x = x_ref[pl.ds(at, step), :].astype(F32)
            h = x * lax.rsqrt(jnp.mean(x * x, axis=1, keepdims=True) + EPSILON) * gain
            h = h.astype(BF16)
            to = pl.ds(pl.multiple_of(c * rows + i * step, step), step)
            h_ref[to, :] = h
            cos, sin = wide(cos_ref[to, :]), wide(sin_ref[to, :])
            k = mm(h, w_ref[:, D : 2 * D], NN)
            k_ref[to, :] = (k * cos + turn(k) * sin).astype(BF16)
            v_ref[to, :] = mm(h, w_ref[:, 2 * D : 3 * D], NN).astype(BF16)
            if c == 2:
                q = mm(h, w_ref[:, 0:D], NN)
                q_ref[pl.ds(at, step), :] = (q * cos + turn(q) * sin).astype(BF16)
            return 0

        lax.fori_loop(0, rows // step, project, 0)

    block = step
    window = LONGEST + block
    lane = iota((1, 128), 1) // HEAD_DIM
    for rb in range(rows // block):
        first = rb * block
        bias_ref[...] = key_bias(start_ref[:, first : first + block], block, first, LONGEST)

        def pair(i, _, first=first):
            lanes = pl.ds(pl.multiple_of(i * 128, 128), 128)
            k = k_ref[first : first + window, lanes]
            vt = v_ref[first : first + window, lanes].T
            q = q_ref[first : first + block, lanes]
            parts = []
            for half in range(2):
                qm = jnp.where(lane == half, q, jnp.zeros_like(q))
                s = mm(k, qm, NT) * (SCORE_SCALE * LOG2E) + bias_ref[...]
                top = jnp.max(s, axis=0, keepdims=True)
                p = jnp.exp2(s - top)
                total = jnp.sum(p, axis=0, keepdims=True)
                out = mm(vt[half * HEAD_DIM : (half + 1) * HEAD_DIM], p.astype(BF16), NN)
                parts.append(out * (1.0 / total))
                lse_ref[pl.ds(i * 2 + half, 1), first : first + block] = top + jnp.log2(total)
            o_ref[first : first + block, lanes] = jnp.concatenate(parts, axis=0).T.astype(BF16)
            return 0

        lax.fori_loop(0, HEADS // 2, pair, 0)


def attention_back_body(q_ref, k_ref, v_ref, do_ref, lse_ref, delta_ref, start_ref, cos_ref, sin_ref, w_ref,
                        dq_ref, dk_ref, dv_ref, d0_ref, d1_ref, d2_ref, bias_ref, dkf_ref, dvf_ref, dqf_ref):
    rows = q_ref.shape[0]
    block = 256
    window = LONGEST + block
    lane = iota((1, 128), 1) // HEAD_DIM
    for rb in range(rows // block):
        first = rb * block
        bias_ref[...] = key_bias(start_ref[:, first : first + block], block, first, LONGEST)

        def pair(i, _, first=first):
            lanes = pl.ds(pl.multiple_of(i * 128, 128), 128)
            k = k_ref[first : first + window, lanes]
            v = v_ref[first : first + window, lanes]
            kt = k.T
            q = q_ref[first : first + block, lanes]
            do = do_ref[first : first + block, lanes]
            dk = jnp.zeros((window, 128), F32)
            dv = jnp.zeros((window, 128), F32)
            parts = []
            for half in range(2):
                qm = jnp.where(lane == half, q, jnp.zeros_like(q))
                dom = jnp.where(lane == half, do, jnp.zeros_like(do))
                head = pl.ds(i * 2 + half, 1)
                s = mm(k, qm, NT) * (SCORE_SCALE * LOG2E) + bias_ref[...]
                p = jnp.exp2(s - lse_ref[head, first : first + block])
                dp = mm(v, dom, NT)
                ds = (p * (dp - delta_ref[head, first : first + block])).astype(BF16)
                dv = dv + mm(p.astype(BF16), dom, NN)
                dk = dk + mm(ds, qm, NN)
                parts.append(mm(kt[half * HEAD_DIM : (half + 1) * HEAD_DIM], ds, NN))
            dqf_ref[first : first + block, lanes] = jnp.concatenate(parts, axis=0).T
            if first == 0:
                dkf_ref[0:window, lanes] = dk
                dvf_ref[0:window, lanes] = dv
            else:
                old = window - block
                dkf_ref[first : first + old, lanes] += dk[0:old]
                dvf_ref[first : first + old, lanes] += dv[0:old]
                dkf_ref[first + old : first + window, lanes] = dk[old:]
                dvf_ref[first + old : first + window, lanes] = dv[old:]
            return 0

        lax.fori_loop(0, HEADS // 2, pair, 0)

    for c, out_ref in enumerate((d2_ref, d1_ref, d0_ref)):
        def finish(i, _, c=c, out_ref=out_ref):
            at = pl.ds(pl.multiple_of(i * block, block), block)
            to = pl.ds(pl.multiple_of(c * rows + i * block, block), block)
            cos, sin = wide(cos_ref[to, :]), wide(sin_ref[to, :])
            dk = dkf_ref[to, :] * SCORE_SCALE
            dk = (dk * cos - turn(dk) * sin).astype(BF16)
            dv = dvf_ref[to, :].astype(BF16)
            dk_ref[to, :] = dk
            dv_ref[to, :] = dv
            total = mm(dk, w_ref[:, D : 2 * D], NT) + mm(dv, w_ref[:, 2 * D : 3 * D], NT)
            if c == 2:
                dq = dqf_ref[at, :] * SCORE_SCALE
                dq = (dq * cos - turn(dq) * sin).astype(BF16)
                dq_ref[at, :] = dq
                total = total + mm(dq, w_ref[:, 0:D], NT)
            out_ref[at, :] = total.astype(out_ref.dtype)
            return 0

        lax.fori_loop(0, rows // block, finish, 0)


def attention_grads_body(x0_ref, x1_ref, x2_ref, h_ref, dq_ref, dk_ref, dv_ref, da_ref, o_ref, d0_ref, d1_ref, d2_ref,
                         gw_ref, gain_ref):
    rows = x0_ref.shape[0]
    h = h_ref[...]
    for c in range(D // 256):
        cols = slice(c * 256, (c + 1) * 256)
        gw_ref[:, c * 256 : c * 256 + 256] = mm(h[2 * rows :], dq_ref[:, cols], TN).astype(BF16)
        gw_ref[:, D + c * 256 : D + c * 256 + 256] = mm(h, dk_ref[:, cols], TN).astype(BF16)
        gw_ref[:, 2 * D + c * 256 : 2 * D + c * 256 + 256] = mm(h, dv_ref[:, cols], TN).astype(BF16)
        gw_ref[:, 3 * D + c * 256 : 3 * D + c * 256 + 256] = mm(da_ref[...], o_ref[:, cols], TN).astype(BF16)
    total = jnp.zeros((1, D), F32)
    for x_ref, d_ref in ((x0_ref, d0_ref), (x1_ref, d1_ref), (x2_ref, d2_ref)):
        x = x_ref[...].astype(F32)
        r = lax.rsqrt(jnp.mean(x * x, axis=1, keepdims=True) + EPSILON)
        total = total + jnp.sum(d_ref[...].astype(F32) * x * r, axis=0, keepdims=True)
    gain_ref[...] = jnp.broadcast_to(total, (8, D))


def router_body(t_ref, o_ref, w_ref, x_ref, gain_ref, res_ref, wrc_ref, routes_ref, x1_ref, hp_ref, gt_ref):
    rows = o_ref.shape[0]
    x1 = x_ref[...].astype(F32) + mm(o_ref[...], w_ref[:, 3 * D : 4 * D], NT)
    x1_ref[...] = x1
    h = x1 * lax.rsqrt(jnp.mean(x1 * x1, axis=1, keepdims=True) + EPSILON) * gain_ref[...]
    h = h.astype(BF16)
    hp_ref[0:rows, :] = h
    high, mid, low = split3(wrc_ref[...])
    z = mm(low, h, NT) + mm(mid, h, NT) + mm(high, h, NT) + res_ref[...]
    route = routes_ref[t_ref[0]]
    expert = iota(z.shape, 0)
    named0, named1 = expert == route[0:1], expert == route[1:2]
    c0 = jnp.sum(jnp.where(named0, z, 0.0), axis=0, keepdims=True)
    c1 = jnp.sum(jnp.where(named1, z, 0.0), axis=0, keepdims=True)
    top = jnp.maximum(c0, c1)
    e0, e1 = jnp.exp(c0 - top), jnp.exp(c1 - top)
    g0, g1 = e0 / (e0 + e1), e1 / (e0 + e1)
    table = [g0, g1]
    for j in range(2):
        l0, l1 = z[12 + 2 * j : 13 + 2 * j], z[13 + 2 * j : 14 + 2 * j]
        top = jnp.maximum(l0, l1)
        m0, m1 = jnp.exp(l0 - top), jnp.exp(l1 - top)
        table += [m0 / (m0 + m1), m1 / (m0 + m1)]
    gt_ref[...] = jnp.concatenate(table + [jnp.zeros((2, rows), F32)], axis=0)
    gates = jnp.where(named0, g0, jnp.where(named1, g1, 0.0))
    gates = jnp.where(expert < EXPERTS, gates, 0.0)
    hp_ref[rows : rows + SPARE, :] = jnp.concatenate([gates, jnp.zeros((SPARE, D - rows), F32)], axis=1).astype(BF16)


def local_body(t_ref, x1_ref, hp_ref, g_ref, gt_ref, routes_ref, v_ref, xl_ref, dhl_ref, sm_ref, gv_ref):
    rows = x1_ref.shape[0]
    h, g = hp_ref[0:rows, :], g_ref[...]
    hf, gf = h.astype(F32), g.astype(F32)
    route = routes_ref[t_ref[0]]
    low0 = gt_ref[0:1].astype(BF16).astype(F32)
    low1 = gt_ref[1:2].astype(BF16).astype(F32)

    def weight(e):
        return jnp.where(route[0:1] == e, low0, 0.0) + jnp.where(route[1:2] == e, low1, 0.0)

    copy, first, second = weight(EXPERTS + 1), weight(EXPERTS + 2), weight(EXPERTS + 3)
    m00, m01, m10, m11 = gt_ref[2:3], gt_ref[3:4], gt_ref[4:5], gt_ref[5:6]
    a = copy + first * m00 + second * m10
    b0, b1 = first * m01, second * m11
    table = jnp.concatenate([a, b0, b1, jnp.zeros((125, rows), F32)], axis=0).T
    ac, b0c, b1c = table[:, 0:1], table[:, 1:2], table[:, 2:3]
    v = v_ref[...]
    xl_ref[...] = x1_ref[...] + ac * hf + b0c * v[0:1] + b1c * v[1:2]
    dhl_ref[...] = ac * gf
    ones = jnp.ones((8, D), BF16)
    high, low = split2(hf * gf)
    gh = (mm(ones, high, NT) + mm(ones, low, NT))[0:1]
    vh, vm, vl = split3(v)
    gvs = mm(vl, g, NT) + mm(vm, g, NT) + mm(vh, g, NT)
    gv0, gv1 = gvs[0:1], gvs[1:2]
    zero = jnp.zeros((9, rows), F32)
    dl0 = first * m00 * m01 * (gh - gv0)
    dl1 = second * m10 * m11 * (gh - gv1)
    sm_ref[...] = jnp.concatenate(
        [zero, gh, m00 * gh + m01 * gv0, m10 * gh + m11 * gv1, dl0, -dl0, dl1, -dl1], axis=0
    )
    bh, bm, bl = split3(jnp.concatenate([b0, b1, jnp.zeros((6, rows), F32)], axis=0))
    gv_ref[...] = mm(bl, g, NN) + mm(bm, g, NN) + mm(bh, g, NN)


def middle_back_body(t_ref, c0_ref, c1_ref, c2_ref, c3_ref, dhl_ref, gt_ref, sm_ref, routes_ref, wrc_ref, x1_ref, gain_ref, g_ref,
                     hp_ref, w_ref, o_ref, gv_ref, dx_ref, da_ref, do_ref, delta_ref, dres_ref, small_ref):
    rows = x1_ref.shape[0]
    chunks = (c0_ref, c1_ref, c2_ref, c3_ref)
    dgf = jnp.zeros((SPARE, rows), F32)
    dh = dhl_ref[...]
    for c in chunks:
        dgf = dgf + c[rows : rows + SPARE, 0:rows].astype(F32)
        dh = dh + c[0:rows, :].astype(F32)
    dgate = jnp.concatenate([dgf[0:EXPERTS] + dgf[EXPERTS:], sm_ref[EXPERTS:SPARE]], axis=0)
    route = routes_ref[t_ref[0]]
    expert = iota((SPARE, rows), 0)
    named0, named1 = expert == route[0:1], expert == route[1:2]
    g0, g1 = gt_ref[0:1], gt_ref[1:2]
    d0 = jnp.sum(jnp.where(named0, dgate, 0.0), axis=0, keepdims=True)
    d1 = jnp.sum(jnp.where(named1, dgate, 0.0), axis=0, keepdims=True)
    inner = g0 * d0 + g1 * d1
    dz = jnp.where(named0, g0 * (d0 - inner), jnp.where(named1, g1 * (d1 - inner), 0.0))
    dres_ref[...] = dz
    dz = jnp.where(expert < 12, dz, sm_ref[...])
    zh, zm, zl = split3(dz)
    wh, wm, wl = split3(wrc_ref[...])
    dh = dh + (mm(zh, wl, TN) + mm(zl, wh, TN) + mm(zm, wm, TN) + mm(zh, wm, TN) + mm(zm, wh, TN) + mm(zh, wh, TN))
    h = hp_ref[0:rows, :]
    small_ref[0:SPARE, :] = mm(zl, h, NN) + mm(zm, h, NN) + mm(zh, h, NN)
    x1 = x1_ref[...]
    r = lax.rsqrt(jnp.mean(x1 * x1, axis=1, keepdims=True) + EPSILON)
    xr = x1 * r
    grad_gain = jnp.sum(dh * xr, axis=0, keepdims=True)
    gv = gv_ref[...]
    small_ref[SPARE : SPARE + 8, :] = jnp.concatenate([gv[0:2], grad_gain, gv[3:8]], axis=0)
    scaled = dh * gain_ref[...]
    dx = g_ref[...].astype(F32) + r * (scaled - xr * jnp.mean(xr * scaled, axis=1, keepdims=True))
    dx_ref[...] = dx
    da = dx.astype(BF16)
    da_ref[...] = da
    do = mm(da, w_ref[:, 3 * D : 4 * D], NN).astype(BF16)
    do_ref[...] = do
    high, low = split2(do.astype(F32) * o_ref[...].astype(F32))
    heads = pick(iota((SPARE, D), 1) // HEAD_DIM == iota((SPARE, D), 0))
    delta_ref[...] = mm(heads, high, NT) + mm(heads, low, NT)


def final_back_body(x_ref, d0_ref, r1_ref, r2_ref, dx_ref, gain_ref, out_ref):
    x = x_ref[...].astype(F32)
    dh = d0_ref[...] + r1_ref[...].astype(F32) + r2_ref[...].astype(F32)
    r = lax.rsqrt(jnp.mean(x * x, axis=1, keepdims=True) + EPSILON)
    xr = x * r
    scaled = dh * gain_ref[...]
    out_ref[...] = (dx_ref[...] + r * (scaled - xr * jnp.mean(xr * scaled, axis=1, keepdims=True))).astype(BF16)


def experts_body(ff, chunks, cnt_ref, *refs):
    h_refs, g_refs = refs[:chunks], refs[chunks : 2 * chunks]
    slot_ref, w_ref = refs[2 * chunks : 2 * chunks + 2]
    o_refs, d_refs = refs[2 * chunks + 2 : 3 * chunks + 2], refs[3 * chunks + 2 : 4 * chunks + 2]
    gw_ref, xbuf, gbuf, cbuf, onehot, fbuf, dbuf, gacc, gates, dgrow, off_ref, base_ref, nt_ref = refs[4 * chunks + 2 :]
    rows = slot_ref.shape[2]
    e = pl.program_id(0)

    def match(j, expert, tile):
        slots = slot_ref[j, pl.ds(expert, 1), :]
        return (iota((TILE, rows), 0) + tile * TILE) == slots

    def store_rows(at, count, hit, x, gs, gate_row):
        to = pl.ds(pl.multiple_of(at, 16), TILE)
        keep = iota((TILE, 1), 0) < count
        col = jnp.sum(jnp.where(hit, gate_row, 0.0), axis=1, keepdims=True)
        xbuf[to, :] = jnp.where(keep, x, xbuf[to, :].astype(F32)).astype(BF16)
        gbuf[to, :] = jnp.where(keep, gs, gbuf[to, :].astype(F32)).astype(BF16)
        cbuf[to, :] = jnp.where(keep, jnp.broadcast_to(col, (TILE, 128)), cbuf[to, :])

    def round16(n):
        return ((n + 15) // 16) * 16

    @pl.when(e == 0)
    def _gather():
        at = jnp.int32(0)
        for ex in range(EXPERTS):
            base_ref[ex] = at
            here = at
            for j in range(chunks):
                off_ref[j * EXPERTS + ex] = here
                here = here + round16(cnt_ref[j * EXPERTS + ex])
            tiles = (here - at + (ROWS - 1)) // ROWS
            nt_ref[ex] = tiles
            tail = pl.ds(pl.multiple_of(here, 16), ROWS)
            xbuf[tail, :] = jnp.zeros((ROWS, D), BF16)
            gbuf[tail, :] = jnp.zeros((ROWS, D), BF16)
            cbuf[tail, :] = jnp.zeros((ROWS, 128), F32)
            at = at + tiles * ROWS
        for j in range(chunks):
            gates[...] = h_refs[j][rows : rows + SPARE, 0:rows].astype(F32)

            def two(i, _, j=j):
                hits = [match(j, 2 * i + half, 0) for half in range(2)]
                sel = jnp.concatenate([pick(hit) for hit in hits], axis=0)
                x = mm(sel, h_refs[j][0:rows, :], NN)
                gs = mm(sel, g_refs[j][...], NN)
                for half in range(2):
                    ex = 2 * i + half
                    count = round16(jnp.minimum(cnt_ref[j * EXPERTS + ex], TILE))
                    part = slice(half * TILE, (half + 1) * TILE)
                    store_rows(off_ref[j * EXPERTS + ex], count, hits[half], x[part], gs[part], gates[pl.ds(ex, 1), :])
                return 0

            lax.fori_loop(0, EXPERTS // 2, two, 0)

            def rare(ex, _, j=j):
                def more(tile, _):
                    hit = match(j, ex, tile)
                    sel = pick(hit)
                    count = round16(jnp.minimum(cnt_ref[j * EXPERTS + ex] - tile * TILE, TILE))
                    store_rows(
                        off_ref[j * EXPERTS + ex] + tile * TILE,
                        count,
                        hit,
                        mm(sel, h_refs[j][0:rows, :], NN),
                        mm(sel, g_refs[j][...], NN),
                        gates[pl.ds(ex, 1), :],
                    )
                    return 0

                return lax.fori_loop(1, (cnt_ref[j * EXPERTS + ex] + (TILE - 1)) // TILE, more, 0)

            lax.fori_loop(0, EXPERTS, rare, 0)

    gacc[...] = jnp.zeros_like(gacc)

    def tile_step(m, _):
        at = pl.ds(pl.multiple_of(base_ref[e] + m * ROWS, 16), ROWS)
        x = xbuf[at, :]
        gs = gbuf[at, :].astype(F32)
        gate = wide(cbuf[at, :])
        u = mm(x, w_ref[:, 0:ff], NN)
        up = mm(x, w_ref[:, ff : 2 * ff], NN)
        sig = jax.nn.sigmoid(u)
        silu = u * sig
        act = (silu * up).astype(BF16)
        f = mm(act, w_ref[:, 2 * ff : 3 * ff], NT)
        cbuf[at, :] = jnp.broadcast_to(jnp.sum(gs * f, axis=1, keepdims=True), (ROWS, 128))
        gbuf[at, :] = (f * gate).astype(BF16)
        df = (gs * gate).astype(BF16)
        dact = mm(df, w_ref[:, 2 * ff : 3 * ff], NN)
        dup = (dact * silu).astype(BF16)
        du = (dact * up * sig * (1.0 + u * (1.0 - sig))).astype(BF16)
        xbuf[at, :] = (mm(du, w_ref[:, 0:ff], NT) + mm(dup, w_ref[:, ff : 2 * ff], NT)).astype(BF16)
        gacc[:, 0:ff] += mm(x, du, TN)
        gacc[:, ff : 2 * ff] += mm(x, dup, TN)
        gacc[:, 2 * ff : 3 * ff] += mm(df, act, TN)
        return 0

    lax.fori_loop(0, nt_ref[e], tile_step, 0)
    gw_ref[...] = gacc[...].astype(BF16)

    @pl.when(e == EXPERTS - 1)
    def _scatter():
        for j in range(chunks):
            def take(ex, _, j=j):
                at = pl.ds(pl.multiple_of(off_ref[j * EXPERTS + ex], 16), TILE)
                to = pl.ds(pl.multiple_of(ex * TILE, 16), TILE)
                hit = match(j, ex, 0)
                onehot[to, :] = pick(hit)
                fbuf[to, :] = gbuf[at, :]
                dbuf[to, :] = xbuf[at, :]
                col = jnp.concatenate([cbuf[at, :]] * (rows // 128), axis=1)
                dgrow[pl.ds(ex, 1), :] = jnp.sum(jnp.where(hit, col, 0.0), axis=0, keepdims=True)
                return 0

            lax.fori_loop(0, EXPERTS, take, 0)
            gacc[0:rows, 0:D] = mm(onehot[...], fbuf[...], TN)
            gacc[0:rows, D : 2 * D] = mm(onehot[...], dbuf[...], TN)

            def rare(ex, _, j=j):
                def more(tile, _):
                    at = pl.ds(pl.multiple_of(off_ref[j * EXPERTS + ex] + tile * TILE, 16), TILE)
                    hit = match(j, ex, tile)
                    sel = pick(hit)
                    gacc[0:rows, 0:D] += mm(sel, gbuf[at, :], TN)
                    gacc[0:rows, D : 2 * D] += mm(sel, xbuf[at, :], TN)
                    col = jnp.concatenate([cbuf[at, :]] * (rows // 128), axis=1)
                    dgrow[pl.ds(ex, 1), :] += jnp.sum(jnp.where(hit, col, 0.0), axis=0, keepdims=True)
                    return 0

                return lax.fori_loop(1, (cnt_ref[j * EXPERTS + ex] + (TILE - 1)) // TILE, more, 0)

            lax.fori_loop(0, EXPERTS, rare, 0)
            o_refs[j][...] = gacc[0:rows, 0:D].astype(BF16)
            d_refs[j][0:rows, :] = gacc[0:rows, D : 2 * D].astype(BF16)
            total = dgrow[...]
            high = total.astype(BF16).astype(F32)
            both = jnp.concatenate([high, total - high], axis=0)
            d_refs[j][rows : rows + SPARE, :] = jnp.concatenate(
                [both, jnp.zeros((SPARE, D - rows), F32)], axis=1
            ).astype(BF16)


def experts_call(counts, hs, gs, slots, weights, ff):
    chunks, rows = len(hs), slots.shape[2]
    width = 3 * ff
    most = (rows + 15 * chunks + ROWS - 1) // ROWS * ROWS * EXPERTS + ROWS
    whole = lambda shape: pl.BlockSpec(shape, lambda e: (0,) * len(shape), pipeline_mode=pl.Buffered(1))
    packed = (rows + SPARE, D)
    return pl.pallas_call(
        functools.partial(experts_body, ff, chunks),
        name="experts",
        grid=(EXPERTS,),
        in_specs=[smem()]
        + [whole(packed)] * chunks
        + [whole((rows, D))] * chunks
        + [whole(slots.shape), pl.BlockSpec((D, width), lambda e: (0, e))],
        out_specs=[whole((rows, D))] * chunks + [whole(packed)] * chunks + [pl.BlockSpec((D, width), lambda e: (0, e))],
        out_shape=[jax.ShapeDtypeStruct((rows, D), BF16)] * chunks
        + [jax.ShapeDtypeStruct(packed, BF16)] * chunks
        + [jax.ShapeDtypeStruct((D, EXPERTS * width), BF16)],
        scratch_shapes=[
            pltpu.VMEM((most, D), BF16),
            pltpu.VMEM((most, D), BF16),
            pltpu.VMEM((most, 128), F32),
            pltpu.VMEM((EXPERTS * TILE, rows), BF16),
            pltpu.VMEM((EXPERTS * TILE, D), BF16),
            pltpu.VMEM((EXPERTS * TILE, D), BF16),
            pltpu.VMEM((D, width), F32),
            pltpu.VMEM((SPARE, rows), F32),
            pltpu.VMEM((EXPERTS, rows), F32),
            pltpu.SMEM((chunks * EXPERTS,), I32),
            pltpu.SMEM((EXPERTS,), I32),
            pltpu.SMEM((EXPERTS,), I32),
        ],
        compiler_params=pltpu.CompilerParams(
            dimension_semantics=("arbitrary",), vmem_limit_bytes=VMEM_CAP
        ),
    )(counts, *hs, *gs, slots, weights)


def rope_tables(lengths, first, count):
    finish = jnp.sum(jnp.where(jnp.arange(lengths.shape[0])[:, None] <= jnp.arange(lengths.shape[0])[None, :], lengths[:, None], 0), axis=0)
    begins = finish - lengths
    rows = first + jnp.arange(count, dtype=I32)
    opening = jnp.max(jnp.where(begins[None, :] <= rows[:, None], begins[None, :], 0), axis=1)
    place = rows - opening
    half = HEAD_DIM // 2
    rates = jnp.exp(jnp.arange(half, dtype=F32) * (-2.0 * math.log(10000.0) / HEAD_DIM))
    angles = place.astype(F32)[:, None] * rates[None, :]
    cos, sin = jnp.cos(angles), jnp.sin(angles)
    return place, jnp.concatenate([cos] * 4, axis=1), jnp.concatenate([-sin, sin] * 2, axis=1)


def body(tokens, cotangent, deal, lengths, routes, gate_residual, w_qkv, w_out, w_gate_up, w_down,
         norm_gain_attn, norm_gain_moe, w_router, w_const, v_const):
    rows = tokens.shape[0]
    n_dp, n_t = lax.axis_size("dp"), lax.axis_size("tensor")
    t = lax.axis_index("tensor")
    t_arr = jnp.reshape(t, (1,)).astype(I32)
    ff = w_down.shape[2]
    d_here = w_qkv.shape[0]

    def swap(v, j):
        return lax.ppermute(v, "tensor", [(i, i ^ j) for i in range(n_t)])

    def shift(v, by):
        return lax.ppermute(v, "tensor", [(i, i + by) for i in range(n_t) if 0 <= i + by < n_t])

    attn_shard = jnp.concatenate([w_qkv, w_out[:, None, :]], axis=1)
    attn_shard = lax.all_gather(attn_shard, "tensor", axis=2, tiled=True).reshape(d_here, 4 * D)
    w_attn = lax.all_gather(attn_shard, "dp", axis=0, tiled=True)
    ff_shard = jnp.concatenate([w_gate_up.reshape(d_here, EXPERTS, 2 * ff), w_down], axis=2)
    w_ff = lax.all_gather(ff_shard.reshape(d_here, EXPERTS * 3 * ff), "dp", axis=0, tiled=True)

    routes_t = routes.reshape(n_t, rows, 2).transpose(0, 2, 1)
    xs, gs, pos, slots, counts = call(
        functools.partial(deal_body, n_dp),
        "deal",
        [((rows, D), BF16), ((rows, D), BF16), ((1, rows), I32), ((n_t, EXPERTS, rows), I32), ((n_t, EXPERTS, 128), I32)],
        [t_arr, deal.reshape(1, rows), tokens, cotangent, routes_t],
        1,
    )
    counts = counts[:, :, 0].reshape(n_t * EXPERTS)
    x0 = lax.all_to_all(xs, "dp", split_axis=0, concat_axis=0, tiled=True)
    g0 = lax.all_to_all(gs, "dp", split_axis=0, concat_axis=0, tiled=True)
    x1, x2 = shift(x0, 1), shift(x0, 2)
    g_chunks = [g0] + [swap(g0, j) for j in range(1, n_t)]

    place, cos, sin = rope_tables(lengths[0], (t - 2) * rows, 3 * rows)
    start = (LONGEST + jnp.arange(rows, dtype=I32) - place[2 * rows :]).reshape(1, rows)
    gain_attn, gain_moe = norm_gain_attn.reshape(1, D), norm_gain_moe.reshape(1, D)
    window = LONGEST + 256
    ext = (3 * rows, D)
    h, q, k, v, o, lse = call(
        attention_body,
        "attention",
        [(ext, BF16), ((rows, D), BF16), (ext, BF16), (ext, BF16), ((rows, D), BF16), ((SPARE, rows), F32)],
        [x0, x1, x2, w_attn, gain_attn, cos, sin, start],
        scratch=[pltpu.VMEM((window, 256), F32)],
    )

    res_t = jnp.concatenate([gate_residual.T, jnp.zeros((4, rows), F32)], axis=0)
    wrc = jnp.concatenate([w_router.T, w_const.transpose(0, 2, 1).reshape(4, D)], axis=0)
    v8 = jnp.concatenate([v_const, jnp.zeros((6, D), F32)], axis=0)
    xm, hp, gt = call(
        router_body,
        "router",
        [((rows, D), F32), ((rows + SPARE, D), BF16), ((8, rows), F32)],
        [t_arr, o, w_attn, x0, gain_moe, res_t, wrc, routes_t],
        1,
    )
    h_chunks = [hp] + [swap(hp, j) for j in range(1, n_t)]
    xl, dhl, sm, gv = call(
        local_body,
        "local_experts",
        [((rows, D), F32), ((rows, D), F32), ((SPARE, rows), F32), ((8, D), F32)],
        [t_arr, xm, hp, g0, gt, routes_t, v8],
        1,
    )

    made = experts_call(counts, h_chunks, g_chunks, slots, w_ff, ff)
    out_parts, back_parts, gw_ff = made[:n_t], made[n_t : 2 * n_t], made[2 * n_t]
    back_chunks = [back_parts[0]] + [swap(back_parts[j], j) for j in range(1, n_t)]
    out_chunks = [out_parts[0]] + [swap(out_parts[j], j) for j in range(1, n_t)]
    ff_sum = lax.psum_scatter(gw_ff, "dp", scatter_dimension=0, tiled=True)

    dx, da, do, delta, dres, small = call(
        middle_back_body,
        "middle_back",
        [((rows, D), F32), ((rows, D), BF16), ((rows, D), BF16), ((SPARE, rows), F32), ((SPARE, rows), F32), ((SPARE + 8, D), F32)],
        [t_arr, *back_chunks, dhl, gt, sm, routes_t, wrc, xm, gain_moe, g0, hp, w_attn, o, gv],
        1,
    )
    small_all = jnp.sum(lax.all_gather(small, ("dp", "tensor"), axis=0, tiled=False), axis=0)

    dq, dk, dv, d0, d1, d2 = call(
        attention_back_body,
        "attention_back",
        [((rows, D), BF16), (ext, BF16), (ext, BF16), ((rows, D), F32), ((rows, D), BF16), ((rows, D), BF16)],
        [q, k, v, do, lse, delta, start, cos, sin, w_attn],
        scratch=[pltpu.VMEM((window, 256), F32), pltpu.VMEM(ext, F32), pltpu.VMEM(ext, F32), pltpu.VMEM((rows, D), F32)],
    )
    r1, r2 = shift(d1, -1), shift(d2, -2)
    gw_attn, gain_part = call(
        attention_grads_body,
        "attention_grads",
        [((D, 4 * D), BF16), ((8, D), F32)],
        [x0, x1, x2, h, dq, dk, dv, da, o, d0, d1, d2],
    )
    gain_all = jnp.sum(lax.all_gather(gain_part[0:1], ("dp", "tensor"), axis=0, tiled=True), axis=0)
    (d_start,) = call(final_back_body, "final_back", [((rows, D), BF16)], [x0, d0, r1, r2, dx, gain_attn])
    result = xl
    for part in out_chunks:
        result = result + part.astype(F32)
    result = result.astype(BF16)
    back_out = lax.all_to_all(result, "dp", split_axis=0, concat_axis=0, tiled=True)
    back_grad = lax.all_to_all(d_start, "dp", split_axis=0, concat_axis=0, tiled=True)
    output, grad_tokens = call(restore_body, "restore", [((rows, D), BF16)] * 2, [pos, back_out, back_grad])

    attn_sum = lax.psum_scatter(gw_attn, "dp", scatter_dimension=0, tiled=True).reshape(d_here, 4, n_t, D // n_t)

    def share(j):
        return lax.dynamic_index_in_dim(attn_sum, t ^ j, 2, keepdims=False)

    attn_own = share(0).astype(F32)
    for j in range(1, n_t):
        attn_own = attn_own + swap(share(j), j).astype(F32)
    ff_own = ff_sum.reshape(d_here, EXPERTS, 3 * ff).astype(F32)
    return (
        output,
        grad_tokens,
        dres[0:12].T,
        attn_own[:, 0:3],
        attn_own[:, 3],
        ff_own[:, :, 0 : 2 * ff].reshape(d_here, EXPERTS, 2, ff),
        ff_own[:, :, 2 * ff :],
        gain_all,
        small_all[SPARE + 2],
        small_all[0:12].T,
        small_all[12:16].reshape(2, 2, D).transpose(0, 2, 1),
        small_all[SPARE : SPARE + 2],
    )


def solution(mesh):
    both, every = P(("dp", "tensor"), None), P()
    weights = (P("dp", None, "tensor"), P("dp", "tensor"), P("dp", None, None, "tensor"), P("dp", None, "tensor"))
    return jax.shard_map(
        body,
        mesh=mesh,
        in_specs=(both, both, P(("dp", "tensor")), P("dp", None), P("dp", None), both, *weights) + (every,) * 5,
        out_specs=(both, both, both, *weights) + (every,) * 5,
        check_vma=False,
    )
```

time: 1500 us -> 770 us (0.51)
  local copies, waits for them, and re-layouts: 348 us -> 30 us
  matrix products: 273 us -> 0 us
  waiting for transfers between devices: 551 us -> 338 us
  Pallas kernels: 0 us -> 184 us
  other arithmetic: 164 us -> 12.5 us
  starting transfers between devices: 8.17 us -> 94.6 us
  blocking collectives: 117 us -> 86.6 us
  loops' own time: 16.7 us -> 0 us
    reduce_scatter x8 -> x2, waiting for transfers between devices: 337 us -> 24.5 us  [the longest x1 24.5 us: body(): ff_sum = lax.psum_scatter(gw_ff, 'dp', scatter_dimension=0, tiled=True)]
    ppermute x0 -> x19, waiting for transfers between devices: none -> 289 us  [the longest x15 231 us: swap(): return lax.ppermute(v, 'tensor', [(i, i ^ j) for i in range(n_t)])]
    dot_general x45 -> x0, matrix products: 268 us -> none  [the longest x8 60.3 us: scores(): jnp.einsum('qhd,khd->hqk', query_rows, keys, preferred_element_type=jnp.f...]
    all_gather x6 -> x3, waiting for transfers between devices: 209 us -> 0.01 us  [the longest x1 0.01 us: body(): w_attn = lax.all_gather(attn_shard, 'dp', axis=0, tiled=True)]
    pallas_call x0 -> x10, Pallas kernels: none -> 184 us  [the longest x9 115 us: call(): pl.pallas_call(body, name=name, out_shape=[jax.ShapeDtypeStruct(*o) for o...]
    gather x11 -> x0, local copies, waits for them, and re-layouts: 166 us -> none  [the longest x2 40 us: body(): table[entry_slot] * gate_entries[:, None]]
    reduce_sum x20 -> x3, other arithmetic: 96.8 us -> 2.82 us  [the longest x1 2.06 us: body(): jnp.sum(lax.all_gather(small, ('dp', 'tensor'), axis=0, tiled=False), axi...]
    ppermute x0 -> x19, starting transfers between devices: none -> 78.1 us  [the longest x15 67.9 us: swap(): return lax.ppermute(v, 'tensor', [(i, i ^ j) for i in range(n_t)])]
  transfers between devices with their start and end apart: 17 -> 28, of which waited for: 13 -> 11; matrix products, arithmetic and copies ran while one was open for 24% -> 4% of each run, Pallas kernels for 0% -> 14%
where the time goes in v1:
time: 770 us; the launch traced here: 760 us
  waiting for transfers between devices  338 us (44%)
  Pallas kernels  184 us (24%)
  starting transfers between devices  94.6 us (12%)
  blocking collectives  86.6 us (11%)
  local copies, waits for them, and re-layouts  30 us (4%)
  between operations  14.4 us (2%)
  other arithmetic  12.5 us (2%)
    ppermute x15, waiting for transfers between devices, swap(): return lax.ppermute(v, 'tensor', [(i, i ^ j) for i in range(n_t)])  231 us
    pallas_call x9, Pallas kernels, call(): pl.pallas_call(body, name=name, out_shape=[jax.ShapeDtypeStruct(*o) for o...  115 us
    pallas_call x1, Pallas kernels, experts_call(): pl.pallas_call(functools.partial(experts_body, ff, chunks), name='experts...  69.2 us
    ppermute x15, starting transfers between devices, swap(): return lax.ppermute(v, 'tensor', [(i, i ^ j) for i in range(n_t)])  67.9 us
    all_gather x1, blocking collectives, body(): lax.all_gather(gain_part[0:1], ('dp', 'tensor'), axis=0, tiled=True)  65.1 us
    ppermute x4, waiting for transfers between devices, shift(): lax.ppermute(v, 'tensor', [(i, i + by) for i in range(n_t) if 0 <= i + by...  57.6 us
    reduce_scatter x1, waiting for transfers between devices, body(): ff_sum = lax.psum_scatter(gw_ff, 'dp', scatter_dimension=0, tiled=True)  24.5 us
    all_gather x1, blocking collectives, body(): lax.all_gather(attn_shard, 'tensor', axis=2, tiled=True)  21.4 us
  transfers between devices with their start and end apart: 28, of which 11 were waited for; matrix products, arithmetic and copies ran while one was open for 4% of the time, Pallas kernels for 14%

profile of v1, /device:TPU:0, one launch (start us, length us, event | category | flops | bytes accessed | tf_op | source)
XLA Modules:
  0.0 760.0 jit_solution(16927337322933858861)
XLA Ops:
  9.5 21.4 %all_gather.18 = bf16[96,4,768]{0,1,2:T(4,128)(2,1)S(1)} all-gather(bf16[96,4,192]{0,1,2:T(4,128)(2,1)S(1)} %pad_maximum_fusion.3), channel_id=1, replica_groups=mesh['dp'=8,'tensor'=4] {'tensor'}, dimensions={2}, use_global_device_ids=true | all-gather | bytes 737280 | tf_op jit(solution)/shard_map/all_gather | solution.py:587
  44.6 13.3 %all-to-all-done = bf16[8,64,768]{2,1,0:T(8,128)(2,1)S(1)} async-done(((bf16[8,64,768]{2,1,0:T(8,128)(2,1)}), bf16[8,64,768]{2,1,0:T(8,128)(2,1)S(1)}, u32[]{:S(2)}, u32[]{:S(2)}) %all-to-all-start) | async-done | bytes 786464 | tf_op jit(solution)/shard_map/all_to_all | solution.py:601
  68.7 4.3 collective-permute-start.1
  73.1 10.4 %all-to-all-done.1 = bf16[8,64,768]{2,1,0:T(8,128)(2,1)} async-done(((bf16[8,64,768]{2,1,0:T(8,128)(2,1)}), bf16[8,64,768]{2,1,0:T(8,128)(2,1)}, u32[]{:S(2)}, u32[]{:S(2)}) %all-to-all-start.1) | async-done | bytes 786464 | tf_op jit(solution)/shard_map/all_to_all | solution.py:602
  90.2 13.3 %collective-permute-done.1.x2_ref = bf16[512,768]{1,0:T(8,128)(2,1)S(1)} collective-permute-done((bf16[512,768]{1,0:T(8,128)(2,1)S(1)}, bf16[512,768]{1,0:T(8,128)(2,1)S(1)}, u32[]{:S(2)}, u32[]{:S(2)}) %collective-permute-start.1) | collective-permute-done | bytes 786464 | tf_op jit(solution)/shard_map/ppermute | solution.py:584
  104.4 34.6 %attention.1 = (bf16[1536,768]{1,0:T(8,128)(2,1)}, bf16[512,768]{1,0:T(8,128)(2,1)}, bf16[1536,768]{1,0:T(8,128)(2,1)}, bf16[1536,768]{1,0:T(8,128)(2,1)}, bf16[512,768]{1,0:T(8,128)(2,1)}, /*index=5*/f32[16,512]{1,0:T(8,128)}) custom-call(bf16[512,768]{1,0:T(8,128)(2,1)} %bitcast.58, bf16[512,768]{1,0:T(8,128)(2,1)} %copy-done.1, ...), custom_call_target="tpu_custom_call" | custom-call | tf_op jit(solution)/shard_map/attention/pallas_call | solution.py:63
  139.0 6.5 router.1
  145.5 17.6 %collective-permute-start.2 = (bf16[528,768]{1,0:T(8,128)(2,1)}, bf16[528,768]{1,0:T(8,128)(2,1)S(1)}, u32[]{:S(2)}, u32[]{:S(2)}) collective-permute-start(bf16[528,768]{1,0:T(8,128)(2,1)} %get-tuple-element.59.hp_ref.refs_0_), channel_id=1, source_target_pairs={{0,1},{1,0},{2,3},{3,2},{4,5},{5,4},{6,7},{7,6},{8,9},{9,8},{10,11... | collective-permute-start | bytes 2433032 | tf_op jit(solution)/shard_map/ppermute | solution.py:581
  171.1 117.3 %collective-permute-done.6.refs_6_ = bf16[512,768]{1,0:T(8,128)(2,1)S(1)} collective-permute-done((bf16[512,768]{1,0:T(8,128)(2,1)}, bf16[512,768]{1,0:T(8,128)(2,1)S(1)}, u32[]{:S(2)}, u32[]{:S(2)}) %collective-permute-start.6) | collective-permute-done | bytes 786464 | tf_op jit(solution)/shard_map/ppermute | solution.py:581
  290.2 69.2 %experts.1 = (bf16[512,768]{1,0:T(8,128)(2,1)}, bf16[512,768]{1,0:T(8,128)(2,1)}, bf16[512,768]{1,0:T(8,128)(2,1)}, bf16[512,768]{1,0:T(8,128)(2,1)}, bf16[528,7...) custom-call(s32[32]{0:T(128)} %reshape_squeeze.3.cnt_ref, ...), custom_call_target="tpu_custom_call" | custom-call | tf_op jit(solution)/shard_map/experts/pallas_call | solution.py:526
  359.4 15.4 %collective-permute-start.11 = (bf16[528,768]{1,0:T(8,128)(2,1)}, bf16[528,768]{1,0:T(8,128)(2,1)S(1)}, u32[]{:S(2)}, u32[]{:S(2)}) collective-permute-start(bf16[528,768]{1,0:T(8,128)(2,1)} %get-tuple-element.73), channel_id=1, source_target_pairs={{0,1},{1,0},{2,3},{3,2},{4,5},{5,4},{6,7},{7,6},{8,9},{9,8},{10,11... | collective-permute-start | bytes 2433032 | tf_op jit(solution)/shard_map/ppermute | solution.py:581
  377.8 4.7 local_experts.1
  382.6 28.1 %collective-permute-done.11.c1_ref = bf16[528,768]{1,0:T(8,128)(2,1)S(1)} collective-permute-done((bf16[528,768]{1,0:T(8,128)(2,1)}, bf16[528,768]{1,0:T(8,128)(2,1)S(1)}, u32[]{:S(2)}, u32[]{:S(2)}) %collective-permute-start.11) | collective-permute-done | bytes 811040 | tf_op jit(solution)/shard_map/ppermute | solution.py:581
  410.6 21.1 %collective-permute-done.12.c2_ref = bf16[528,768]{1,0:T(8,128)(2,1)} collective-permute-done((bf16[528,768]{1,0:T(8,128)(2,1)}, bf16[528,768]{1,0:T(8,128)(2,1)}, u32[]{:S(2)}, u32[]{:S(2)}) %collective-permute-start.12) | collective-permute-done | bytes 811040 | tf_op jit(solution)/shard_map/ppermute | solution.py:581
  431.8 9.3 %middle_back.1 = (f32[512,768]{1,0:T(8,128)}, bf16[512,768]{1,0:T(8,128)(2,1)}, bf16[512,768]{1,0:T(8,128)(2,1)}, f32[16,512]{1,0:T(8,128)}, f32[16,512]{1,0:T(8,128)}, /*index=5*/f32[24,768]{1,0:T(8,128)}) custom-call(s32[1]{0:T(128)} %bitcast.t_ref, bf16[528,768]{1,0:T(8,128)(2,1)} %get-tuple-element.72.c0_ref, bf16[528,768]{1,0:T(8,128)(2,1)} %copy-done.7, ...), custom_call_target="tpu_custom_call" | custom-call | tf_op jit(solution)/shard_map/middle_back/pallas_call | solution.py:63
  441.2 35.4 %attention_back.1 = (bf16[512,768]{1,0:T(8,128)(2,1)}, bf16[1536,768]{1,0:T(8,128)(2,1)}, bf16[1536,768]{1,0:T(8,128)(2,1)}, f32[512,768]{1,0:T(8,128)}, bf16[51...) custom-call(bf16[512,768]{1,0:T(8,128)(2,1)} %get-tuple-element.69.q_ref, bf16[1536,768]{1,0:T(8,128)(2,1)} %get-tuple-element.70.k_ref, ...), custom_call_target="tpu_custom_call" | custom-call | tf_op jit(solution)/shard_map/attention_back/pallas_call | solution.py:63
  476.5 13.2 %attention_grads.1 = (bf16[768,3072]{1,0:T(8,128)(2,1)}, f32[8,768]{1,0:T(8,128)}) custom-call(bf16[512,768]{1,0:T(8,128)(2,1)} %bitcast.60, bf16[512,768]{1,0:T(8,128)(2,1)} %copy-done.1, bf16[512,768]{1,0:T(8,128)(2,1)} %copy-done.2, bf16[1536,768]{1,0:T(8,128)(2,1)} %get-tuple-element.89.h_ref, bf16[512,768]{1,0:T(8,128)(2,1)} %get-tuple-element.90.dq_ref, ...), custom_call_target="tpu_custom_call" | custom-call | tf_op jit(solution)/shard_map/attention_grads/pallas_call | solution.py:63
  492.6 16.8 %collective-permute-start.9 = (bf16[512,768]{1,0:T(8,128)(2,1)}, bf16[512,768]{1,0:T(8,128)(2,1)S(1)}, u32[]{:S(2)}, u32[]{:S(2)}) collective-permute-start(bf16[512,768]{1,0:T(8,128)(2,1)} %get-tuple-element.67), channel_id=1, source_target_pairs={{0,2},{1,3},{2,0},{3,1},{4,6},{5,7},{6,4},{7,5},{8,10},{9,11},{10,... | collective-permute-start | bytes 2359304 | tf_op jit(solution)/shard_map/ppermute | solution.py:581
  512.1 57.0 %collective-permute-done.9 = bf16[512,768]{1,0:T(8,128)(2,1)S(1)} collective-permute-done((bf16[512,768]{1,0:T(8,128)(2,1)}, bf16[512,768]{1,0:T(8,128)(2,1)S(1)}, u32[]{:S(2)}, u32[]{:S(2)}) %collective-permute-start.9) | collective-permute-done | bytes 786464 | tf_op jit(solution)/shard_map/ppermute | solution.py:581
  574.7 44.3 %collective-permute-done.15.r2_ref = bf16[512,768]{1,0:T(8,128)(2,1)} collective-permute-done((bf16[512,768]{1,0:T(8,128)(2,1)S(1)}, bf16[512,768]{1,0:T(8,128)(2,1)}, u32[]{:S(2)}, u32[]{:S(2)}) %collective-permute-start.15) | collective-permute-done | bytes 786464 | tf_op jit(solution)/shard_map/ppermute | solution.py:584
  619.0 4.3 final_back.1
  628.4 65.1 %all-gather.1 = f32[32,1,768]{2,1,0:T(1,128)S(1)} all-gather(f32[1,1,768]{2,1,0:T(1,128)S(1)} %slice_bitcast_fusion.3), channel_id=1, replica_groups=mesh['dp'=8,'tensor'=4] {'dp','tensor'}, dimensions={0}, use_global_device_ids=true | all-gather | bytes 101376 | tf_op jit(solution)/shard_map/all_gather | solution.py:667
  712.1 7.4 collective-permute-done.17
  721.0 24.5 %reduce-scatter.5.cloned.1.call-done = bf16[96,12288]{1,0:T(8,128)(2,1)} async-done(((bf16[768,12288]{1,0:T(8,128)(2,1)}), bf16[96,12288]{1,0:T(8,128)(2,1)}) %reduce-scatter.5.cloned.1.call-update) | async-done | bytes 2359312 | tf_op jit(solution)/shard_map/reduce_scatter | solution.py:642
  (138 shorter events, 91.1 us)
Async XLA Ops:
  7.2 96.3 %all-gather.6.cloned.1.call-start = ((), (), s32[]{:S(2)}) async-start(), calls=%async_computation.6 | async-start | bytes 5308416 | tf_op jit(solution)/shard_map/all_gather | solution.py:588
  32.5 257.0 %all-gather.8.cloned.1.call-start = ((), (), s32[]{:S(2)}) async-start(), calls=%async_computation.7 | async-start | bytes 21233664 | tf_op jit(solution)/shard_map/all_gather | solution.py:590
  57.9 25.6 %all-to-all-start.1 = ((bf16[8,64,768]{2,1,0:T(8,128)(2,1)}), bf16[8,64,768]{2,1,0:T(8,128)(2,1)}, u32[]{:S(2)}, u32[]{:S(2)}) async-start(bf16[8,64,768]{2,1,0:T(8,128)(2,1)} %bitcast.72), calls=%async_computation.1 | async-start | bytes 1572864 | tf_op jit(solution)/shard_map/all_to_all | solution.py:602
  62.1 636.1 %all-gather.10.cloned.1.call-start = ((), (), s32[]{:S(2)}) async-start(), calls=%async_computation.10 | async-start | bytes 2433024 | tf_op jit(solution)/shard_map/all_gather | solution.py:651
  65.3 24.8 %collective-permute-start = (bf16[512,768]{1,0:T(8,128)(2,1)S(1)}, bf16[512,768]{1,0:T(8,128)(2,1)S(1)}, u32[]{:S(2)}, u32[]{:S(2)}) collective-permute-start(bf16[512,768]{1,0:T(8,128)(2,1)S(1)} %bitcast.56), channel_id=1, source_target_pairs={{0,1},{1,2},{2,3},{4,5},{5,6},{6,7},{8,9},{9,10},{10,11},{12,13},{... | collective-permute-start | bytes 2359304 | tf_op jit(solution)/shard_map/ppermute | solution.py:584
  68.7 34.8 %collective-permute-start.1 = (bf16[512,768]{1,0:T(8,128)(2,1)S(1)}, bf16[512,768]{1,0:T(8,128)(2,1)S(1)}, u32[]{:S(2)}, u32[]{:S(2)}) collective-permute-start(bf16[512,768]{1,0:T(8,128)(2,1)S(1)} %bitcast.57), channel_id=1, source_target_pairs={{0,2},{1,3},{4,6},{5,7},{8,10},{9,11},{12,14},{13,15},{16,18},{17,... | collective-permute-start | bytes 2359304 | tf_op jit(solution)/shard_map/ppermute | solution.py:584
  83.5 84.5 %collective-permute-start.5 = (bf16[512,768]{1,0:T(8,128)(2,1)}, bf16[512,768]{1,0:T(8,128)(2,1)}, u32[]{:S(2)}, u32[]{:S(2)}) collective-permute-start(bf16[512,768]{1,0:T(8,128)(2,1)} %bitcast.16.g_ref.refs_4_), channel_id=1, source_target_pairs={{0,1},{1,0},{2,3},{3,2},{4,5},{5,4},{6,7},{7,6},{8,9},{9,8},{10,11... | collective-permute-start | bytes 2359304 | tf_op jit(solution)/shard_map/ppermute | solution.py:581
  145.5 142.8 %collective-permute-start.2 = (bf16[528,768]{1,0:T(8,128)(2,1)}, bf16[528,768]{1,0:T(8,128)(2,1)S(1)}, u32[]{:S(2)}, u32[]{:S(2)}) collective-permute-start(bf16[528,768]{1,0:T(8,128)(2,1)} %get-tuple-element.59.hp_ref.refs_0_), channel_id=1, source_target_pairs={{0,1},{1,0},{2,3},{3,2},{4,5},{5,4},{6,7},{7,6},{8,9},{9,8},{10,11... | collective-permute-start | bytes 2433032 | tf_op jit(solution)/shard_map/ppermute | solution.py:581
  163.1 126.2 %collective-permute-start.3 = (bf16[528,768]{1,0:T(8,128)(2,1)}, bf16[528,768]{1,0:T(8,128)(2,1)}, u32[]{:S(2)}, u32[]{:S(2)}) collective-permute-start(bf16[528,768]{1,0:T(8,128)(2,1)} %get-tuple-element.59.hp_ref.refs_0_), channel_id=1, source_target_pairs={{0,2},{1,3},{2,0},{3,1},{4,6},{5,7},{6,4},{7,5},{8,10},{9,11},{10,... | collective-permute-start | bytes 2433032 | tf_op jit(solution)/shard_map/ppermute | solution.py:581
  166.5 123.0 %collective-permute-start.4 = (bf16[528,768]{1,0:T(8,128)(2,1)}, bf16[528,768]{1,0:T(8,128)(2,1)}, u32[]{:S(2)}, u32[]{:S(2)}) collective-permute-start(bf16[528,768]{1,0:T(8,128)(2,1)} %get-tuple-element.59.hp_ref.refs_0_), channel_id=1, source_target_pairs={{0,3},{1,2},{2,1},{3,0},{4,7},{5,6},{6,5},{7,4},{8,11},{9,10},{10,... | collective-permute-start | bytes 2433032 | tf_op jit(solution)/shard_map/ppermute | solution.py:581
  166.5 121.9 %collective-permute-start.6 = (bf16[512,768]{1,0:T(8,128)(2,1)}, bf16[512,768]{1,0:T(8,128)(2,1)S(1)}, u32[]{:S(2)}, u32[]{:S(2)}) collective-permute-start(bf16[512,768]{1,0:T(8,128)(2,1)} %bitcast.16.g_ref.refs_4_), channel_id=1, source_target_pairs={{0,2},{1,3},{2,0},{3,1},{4,6},{5,7},{6,4},{7,5},{8,10},{9,11},{10,... | collective-permute-start | bytes 2359304 | tf_op jit(solution)/shard_map/ppermute | solution.py:581
  168.0 120.4 %collective-permute-start.7 = (bf16[512,768]{1,0:T(8,128)(2,1)}, bf16[512,768]{1,0:T(8,128)(2,1)S(1)}, u32[]{:S(2)}, u32[]{:S(2)}) collective-permute-start(bf16[512,768]{1,0:T(8,128)(2,1)} %bitcast.16.g_ref.refs_4_), channel_id=1, source_target_pairs={{0,3},{1,2},{2,1},{3,0},{4,7},{5,6},{6,5},{7,4},{8,11},{9,10},{10,... | collective-permute-start | bytes 2359304 | tf_op jit(solution)/shard_map/ppermute | solution.py:581
  359.4 51.3 %collective-permute-start.11 = (bf16[528,768]{1,0:T(8,128)(2,1)}, bf16[528,768]{1,0:T(8,128)(2,1)S(1)}, u32[]{:S(2)}, u32[]{:S(2)}) collective-permute-start(bf16[528,768]{1,0:T(8,128)(2,1)} %get-tuple-element.73), channel_id=1, source_target_pairs={{0,1},{1,0},{2,3},{3,2},{4,5},{5,4},{6,7},{7,6},{8,9},{9,8},{10,11... | collective-permute-start | bytes 2433032 | tf_op jit(solution)/shard_map/ppermute | solution.py:581
  374.8 57.0 %collective-permute-start.12 = (bf16[528,768]{1,0:T(8,128)(2,1)}, bf16[528,768]{1,0:T(8,128)(2,1)}, u32[]{:S(2)}, u32[]{:S(2)}) collective-permute-start(bf16[528,768]{1,0:T(8,128)(2,1)} %get-tuple-element.74), channel_id=1, source_target_pairs={{0,2},{1,3},{2,0},{3,1},{4,6},{5,7},{6,4},{7,5},{8,10},{9,11},{10,... | collective-permute-start | bytes 2433032 | tf_op jit(solution)/shard_map/ppermute | solution.py:581
  375.7 56.0 %collective-permute-start.13 = (bf16[528,768]{1,0:T(8,128)(2,1)}, bf16[528,768]{1,0:T(8,128)(2,1)}, u32[]{:S(2)}, u32[]{:S(2)}) collective-permute-start(bf16[528,768]{1,0:T(8,128)(2,1)} %get-tuple-element.75), channel_id=1, source_target_pairs={{0,3},{1,2},{2,1},{3,0},{4,7},{5,6},{6,5},{7,4},{8,11},{9,10},{10,... | collective-permute-start | bytes 2433032 | tf_op jit(solution)/shard_map/ppermute | solution.py:581
  441.1 259.2 %reduce-scatter.3.cloned.1.call-start = ((), (), s32[]{:S(2)}) async-start(), calls=%async_computation.8 | async-start | bytes 5308416 | tf_op jit(solution)/shard_map/reduce_scatter | solution.py:677
  489.7 255.8 %reduce-scatter.5.cloned.1.call-start = ((), (), s32[]{:S(2)}) async-start(), calls=%async_computation.9 | async-start | bytes 21233664 | tf_op jit(solution)/shard_map/reduce_scatter | solution.py:642
  490.3 21.8 %collective-permute-start.10 = (bf16[512,768]{1,0:T(8,128)(2,1)}, bf16[512,768]{1,0:T(8,128)(2,1)S(1)}, u32[]{:S(2)}, u32[]{:S(2)}) collective-permute-start(bf16[512,768]{1,0:T(8,128)(2,1)} %get-tuple-element.68), channel_id=1, source_target_pairs={{0,3},{1,2},{2,1},{3,0},{4,7},{5,6},{6,5},{7,4},{8,11},{9,10},{10,... | collective-permute-start | bytes 2359304 | tf_op jit(solution)/shard_map/ppermute | solution.py:581
  492.6 76.5 %collective-permute-start.9 = (bf16[512,768]{1,0:T(8,128)(2,1)}, bf16[512,768]{1,0:T(8,128)(2,1)S(1)}, u32[]{:S(2)}, u32[]{:S(2)}) collective-permute-start(bf16[512,768]{1,0:T(8,128)(2,1)} %get-tuple-element.67), channel_id=1, source_target_pairs={{0,2},{1,3},{2,0},{3,1},{4,6},{5,7},{6,4},{7,5},{8,10},{9,11},{10,... | collective-permute-start | bytes 2359304 | tf_op jit(solution)/shard_map/ppermute | solution.py:581
  509.5 59.6 %collective-permute-start.8 = (bf16[512,768]{1,0:T(8,128)(2,1)}, bf16[512,768]{1,0:T(8,128)(2,1)S(1)}, u32[]{:S(2)}, u32[]{:S(2)}) collective-permute-start(bf16[512,768]{1,0:T(8,128)(2,1)} %get-tuple-element.66), channel_id=1, source_target_pairs={{0,1},{1,0},{2,3},{3,2},{4,5},{5,4},{6,7},{7,6},{8,9},{9,8},{10,11... | collective-permute-start | bytes 2359304 | tf_op jit(solution)/shard_map/ppermute | solution.py:581
  509.5 65.2 %collective-permute-start.14 = (bf16[512,768]{1,0:T(8,128)(2,1)}, bf16[512,768]{1,0:T(8,128)(2,1)}, u32[]{:S(2)}, u32[]{:S(2)}) collective-permute-start(bf16[512,768]{1,0:T(8,128)(2,1)} %get-tuple-element.83.d1_ref), channel_id=1, source_target_pairs={{1,0},{2,1},{3,2},{5,4},{6,5},{7,6},{9,8},{10,9},{11,10},{13,12},{... | collective-permute-start | bytes 2359304 | tf_op jit(solution)/shard_map/ppermute | solution.py:584
  510.8 108.3 %collective-permute-start.15 = (bf16[512,768]{1,0:T(8,128)(2,1)S(1)}, bf16[512,768]{1,0:T(8,128)(2,1)}, u32[]{:S(2)}, u32[]{:S(2)}) collective-permute-start(bf16[512,768]{1,0:T(8,128)(2,1)S(1)} %copy-done.8), channel_id=1, source_target_pairs={{2,0},{3,1},{6,4},{7,5},{10,8},{11,9},{14,12},{15,13},{18,16},{19,... | collective-permute-start | bytes 2359304 | tf_op jit(solution)/shard_map/ppermute | solution.py:584
  570.6 52.8 %all-to-all-start.2 = ((bf16[8,64,768]{2,1,0:T(8,128)(2,1)}), bf16[8,64,768]{2,1,0:T(8,128)(2,1)S(1)}, u32[]{:S(2)}, u32[]{:S(2)}) async-start(bf16[8,64,768]{2,1,0:T(8,128)(2,1)} %bitcast.17), calls=%async_computation.2 | async-start | bytes 1572864 | tf_op jit(solution)/shard_map/all_to_all | solution.py:673
  623.3 71.4 %all-to-all-start.3 = ((bf16[8,64,768]{2,1,0:T(8,128)(2,1)}), bf16[8,64,768]{2,1,0:T(8,128)(2,1)}, u32[]{:S(2)}, u32[]{:S(2)}) async-start(bf16[8,64,768]{2,1,0:T(8,128)(2,1)} %bitcast.66), calls=%async_computation.3 | async-start | bytes 1572864 | tf_op jit(solution)/shard_map/all_to_all | solution.py:674
  (25 other events, 726.4 us)
Sparse Core Ops, SparseCore 0:
  32.6 53.6 all-gather.5
  88.2 98.5 all-gather.7
  441.2 101.2 all-gather.9
  545.9 61.6 reduce-scatter.2
  611.0 134.4 reduce-scatter.4

commit v2 on v1

v2 whole, which is shorter than its diff:
```python
import functools
import math

import jax
import jax.numpy as jnp
from jax import lax
from jax.experimental import pallas as pl
from jax.experimental.pallas import tpu as pltpu
from jax.sharding import PartitionSpec as P

D = 768
HEAD_DIM = 64
HEADS = 12
EXPERTS = 8
LONGEST = 1024
EPSILON = 1e-6
MASKED = -1e30
F32, BF16, I32 = jnp.float32, jnp.bfloat16, jnp.int32
NN = (((1,), (0,)), ((), ()))
NT = (((1,), (1,)), ((), ()))
TN = (((0,), (0,)), ((), ()))
SCORE_SCALE = HEAD_DIM**-0.5
LOG2E = 1.4426950408889634
TILE = 160
ROWS = 256
SPARE = 16
VMEM_CAP = 66_000_000


def mm(a, b, dims):
    return lax.dot_general(a, b, dims, preferred_element_type=F32)


def iota(shape, axis):
    return lax.broadcasted_iota(I32, shape, axis)


def pick(cond):
    return jnp.where(cond, 1.0, 0.0).astype(BF16)


def split2(v):
    high = v.astype(BF16)
    return high, (v - high.astype(F32)).astype(BF16)


def split3(v):
    high = v.astype(BF16)
    rest = v - high.astype(F32)
    mid = rest.astype(BF16)
    return high, mid, (rest - mid.astype(F32)).astype(BF16)


def vmem():
    return pl.BlockSpec(memory_space=pltpu.VMEM)


def smem():
    return pl.BlockSpec(memory_space=pltpu.SMEM)


def call(body, name, outs, operands, scalars=0, scratch=(), meet=None):
    return pl.pallas_call(
        body,
        name=name,
        out_shape=[jax.ShapeDtypeStruct(*o) for o in outs],
        in_specs=[smem()] * scalars + [vmem()] * (len(operands) - scalars),
        out_specs=[vmem()] * len(outs),
        scratch_shapes=list(scratch),
        compiler_params=pltpu.CompilerParams(
            vmem_limit_bytes=VMEM_CAP, collective_id=meet, has_side_effects=meet is not None
        ),
    )(*operands)


def deal_body(n_dp, deal_ref, tok_ref, cot_ref, routes_ref, xs_ref, gs_ref, pos_ref, slot_ref, cnt_ref):
    rows = tok_ref.shape[0]
    first, second = iota((rows, rows), 0), iota((rows, rows), 1)
    before = pick(first < second)
    deal = deal_ref[...]
    hit = iota((n_dp, rows), 0) == deal
    rank = mm(pick(hit), before, NN)
    rank = jnp.sum(jnp.where(hit, rank, 0.0), axis=0, keepdims=True).astype(I32)
    pos = deal * (rows // n_dp) + rank
    pos_ref[...] = pos
    place = pick(first == pos)
    xs_ref[...] = mm(place, tok_ref[...], NN).astype(BF16)
    gs_ref[...] = mm(place, cot_ref[...], NN).astype(BF16)
    expert = iota((EXPERTS, rows), 0)
    for j in range(routes_ref.shape[0]):
        route = routes_ref[j]
        named = (expert == route[0:1]) | (expert == route[1:2])
        ahead = mm(pick(named), before, NN).astype(I32)
        slot_ref[j] = jnp.where(named, ahead, -1)
        total = jnp.sum(jnp.where(named, 1.0, 0.0), axis=1, keepdims=True).astype(I32)
        cnt_ref[j] = jnp.broadcast_to(total, (EXPERTS, 128))


def restore_body(pos_ref, a_ref, b_ref, oa_ref, ob_ref):
    rows = a_ref.shape[0]
    place = pick(iota((rows, rows), 0) == pos_ref[...])
    oa_ref[...] = mm(place, a_ref[...], TN).astype(BF16)
    ob_ref[...] = mm(place, b_ref[...], TN).astype(BF16)


class Line:
    def __init__(self, size):
        self.size = size
        self.place = lax.axis_index("tensor")
        self.sent = {k: [] for k in range(size)}

    def each(self, body):
        for k in range(self.size):
            pl.when(self.place == k)(functools.partial(body, k))

    def enter(self):
        sem = pltpu.get_barrier_semaphore()

        def greet(k):
            near = [n for n in (k - 1, k + 1) if 0 <= n < self.size]
            for n in near:
                pl.semaphore_signal(sem, 1, device_id={"tensor": self.place + (n - k)}, device_id_type=pl.DeviceIdType.MESH)
            pl.semaphore_wait(sem, len(near))

        self.each(greet)

    def copy(self, hop, src, dst, sems):
        return pltpu.make_async_remote_copy(
            src_ref=src,
            dst_ref=dst,
            send_sem=sems[0],
            recv_sem=sems[1],
            device_id={"tensor": self.place + hop},
            device_id_type=pl.DeviceIdType.MESH,
        )

    def send(self, k, to, refs):
        self.copy(to - k, *refs()).start()
        self.sent[k].append((to - k, refs))

    def arrived(self, k, dst, sems):
        self.copy((k ^ 1) - k, dst, dst, sems).wait_recv()

    def leave(self):
        def drain(k):
            for hop, refs in self.sent[k]:
                self.copy(hop, *refs()).wait_send()

        self.each(drain)


def sum_events(size, k):
    events = []
    for dest in range(size):
        if dest >= k and dest > 0:
            events.append((0 if k == 0 else size - 1 - dest + k, 1, dest))
        if dest <= k and dest < size - 1:
            events.append((0 if k == size - 1 else dest + size - 1 - k, -1, dest))
    drop = [(t, w, d) for t, w, d in events if (k == 0 and w == 1 and d == 0) or (k == size - 1 and w == -1 and d == k)]
    return sorted(ev for ev in events if ev not in drop)


def turn(u):
    low = (iota((1, u.shape[1]), 1) % HEAD_DIM) < HEAD_DIM // 2
    half = HEAD_DIM // 2
    return jnp.where(low, pltpu.roll(u, u.shape[1] - half, 1), pltpu.roll(u, half, 1))


def wide(table):
    return jnp.concatenate([table] * (D // 128), axis=1)


def key_bias(start, block, first_row, base):
    window = LONGEST + block
    key = iota((window, block), 0) + first_row
    row = iota((1, block), 1) + (base + first_row)
    return jnp.where((key >= start) & (key <= row), 0.0, MASKED)


def router_part(route, o_ref, w_ref, x_ref, gain_ref, res_ref, wrc_ref, x1_ref, hp_ref, gt_ref):
    rows = o_ref.shape[0]
    x1 = x_ref[...].astype(F32) + mm(o_ref[...], w_ref[:, 3 * D : 4 * D], NT)
    x1_ref[...] = x1
    h = x1 * lax.rsqrt(jnp.mean(x1 * x1, axis=1, keepdims=True) + EPSILON) * gain_ref[...]
    h = h.astype(BF16)
    hp_ref[0:rows, :] = h
    high, mid, low = split3(wrc_ref[...])
    z = mm(low, h, NT) + mm(mid, h, NT) + mm(high, h, NT) + res_ref[...]
    expert = iota(z.shape, 0)
    named0, named1 = expert == route[0:1], expert == route[1:2]
    c0 = jnp.sum(jnp.where(named0, z, 0.0), axis=0, keepdims=True)
    c1 = jnp.sum(jnp.where(named1, z, 0.0), axis=0, keepdims=True)
    top = jnp.maximum(c0, c1)
    e0, e1 = jnp.exp(c0 - top), jnp.exp(c1 - top)
    g0, g1 = e0 / (e0 + e1), e1 / (e0 + e1)
    table = [g0, g1]
    for j in range(2):
        l0, l1 = z[12 + 2 * j : 13 + 2 * j], z[13 + 2 * j : 14 + 2 * j]
        top = jnp.maximum(l0, l1)
        m0, m1 = jnp.exp(l0 - top), jnp.exp(l1 - top)
        table += [m0 / (m0 + m1), m1 / (m0 + m1)]
    gt_ref[...] = jnp.concatenate(table + [jnp.zeros((2, rows), F32)], axis=0)
    gates = jnp.where(named0, g0, jnp.where(named1, g1, 0.0))
    gates = jnp.where(expert < EXPERTS, gates, 0.0)
    hp_ref[rows : rows + SPARE, :] = jnp.concatenate([gates, jnp.zeros((SPARE, D - rows), F32)], axis=1).astype(BF16)


def local_part(route, x1_ref, hp_ref, g_ref, gt_ref, v_ref, xl_ref, dhl_ref, sm_ref, gv_ref):
    rows = x1_ref.shape[0]
    h, g = hp_ref[0:rows, :], g_ref[...]
    hf, gf = h.astype(F32), g.astype(F32)
    low0 = gt_ref[0:1].astype(BF16).astype(F32)
    low1 = gt_ref[1:2].astype(BF16).astype(F32)

    def weight(e):
        return jnp.where(route[0:1] == e, low0, 0.0) + jnp.where(route[1:2] == e, low1, 0.0)

    copy, first, second = weight(EXPERTS + 1), weight(EXPERTS + 2), weight(EXPERTS + 3)
    m00, m01, m10, m11 = gt_ref[2:3], gt_ref[3:4], gt_ref[4:5], gt_ref[5:6]
    a = copy + first * m00 + second * m10
    b0, b1 = first * m01, second * m11
    table = jnp.concatenate([a, b0, b1, jnp.zeros((125, rows), F32)], axis=0).T
    ac, b0c, b1c = table[:, 0:1], table[:, 1:2], table[:, 2:3]
    v = v_ref[...]
    xl_ref[...] = x1_ref[...] + ac * hf + b0c * v[0:1] + b1c * v[1:2]
    dhl_ref[...] = ac * gf
    ones = jnp.ones((8, D), BF16)
    high, low = split2(hf * gf)
    gh = (mm(ones, high, NT) + mm(ones, low, NT))[0:1]
    vh, vm, vl = split3(v)
    gvs = mm(vl, g, NT) + mm(vm, g, NT) + mm(vh, g, NT)
    gv0, gv1 = gvs[0:1], gvs[1:2]
    zero = jnp.zeros((9, rows), F32)
    dl0 = first * m00 * m01 * (gh - gv0)
    dl1 = second * m10 * m11 * (gh - gv1)
    sm_ref[...] = jnp.concatenate(
        [zero, gh, m00 * gh + m01 * gv0, m10 * gh + m11 * gv1, dl0, -dl0, dl1, -dl1], axis=0
    )
    bh, bm, bl = split3(jnp.concatenate([b0, b1, jnp.zeros((6, rows), F32)], axis=0))
    gv_ref[...] = mm(bl, g, NN) + mm(bm, g, NN) + mm(bh, g, NN)


def forward_body(size, x0_ref, g0_ref, w_ref, gain_ref, gain2_ref, cos_ref, sin_ref, start_ref, res_ref, wrc_ref, routes_ref, v8_ref,
                 x1_ref, x2_ref, h_ref, q_ref, k_ref, v_ref, o_ref, lse_ref, xm_ref, hp_ref, gall_ref, gt_ref, xl_ref,
                 dhl_ref, sm_ref, gv_ref,
                 bias_ref, sx, rx, sgu, rgu, sgd, rgd, shu, rhu, shd, rhd):
    rows = x0_ref.shape[0]
    step = 256
    line = Line(size)
    t = line.place
    last = size - 1
    line.enter()

    def begin(k):
        if k < last:
            line.send(k, k + 1, lambda: (x0_ref, x1_ref, (sx.at[0], rx.at[0])))
        if k > 0:
            line.send(k, k - 1, lambda: (g0_ref, gall_ref.at[k], (sgd.at[0], rgd.at[0])))

    line.each(begin)
    gain = gain_ref[...]

    def project_chunk(c, x_ref):
        def project(i, _):
            at = pl.multiple_of(i * step, step)
            x = x_ref[pl.ds(at, step), :].astype(F32)
            h = x * lax.rsqrt(jnp.mean(x * x, axis=1, keepdims=True) + EPSILON) * gain
            h = h.astype(BF16)
            to = pl.ds(pl.multiple_of(c * rows + i * step, step), step)
            h_ref[to, :] = h
            cos, sin = wide(cos_ref[to, :]), wide(sin_ref[to, :])
            k = mm(h, w_ref[:, D : 2 * D], NN)
            k_ref[to, :] = (k * cos + turn(k) * sin).astype(BF16)
            v_ref[to, :] = mm(h, w_ref[:, 2 * D : 3 * D], NN).astype(BF16)
            if c == 2:
                q = mm(h, w_ref[:, 0:D], NN)
                q_ref[pl.ds(at, step), :] = (q * cos + turn(q) * sin).astype(BF16)
            return 0

        lax.fori_loop(0, rows // step, project, 0)

    project_chunk(2, x0_ref)
    gall_ref[t] = g0_ref[...]

    def second(k):
        if k > 0:
            line.arrived(k, x1_ref, (sx.at[0], rx.at[0]))
        else:
            x1_ref[...] = jnp.zeros_like(x1_ref)
        if 0 < k < last:
            line.send(k, k + 1, lambda: (x1_ref, x2_ref, (sx.at[1], rx.at[1])))
        if k < last:
            line.send(k, k + 1, lambda: (g0_ref, gall_ref.at[k], (sgu.at[0], rgu.at[0])))
            line.arrived(k, gall_ref.at[k + 1], (sgd.at[0], rgd.at[0]))
            if k > 0:
                line.send(k, k - 1, lambda: (gall_ref.at[k + 1], gall_ref.at[k + 1], (sgd.at[1], rgd.at[1])))

    line.each(second)
    project_chunk(1, x1_ref)

    def third(k):
        if k > 1:
            line.arrived(k, x2_ref, (sx.at[1], rx.at[1]))
        else:
            x2_ref[...] = jnp.zeros_like(x2_ref)
        if k + 2 <= last:
            line.arrived(k, gall_ref.at[k + 2], (sgd.at[1], rgd.at[1]))
            if k > 0:
                line.send(k, k - 1, lambda: (gall_ref.at[k + 2], gall_ref.at[k + 2], (sgd.at[2], rgd.at[2])))

    line.each(third)
    project_chunk(0, x2_ref)

    block = step
    window = LONGEST + block
    lane = iota((1, 128), 1) // HEAD_DIM
    for rb in range(rows // block):
        first = rb * block
        bias_ref[...] = key_bias(start_ref[:, first : first + block], block, first, LONGEST)

        def pair(i, _, first=first):
            lanes = pl.ds(pl.multiple_of(i * 128, 128), 128)
            k = k_ref[first : first + window, lanes]
            vt = v_ref[first : first + window, lanes].T
            q = q_ref[first : first + block, lanes]
            parts = []
            for half in range(2):
                qm = jnp.where(lane == half, q, jnp.zeros_like(q))
                s = mm(k, qm, NT) * (SCORE_SCALE * LOG2E) + bias_ref[...]
                top = jnp.max(s, axis=0, keepdims=True)
                p = jnp.exp2(s - top)
                total = jnp.sum(p, axis=0, keepdims=True)
                out = mm(vt[half * HEAD_DIM : (half + 1) * HEAD_DIM], p.astype(BF16), NN)
                parts.append(out * (1.0 / total))
                lse_ref[pl.ds(i * 2 + half, 1), first : first + block] = top + jnp.log2(total)
            o_ref[first : first + block, lanes] = jnp.concatenate(parts, axis=0).T.astype(BF16)
            return 0

        lax.fori_loop(0, HEADS // 2, pair, 0)
        if rb == 0:
            def fourth(k):
                if k > 0:
                    line.arrived(k, gall_ref.at[k - 1], (sgu.at[0], rgu.at[0]))
                    if k < last:
                        line.send(k, k + 1, lambda: (gall_ref.at[k - 1], gall_ref.at[k - 1], (sgu.at[1], rgu.at[1])))

            line.each(fourth)

    route = routes_ref[t]
    router_part(route, o_ref, w_ref, x0_ref, gain2_ref, res_ref, wrc_ref, xm_ref, hp_ref.at[t], gt_ref)

    def fifth(k):
        if k < last:
            line.send(k, k + 1, lambda: (hp_ref.at[k], hp_ref.at[k], (shu.at[0], rhu.at[0])))
        if k > 0:
            line.send(k, k - 1, lambda: (hp_ref.at[k], hp_ref.at[k], (shd.at[0], rhd.at[0])))
        if k > 1:
            line.arrived(k, gall_ref.at[k - 2], (sgu.at[1], rgu.at[1]))
            if k < last:
                line.send(k, k + 1, lambda: (gall_ref.at[k - 2], gall_ref.at[k - 2], (sgu.at[2], rgu.at[2])))

    line.each(fifth)
    local_part(route, xm_ref, hp_ref.at[t], g0_ref, gt_ref, v8_ref, xl_ref, dhl_ref, sm_ref, gv_ref)

    def sixth(k):
        for hop in range(2):
            up, down = k - 1 - hop, k + 1 + hop
            if up >= 0:
                line.arrived(k, hp_ref.at[up], (shu.at[hop], rhu.at[hop]))
                if k < last:
                    line.send(k, k + 1, lambda up=up, hop=hop: (hp_ref.at[up], hp_ref.at[up], (shu.at[hop + 1], rhu.at[hop + 1])))
            if down <= last:
                line.arrived(k, hp_ref.at[down], (shd.at[hop], rhd.at[hop]))
                if k > 0:
                    line.send(k, k - 1, lambda down=down, hop=hop: (hp_ref.at[down], hp_ref.at[down], (shd.at[hop + 1], rhd.at[hop + 1])))
        if k == last:
            line.arrived(k, hp_ref.at[0], (shu.at[2], rhu.at[2]))
            line.arrived(k, gall_ref.at[0], (sgu.at[2], rgu.at[2]))
        if k == 0:
            line.arrived(k, hp_ref.at[last], (shd.at[2], rhd.at[2]))
            line.arrived(k, gall_ref.at[last], (sgd.at[2], rgd.at[2]))

    line.each(sixth)
    line.leave()


def middle_part(route, dh_ref, gt_ref, sm_ref, wrc_ref, x1_ref, gain_ref, g_ref, h2_ref, w_ref, o_ref, gv_ref,
                dx_ref, da_ref, do_ref, delta_ref, dres_ref, small_ref):
    rows = x1_ref.shape[0]
    dgf = dh_ref[rows : rows + SPARE, 0:rows]
    dh = dh_ref[0:rows, :]
    dgate = jnp.concatenate([dgf[0:EXPERTS] + dgf[EXPERTS:], sm_ref[EXPERTS:SPARE]], axis=0)
    expert = iota((SPARE, rows), 0)
    named0, named1 = expert == route[0:1], expert == route[1:2]
    g0, g1 = gt_ref[0:1], gt_ref[1:2]
    d0 = jnp.sum(jnp.where(named0, dgate, 0.0), axis=0, keepdims=True)
    d1 = jnp.sum(jnp.where(named1, dgate, 0.0), axis=0, keepdims=True)
    inner = g0 * d0 + g1 * d1
    dz = jnp.where(named0, g0 * (d0 - inner), jnp.where(named1, g1 * (d1 - inner), 0.0))
    dres_ref[...] = dz
    dz = jnp.where(expert < 12, dz, sm_ref[...])
    zh, zm, zl = split3(dz)
    wh, wm, wl = split3(wrc_ref[...])
    dh = dh + (mm(zh, wl, TN) + mm(zl, wh, TN) + mm(zm, wm, TN) + mm(zh, wm, TN) + mm(zm, wh, TN) + mm(zh, wh, TN))
    h = h2_ref[...]
    small_ref[0:SPARE, :] = mm(zl, h, NN) + mm(zm, h, NN) + mm(zh, h, NN)
    x1 = x1_ref[...]
    r = lax.rsqrt(jnp.mean(x1 * x1, axis=1, keepdims=True) + EPSILON)
    xr = x1 * r
    grad_gain = jnp.sum(dh * xr, axis=0, keepdims=True)
    gv = gv_ref[...]
    small_ref[SPARE : SPARE + 8, :] = jnp.concatenate([gv[0:2], grad_gain, gv[3:8]], axis=0)
    scaled = dh * gain_ref[...]
    dx = g_ref[...].astype(F32) + r * (scaled - xr * jnp.mean(xr * scaled, axis=1, keepdims=True))
    dx_ref[...] = dx
    da = dx.astype(BF16)
    da_ref[...] = da
    do = mm(da, w_ref[:, 3 * D : 4 * D], NN).astype(BF16)
    do_ref[...] = do
    high, low = split2(do.astype(F32) * o_ref[...].astype(F32))
    heads = pick(iota((SPARE, D), 1) // HEAD_DIM == iota((SPARE, D), 0))
    delta_ref[...] = mm(heads, high, NT) + mm(heads, low, NT)


def backward_body(size, back_ref, out_ref, dhl_ref, gt_ref, sm_ref, routes_ref, wrc_ref, xm_ref, gain_ref, g_ref, h2_ref, w_ref,
                  o_ref, gv_ref, q_ref, k_ref, v_ref, lse_ref, start_ref, cos_ref, sin_ref, xl_ref,
                  dx_ref, da_ref, dres_ref, small_ref, dq_ref, dk_ref, dv_ref, y_ref,
                  bias_ref, dkf_ref, dvf_ref, dh_ref, do_ref, delta_ref, bu_ref, bd_ref, fu_ref, fd_ref,
                  sbu, rbu, sbd, rbd, sfu, rfu, sfd, rfd):
    rows = xm_ref.shape[0]
    packed = rows + SPARE
    cut = 272
    pieces = (slice(0, cut), slice(cut, packed))
    line = Line(size)
    t = line.place
    last = size - 1
    line.enter()

    def handle(k, way, dest, part, index, mine_ref, up_ref, down_ref, ups, downs):
        slot = dest - 1 if way == 1 else dest
        first = k == (0 if way == 1 else last)
        mine = mine_ref.at[dest, part]

        def refs():
            held = (up_ref if way == 1 else down_ref).at[slot, part]
            sems = tuple(s.at[slot, index] for s in (ups if way == 1 else downs))
            return mine_ref.at[dest, part] if first else held, held, sems

        _, held, sems = refs()
        if not first:
            line.arrived(k, held, sems)
        if dest != k:
            if not first:
                held[...] = (held[...].astype(F32) + mine[...].astype(F32)).astype(BF16)
            line.send(k, k + way, refs)

    def sum_back(k):
        for _, way, dest in sum_events(size, k):
            for index, part in enumerate(pieces):
                handle(k, way, dest, part, index, back_ref, bu_ref, bd_ref, (sbu, rbu), (sbd, rbd))

    def sum_out(k, now):
        for time, way, dest in sum_events(size, k):
            if time == now:
                handle(k, way, dest, slice(0, rows), 0, out_ref, fu_ref, fd_ref, (sfu, rfu), (sfd, rfd))

    line.each(sum_back)
    line.each(lambda k: sum_out(k, 0))
    dh_ref[...] = back_ref[t].astype(F32)

    @pl.when(t > 0)
    def _():
        dh_ref[...] += bu_ref[t - 1].astype(F32)

    @pl.when(t < last)
    def _():
        dh_ref[...] += bd_ref[t].astype(F32)

    dh_ref[0:rows, :] += dhl_ref[...]
    middle_part(routes_ref[t], dh_ref, gt_ref, sm_ref, wrc_ref, xm_ref, gain_ref, g_ref, h2_ref, w_ref, o_ref, gv_ref,
                dx_ref, da_ref, do_ref, delta_ref, dres_ref, small_ref)
    line.each(lambda k: sum_out(k, 1))

    block = 256
    window = LONGEST + block
    lane = iota((1, 128), 1) // HEAD_DIM
    for rb in range(rows // block):
        first = rb * block
        bias_ref[rb] = key_bias(start_ref[:, first : first + block], block, first, LONGEST)

    def pair(i, _):
        lanes = pl.ds(pl.multiple_of(i * 128, 128), 128)
        for rb in range(rows // block):
            first = rb * block
            k = k_ref[first : first + window, lanes]
            v = v_ref[first : first + window, lanes]
            kt = k.T
            q = q_ref[first : first + block, lanes]
            do = do_ref[first : first + block, lanes]
            dk = jnp.zeros((window, 128), F32)
            dv = jnp.zeros((window, 128), F32)
            parts = []
            for half in range(2):
                qm = jnp.where(lane == half, q, jnp.zeros_like(q))
                dom = jnp.where(lane == half, do, jnp.zeros_like(do))
                head = pl.ds(i * 2 + half, 1)
                s = mm(k, qm, NT) * (SCORE_SCALE * LOG2E) + bias_ref[rb]
                p = jnp.exp2(s - lse_ref[head, first : first + block])
                dp = mm(v, dom, NT)
                ds = (p * (dp - delta_ref[head, first : first + block])).astype(BF16)
                dv = dv + mm(p.astype(BF16), dom, NN)
                dk = dk + mm(ds, qm, NN)
                parts.append(mm(kt[half * HEAD_DIM : (half + 1) * HEAD_DIM], ds, NN))
            dq = jnp.concatenate(parts, axis=0).T * SCORE_SCALE
            at = slice(2 * rows + first, 2 * rows + first + block)
            dq_ref[first : first + block, lanes] = (dq * cos_ref[at, :] - turn(dq) * sin_ref[at, :]).astype(BF16)
            if first == 0:
                dkf_ref[0:window, :] = dk
                dvf_ref[0:window, :] = dv
            else:
                old = window - block
                dkf_ref[first : first + old, :] += dk[0:old]
                dvf_ref[first : first + old, :] += dv[0:old]
                dkf_ref[first + old : first + window, :] = dk[old:]
                dvf_ref[first + old : first + window, :] = dv[old:]
        dk = dkf_ref[...] * SCORE_SCALE
        dk_ref[:, lanes] = (dk * cos_ref[...] - turn(dk) * sin_ref[...]).astype(BF16)
        dv_ref[:, lanes] = dvf_ref[...].astype(BF16)
        return 0

    lax.fori_loop(0, HEADS // 4, pair, 0)
    line.each(lambda k: sum_out(k, 2))
    lax.fori_loop(HEADS // 4, HEADS // 2, pair, 0)
    line.each(lambda k: sum_out(k, 3))
    xl_ref[...] += out_ref[t].astype(F32)

    @pl.when(t > 0)
    def _():
        xl_ref[...] += fu_ref[t - 1].astype(F32)

    @pl.when(t < last)
    def _():
        xl_ref[...] += fd_ref[t].astype(F32)

    y_ref[...] = xl_ref[...].astype(BF16)
    line.leave()


def grads_body(size, x0_ref, x1_ref, x2_ref, h_ref, dq_ref, dk_ref, dv_ref, da_ref, o_ref, w_ref, dx_ref, gain_ref,
               gw_ref, gpart_ref, out_ref, d0_ref, d1_ref, d2_ref, ra_ref, rb_ref, sems_s, sems_r):
    rows = x0_ref.shape[0]
    line = Line(size)
    last = size - 1
    block = 256
    line.enter()

    def hidden(c, d_ref):
        def one(i, _):
            at = pl.ds(pl.multiple_of(i * block, block), block)
            to = pl.ds(pl.multiple_of(c * rows + i * block, block), block)
            total = mm(dk_ref[to, :], w_ref[:, D : 2 * D], NT) + mm(dv_ref[to, :], w_ref[:, 2 * D : 3 * D], NT)
            if c == 2:
                total = total + mm(dq_ref[at, :], w_ref[:, 0:D], NT)
            d_ref[at, :] = total.astype(d_ref.dtype)
            return 0

        lax.fori_loop(0, rows // block, one, 0)

    def gain_of(x_ref, d_ref):
        x = x_ref[...].astype(F32)
        r = lax.rsqrt(jnp.mean(x * x, axis=1, keepdims=True) + EPSILON)
        return jnp.sum(d_ref[...].astype(F32) * x * r, axis=0, keepdims=True)

    hidden(0, d2_ref)

    def first(k):
        if k > 1:
            line.send(k, k - 1, lambda: (d2_ref, ra_ref, (sems_s.at[0], sems_r.at[0])))

    line.each(first)
    hidden(1, d1_ref)
    gain = gain_of(x2_ref, d2_ref) + gain_of(x1_ref, d1_ref)
    h = h_ref[...]

    def weight(column, left, right_ref):
        for c in range(D // 256):
            cols = slice(c * 256, (c + 1) * 256)
            gw_ref[:, column * D + c * 256 : column * D + c * 256 + 256] = mm(left, right_ref[:, cols], TN).astype(BF16)

    weight(1, h, dk_ref)

    def second(k):
        if 0 < k < last:
            line.arrived(k, ra_ref, (sems_s.at[0], sems_r.at[0]))
            d1_ref[...] = (d1_ref[...].astype(F32) + ra_ref[...].astype(F32)).astype(BF16)
        if k > 0:
            line.send(k, k - 1, lambda: (d1_ref, rb_ref, (sems_s.at[1], sems_r.at[1])))

    line.each(second)
    hidden(2, d0_ref)
    gpart_ref[...] = jnp.broadcast_to(gain + gain_of(x0_ref, d0_ref), (8, D))
    weight(2, h, dv_ref)
    weight(0, h[2 * rows :], dq_ref)
    weight(3, da_ref[...], o_ref)

    def third(k):
        if k < last:
            line.arrived(k, rb_ref, (sems_s.at[1], sems_r.at[1]))
            d0_ref[...] += rb_ref[...].astype(F32)

    line.each(third)
    x = x0_ref[...].astype(F32)
    r = lax.rsqrt(jnp.mean(x * x, axis=1, keepdims=True) + EPSILON)
    xr = x * r
    scaled = d0_ref[...] * gain_ref[...]
    out_ref[...] = (dx_ref[...] + r * (scaled - xr * jnp.mean(xr * scaled, axis=1, keepdims=True))).astype(BF16)
    line.leave()


def experts_body(ff, chunks, cnt_ref, h_refs, g_refs, slot_ref, w_ref, o_refs, d_refs, gw_ref,
                 xbuf, gbuf, cbuf, onehot, fbuf, dbuf, gacc, gates, dgrow, off_ref, base_ref, nt_ref):
    rows = slot_ref.shape[2]
    e = pl.program_id(0)

    def match(j, expert, tile):
        slots = slot_ref[j, pl.ds(expert, 1), :]
        return (iota((TILE, rows), 0) + tile * TILE) == slots

    def store_rows(at, count, hit, x, gs, gate_row):
        to = pl.ds(pl.multiple_of(at, 16), TILE)
        keep = iota((TILE, 1), 0) < count
        col = jnp.sum(jnp.where(hit, gate_row, 0.0), axis=1, keepdims=True)
        xbuf[to, :] = jnp.where(keep, x, xbuf[to, :].astype(F32)).astype(BF16)
        gbuf[to, :] = jnp.where(keep, gs, gbuf[to, :].astype(F32)).astype(BF16)
        cbuf[to, :] = jnp.where(keep, jnp.broadcast_to(col, (TILE, 128)), cbuf[to, :])

    def round16(n):
        return ((n + 15) // 16) * 16

    @pl.when(e == 0)
    def _gather():
        at = jnp.int32(0)
        for ex in range(EXPERTS):
            base_ref[ex] = at
            here = at
            for j in range(chunks):
                off_ref[j * EXPERTS + ex] = here
                here = here + round16(cnt_ref[j * EXPERTS + ex])
            tiles = (here - at + (ROWS - 1)) // ROWS
            nt_ref[ex] = tiles
            tail = pl.ds(pl.multiple_of(here, 16), ROWS)
            xbuf[tail, :] = jnp.zeros((ROWS, D), BF16)
            gbuf[tail, :] = jnp.zeros((ROWS, D), BF16)
            cbuf[tail, :] = jnp.zeros((ROWS, 128), F32)
            at = at + tiles * ROWS
        for j in range(chunks):
            gates[...] = h_refs[j, rows : rows + SPARE, 0:rows].astype(F32)

            def two(i, _, j=j):
                hits = [match(j, 2 * i + half, 0) for half in range(2)]
                sel = jnp.concatenate([pick(hit) for hit in hits], axis=0)
                x = mm(sel, h_refs[j, 0:rows, :], NN)
                gs = mm(sel, g_refs[j], NN)
                for half in range(2):
                    ex = 2 * i + half
                    count = round16(jnp.minimum(cnt_ref[j * EXPERTS + ex], TILE))
                    part = slice(half * TILE, (half + 1) * TILE)
                    store_rows(off_ref[j * EXPERTS + ex], count, hits[half], x[part], gs[part], gates[pl.ds(ex, 1), :])
                return 0

            lax.fori_loop(0, EXPERTS // 2, two, 0)

            def rare(ex, _, j=j):
                def more(tile, _):
                    hit = match(j, ex, tile)
                    sel = pick(hit)
                    count = round16(jnp.minimum(cnt_ref[j * EXPERTS + ex] - tile * TILE, TILE))
                    store_rows(
                        off_ref[j * EXPERTS + ex] + tile * TILE,
                        count,
                        hit,
                        mm(sel, h_refs[j, 0:rows, :], NN),
                        mm(sel, g_refs[j], NN),
                        gates[pl.ds(ex, 1), :],
                    )
                    return 0

                return lax.fori_loop(1, (cnt_ref[j * EXPERTS + ex] + (TILE - 1)) // TILE, more, 0)

            lax.fori_loop(0, EXPERTS, rare, 0)

    gacc[...] = jnp.zeros_like(gacc)

    def tile_step(m, _):
        at = pl.ds(pl.multiple_of(base_ref[e] + m * ROWS, 16), ROWS)
        x = xbuf[at, :]
        gs = gbuf[at, :].astype(F32)
        gate = wide(cbuf[at, :])
        u = mm(x, w_ref[:, 0:ff], NN)
        up = mm(x, w_ref[:, ff : 2 * ff], NN)
        sig = jax.nn.sigmoid(u)
        silu = u * sig
        act = (silu * up).astype(BF16)
        f = mm(act, w_ref[:, 2 * ff : 3 * ff], NT)
        cbuf[at, :] = jnp.broadcast_to(jnp.sum(gs * f, axis=1, keepdims=True), (ROWS, 128))
        gbuf[at, :] = (f * gate).astype(BF16)
        df = (gs * gate).astype(BF16)
        dact = mm(df, w_ref[:, 2 * ff : 3 * ff], NN)
        dup = (dact * silu).astype(BF16)
        du = (dact * up * sig * (1.0 + u * (1.0 - sig))).astype(BF16)
        xbuf[at, :] = (mm(du, w_ref[:, 0:ff], NT) + mm(dup, w_ref[:, ff : 2 * ff], NT)).astype(BF16)
        gacc[:, 0:ff] += mm(x, du, TN)
        gacc[:, ff : 2 * ff] += mm(x, dup, TN)
        gacc[:, 2 * ff : 3 * ff] += mm(df, act, TN)
        return 0

    lax.fori_loop(0, nt_ref[e], tile_step, 0)
    gw_ref[...] = gacc[...].astype(BF16)

    @pl.when(e == EXPERTS - 1)
    def _scatter():
        for j in range(chunks):
            def take(ex, _, j=j):
                at = pl.ds(pl.multiple_of(off_ref[j * EXPERTS + ex], 16), TILE)
                to = pl.ds(pl.multiple_of(ex * TILE, 16), TILE)
                hit = match(j, ex, 0)
                onehot[to, :] = pick(hit)
                fbuf[to, :] = gbuf[at, :]
                dbuf[to, :] = xbuf[at, :]
                col = jnp.concatenate([cbuf[at, :]] * (rows // 128), axis=1)
                dgrow[pl.ds(ex, 1), :] = jnp.sum(jnp.where(hit, col, 0.0), axis=0, keepdims=True)
                return 0

            lax.fori_loop(0, EXPERTS, take, 0)
            gacc[0:rows, 0:D] = mm(onehot[...], fbuf[...], TN)
            gacc[0:rows, D : 2 * D] = mm(onehot[...], dbuf[...], TN)

            def rare(ex, _, j=j):
                def more(tile, _):
                    at = pl.ds(pl.multiple_of(off_ref[j * EXPERTS + ex] + tile * TILE, 16), TILE)
                    hit = match(j, ex, tile)
                    sel = pick(hit)
                    gacc[0:rows, 0:D] += mm(sel, gbuf[at, :], TN)
                    gacc[0:rows, D : 2 * D] += mm(sel, xbuf[at, :], TN)
                    col = jnp.concatenate([cbuf[at, :]] * (rows // 128), axis=1)
                    dgrow[pl.ds(ex, 1), :] += jnp.sum(jnp.where(hit, col, 0.0), axis=0, keepdims=True)
                    return 0

                return lax.fori_loop(1, (cnt_ref[j * EXPERTS + ex] + (TILE - 1)) // TILE, more, 0)

            lax.fori_loop(0, EXPERTS, rare, 0)
            o_refs[j] = gacc[0:rows, 0:D].astype(BF16)
            d_refs[j, 0:rows, :] = gacc[0:rows, D : 2 * D].astype(BF16)
            total = dgrow[...]
            high = total.astype(BF16).astype(F32)
            both = jnp.concatenate([high, total - high], axis=0)
            d_refs[j, rows : rows + SPARE, :] = jnp.concatenate(
                [both, jnp.zeros((SPARE, D - rows), F32)], axis=1
            ).astype(BF16)


def experts_call(counts, hs, gs, slots, weights, ff):
    chunks, rows = gs.shape[:2]
    width = 3 * ff
    most = (rows + 15 * chunks + ROWS - 1) // ROWS * ROWS * EXPERTS + ROWS
    whole = lambda shape: pl.BlockSpec(shape, lambda e: (0,) * len(shape), pipeline_mode=pl.Buffered(1))
    return pl.pallas_call(
        functools.partial(experts_body, ff, chunks),
        name="experts",
        grid=(EXPERTS,),
        in_specs=[smem(), whole(hs.shape), whole(gs.shape), whole(slots.shape), pl.BlockSpec((D, width), lambda e: (0, e))],
        out_specs=[whole(gs.shape), whole(hs.shape), pl.BlockSpec((D, width), lambda e: (0, e))],
        out_shape=[
            jax.ShapeDtypeStruct(gs.shape, BF16),
            jax.ShapeDtypeStruct(hs.shape, BF16),
            jax.ShapeDtypeStruct((D, EXPERTS * width), BF16),
        ],
        scratch_shapes=[
            pltpu.VMEM((most, D), BF16),
            pltpu.VMEM((most, D), BF16),
            pltpu.VMEM((most, 128), F32),
            pltpu.VMEM((EXPERTS * TILE, rows), BF16),
            pltpu.VMEM((EXPERTS * TILE, D), BF16),
            pltpu.VMEM((EXPERTS * TILE, D), BF16),
            pltpu.VMEM((D, width), F32),
            pltpu.VMEM((SPARE, rows), F32),
            pltpu.VMEM((EXPERTS, rows), F32),
            pltpu.SMEM((chunks * EXPERTS,), I32),
            pltpu.SMEM((EXPERTS,), I32),
            pltpu.SMEM((EXPERTS,), I32),
        ],
        compiler_params=pltpu.CompilerParams(
            dimension_semantics=("arbitrary",), vmem_limit_bytes=VMEM_CAP
        ),
    )(counts, hs, gs, slots, weights)


def rope_tables(lengths, first, count):
    finish = jnp.sum(jnp.where(jnp.arange(lengths.shape[0])[:, None] <= jnp.arange(lengths.shape[0])[None, :], lengths[:, None], 0), axis=0)
    begins = finish - lengths
    rows = first + jnp.arange(count, dtype=I32)
    opening = jnp.max(jnp.where(begins[None, :] <= rows[:, None], begins[None, :], 0), axis=1)
    place = rows - opening
    half = HEAD_DIM // 2
    rates = jnp.exp(jnp.arange(half, dtype=F32) * (-2.0 * math.log(10000.0) / HEAD_DIM))
    angles = place.astype(F32)[:, None] * rates[None, :]
    cos, sin = jnp.cos(angles), jnp.sin(angles)
    return place, jnp.concatenate([cos] * 4, axis=1), jnp.concatenate([-sin, sin] * 2, axis=1)


def body(tokens, cotangent, deal, lengths, routes, gate_residual, w_qkv, w_out, w_gate_up, w_down,
         norm_gain_attn, norm_gain_moe, w_router, w_const, v_const):
    rows = tokens.shape[0]
    n_dp, n_t = lax.axis_size("dp"), lax.axis_size("tensor")
    t = lax.axis_index("tensor")
    ff = w_down.shape[2]
    d_here = w_qkv.shape[0]

    def swap(v, j):
        return lax.ppermute(v, "tensor", [(i, i ^ j) for i in range(n_t)])

    def place_in(parts):
        stacked = jnp.stack(parts)
        return jnp.stack([lax.dynamic_index_in_dim(stacked, t ^ i, 0, keepdims=False) for i in range(n_t)], axis=2)

    attn_shard = jnp.concatenate([w_qkv, w_out[:, None, :]], axis=1)
    attn_shard = place_in([attn_shard] + [swap(attn_shard, j) for j in range(1, n_t)]).reshape(d_here, 4 * D)
    w_attn = lax.all_gather(attn_shard, "dp", axis=0, tiled=True)
    ff_shard = jnp.concatenate([w_gate_up.reshape(d_here, EXPERTS, 2 * ff), w_down], axis=2)
    w_ff = lax.all_gather(ff_shard.reshape(d_here, EXPERTS * 3 * ff), "dp", axis=0, tiled=True)

    routes_t = routes.reshape(n_t, rows, 2).transpose(0, 2, 1)
    row, ext = (rows, D), (3 * rows, D)
    every, every_packed = (n_t, rows, D), (n_t, rows + SPARE, D)
    xs, gs, pos, slots, counts = call(
        functools.partial(deal_body, n_dp),
        "deal",
        [(row, BF16), (row, BF16), ((1, rows), I32), ((n_t, EXPERTS, rows), I32), ((n_t, EXPERTS, 128), I32)],
        [deal.reshape(1, rows), tokens, cotangent, routes_t],
    )
    counts = counts[:, :, 0].reshape(n_t * EXPERTS)
    x0 = lax.all_to_all(xs, "dp", split_axis=0, concat_axis=0, tiled=True)
    g0 = lax.all_to_all(gs, "dp", split_axis=0, concat_axis=0, tiled=True)

    place, cos, sin = rope_tables(lengths[0], (t - 2) * rows, 3 * rows)
    start = (LONGEST + jnp.arange(rows, dtype=I32) - place[2 * rows :]).reshape(1, rows)
    gain_attn, gain_moe = norm_gain_attn.reshape(1, D), norm_gain_moe.reshape(1, D)
    window = LONGEST + 256
    res_t = jnp.concatenate([gate_residual.T, jnp.zeros((4, rows), F32)], axis=0)
    wrc = jnp.concatenate([w_router.T, w_const.transpose(0, 2, 1).reshape(4, D)], axis=0)
    v8 = jnp.concatenate([v_const, jnp.zeros((6, D), F32)], axis=0)
    dma = lambda *shape: pltpu.SemaphoreType.DMA(shape)
    x1, x2, h, q, k, v, o, lse, xm, hp_all, g_all, gt, xl, dhl, sm, gv = call(
        functools.partial(forward_body, n_t),
        "forward",
        [(row, BF16), (row, BF16), (ext, BF16), (row, BF16), (ext, BF16), (ext, BF16), (row, BF16), ((SPARE, rows), F32),
         (row, F32), (every_packed, BF16), (every, BF16), ((8, rows), F32), (row, F32), (row, F32), ((SPARE, rows), F32), ((8, D), F32)],
        [x0, g0, w_attn, gain_attn, gain_moe, cos, sin, start, res_t, wrc, routes_t, v8],
        scratch=[pltpu.VMEM((window, 256), F32), dma(2), dma(2)] + [dma(3)] * 8,
        meet=0,
    )

    out_all, back_all, gw_ff = experts_call(counts, hp_all, g_all, slots, w_ff, ff)
    ff_sum = lax.psum_scatter(gw_ff, "dp", scatter_dimension=0, tiled=True)
    h2 = lax.dynamic_index_in_dim(hp_all, t, 0, keepdims=False)[0:rows]

    dx, da, dres, small, dq, dk, dv, result = call(
        functools.partial(backward_body, n_t),
        "backward",
        [(row, F32), (row, BF16), ((SPARE, rows), F32), ((SPARE + 8, D), F32), (row, BF16), (ext, BF16), (ext, BF16), (row, BF16)],
        [back_all, out_all, dhl, gt, sm, routes_t, wrc, xm, gain_moe, g0, h2, w_attn, o, gv, q, k, v, lse, start, cos, sin, xl],
        scratch=[pltpu.VMEM((rows // 256, window, 256), F32), pltpu.VMEM((3 * rows, 128), F32), pltpu.VMEM((3 * rows, 128), F32),
                 pltpu.VMEM((rows + SPARE, D), F32), pltpu.VMEM(row, BF16), pltpu.VMEM((SPARE, rows), F32)]
        + [pltpu.VMEM((n_t - 1, rows + SPARE, D), BF16)] * 2 + [pltpu.VMEM((n_t - 1, rows, D), BF16)] * 2
        + [dma(n_t - 1, 2)] * 4 + [dma(n_t - 1, 1)] * 4,
        meet=1,
    )
    back_out = lax.all_to_all(result, "dp", split_axis=0, concat_axis=0, tiled=True)
    gw_attn, gain_part, d_start = call(
        functools.partial(grads_body, n_t),
        "grads",
        [((D, 4 * D), BF16), ((8, D), F32), (row, BF16)],
        [x0, x1, x2, h, dq, dk, dv, da, o, w_attn, dx, gain_attn],
        scratch=[pltpu.VMEM(row, F32)] + [pltpu.VMEM(row, BF16)] * 4 + [dma(2), dma(2)],
        meet=2,
    )
    back_grad = lax.all_to_all(d_start, "dp", split_axis=0, concat_axis=0, tiled=True)
    output, grad_tokens = call(restore_body, "restore", [(row, BF16)] * 2, [pos, back_out, back_grad])

    def total(v):
        for axis, count in (("tensor", n_t), ("dp", n_dp)):
            bit = 1
            while bit < count:
                v = v + lax.ppermute(v, axis, [(i, i ^ bit) for i in range(count)])
                bit *= 2
        return v

    small_all = total(small)
    gain_all = total(gain_part[0:1])[0]
    attn_sum = lax.psum_scatter(gw_attn, "dp", scatter_dimension=0, tiled=True).reshape(d_here, 4, n_t, D // n_t)

    def share(j):
        return lax.dynamic_index_in_dim(attn_sum, t ^ j, 2, keepdims=False)

    attn_own = share(0).astype(F32)
    for j in range(1, n_t):
        attn_own = attn_own + swap(share(j), j).astype(F32)
    ff_own = ff_sum.reshape(d_here, EXPERTS, 3 * ff).astype(F32)
    return (
        output,
        grad_tokens,
        dres[0:12].T,
        attn_own[:, 0:3],
        attn_own[:, 3],
        ff_own[:, :, 0 : 2 * ff].reshape(d_here, EXPERTS, 2, ff),
        ff_own[:, :, 2 * ff :],
        gain_all,
        small_all[SPARE + 2],
        small_all[0:12].T,
        small_all[12:16].reshape(2, 2, D).transpose(0, 2, 1),
        small_all[SPARE : SPARE + 2],
    )


def solution(mesh):
    both, every = P(("dp", "tensor"), None), P()
    weights = (P("dp", None, "tensor"), P("dp", "tensor"), P("dp", None, None, "tensor"), P("dp", None, "tensor"))
    return jax.shard_map(
        body,
        mesh=mesh,
        in_specs=(both, both, P(("dp", "tensor")), P("dp", None), P("dp", None), both, *weights) + (every,) * 5,
        out_specs=(both, both, both, *weights) + (every,) * 5,
        check_vma=False,
    )
```

time: 770 us -> 714 us (0.927)
  Pallas kernels: 184 us -> 410 us
  waiting for transfers between devices: 338 us -> 191 us
  blocking collectives: 86.6 us -> 0 us
  starting transfers between devices: 94.6 us -> 49.6 us
    pallas_call x9 -> x5, Pallas kernels: 115 us -> 331 us  [call(): pl.pallas_call(body, name=name, out_shape=[jax.ShapeDtypeStruct(*o) for o...]
    ppermute x15 -> x6, waiting for transfers between devices: 231 us -> 24.9 us  [swap(): return lax.ppermute(v, 'tensor', [(i, i ^ j) for i in range(n_t)])]
    all_gather x2 -> x0, blocking collectives: 86.6 us -> none  [the longest x1 65.1 us: body(): lax.all_gather(gain_part[0:1], ('dp', 'tensor'), axis=0, tiled=True)]
    reduce_scatter x1, waiting for transfers between devices: 24.5 us -> 102 us  [body(): ff_sum = lax.psum_scatter(gw_ff, 'dp', scatter_dimension=0, tiled=True)]
    ppermute x15 -> x6, starting transfers between devices: 67.9 us -> 10.3 us  [swap(): return lax.ppermute(v, 'tensor', [(i, i ^ j) for i in range(n_t)])]
    ppermute x4 -> x10, waiting for transfers between devices: 57.6 us -> 21.6 us  [total(): v = v + lax.ppermute(v, axis, [(i, i ^ bit) for i in range(count)])]
    reduce_scatter x1, waiting for transfers between devices: 0.02 us -> 14.3 us  [body(): lax.psum_scatter(gw_attn, 'dp', scatter_dimension=0, tiled=True)]
    pallas_call x1, Pallas kernels: 69.2 us -> 78.9 us  [experts_call(): pl.pallas_call(functools.partial(experts_body, ff, chunks), name='experts...]
  transfers between devices with their start and end apart: 28 -> 24, of which waited for: 11 -> 14; matrix products, arithmetic and copies ran while one was open for 4% -> 4% of each run, Pallas kernels for 14% -> 20%
where the time goes in v2:
time: 714 us; the launch traced here: 708 us
  Pallas kernels  410 us (57%)
  waiting for transfers between devices  191 us (27%)
  starting transfers between devices  49.6 us (7%)
  local copies, waits for them, and re-layouts  31.3 us (4%)
  between operations  14.3 us (2%)
  other arithmetic  12.2 us (2%)
    pallas_call x5, Pallas kernels, call(): pl.pallas_call(body, name=name, out_shape=[jax.ShapeDtypeStruct(*o) for o...  331 us
    reduce_scatter x1, waiting for transfers between devices, body(): ff_sum = lax.psum_scatter(gw_ff, 'dp', scatter_dimension=0, tiled=True)  102 us
    pallas_call x1, Pallas kernels, experts_call(): pl.pallas_call(functools.partial(experts_body, ff, chunks), name='experts...  78.9 us
    ppermute x6, waiting for transfers between devices, swap(): return lax.ppermute(v, 'tensor', [(i, i ^ j) for i in range(n_t)])  24.9 us
    ppermute x10, waiting for transfers between devices, total(): v = v + lax.ppermute(v, axis, [(i, i ^ bit) for i in range(count)])  21.6 us
    all_to_all x1, waiting for transfers between devices, body(): g0 = lax.all_to_all(gs, 'dp', split_axis=0, concat_axis=0, tiled=True)  15.8 us
    ppermute x10, starting transfers between devices, total(): v = v + lax.ppermute(v, axis, [(i, i ^ bit) for i in range(count)])  15.2 us
    reduce_scatter x1, waiting for transfers between devices, body(): lax.psum_scatter(gw_attn, 'dp', scatter_dimension=0, tiled=True)  14.3 us
  transfers between devices with their start and end apart: 24, of which 14 were waited for; matrix products, arithmetic and copies ran while one was open for 4% of the time, Pallas kernels for 20%

profile of v2, /device:TPU:0, one launch (start us, length us, event | category | flops | bytes accessed | tf_op | source)
XLA Modules:
  0.0 708.4 jit_solution(3371923167728014372)
XLA Ops:
  8.2 5.1 collective-permute-start.2
  14.0 5.3 collective-permute-done.2
  19.2 10.8 %collective-permute-done.1 = bf16[96,4,192]{2,0,1:T(8,128)(2,1)S(1)} collective-permute-done((bf16[96,4,192]{2,0,1:T(8,128)(2,1)S(1)}, bf16[96,4,192]{2,0,1:T(8,128)(2,1)S(1)}, u32[]{:S(2)}, u32[]{:S(2)}) %collective-permute-start.1) | collective-permute-done | bytes 147488 | tf_op jit(solution)/shard_map/ppermute | solution.py:820
  37.7 3.5 deal.1
  41.2 3.7 all-to-all-start
  50.3 8.8 %all-to-all-done = bf16[8,64,768]{2,1,0:T(8,128)(2,1)S(1)} async-done(((bf16[8,64,768]{2,1,0:T(8,128)(2,1)}), bf16[8,64,768]{2,1,0:T(8,128)(2,1)S(1)}, u32[]{:S(2)}, u32[]{:S(2)}) %all-to-all-start) | async-done | bytes 786464 | tf_op jit(solution)/shard_map/all_to_all | solution.py:842
  59.1 3.5 all-to-all-start.1
  68.0 15.8 %all-to-all-done.1 = bf16[8,64,768]{2,1,0:T(8,128)(2,1)S(1)} async-done(((bf16[8,64,768]{2,1,0:T(8,128)(2,1)}), bf16[8,64,768]{2,1,0:T(8,128)(2,1)S(1)}, u32[]{:S(2)}, u32[]{:S(2)}) %all-to-all-start.1) | async-done | bytes 786464 | tf_op jit(solution)/shard_map/all_to_all | solution.py:843
  87.9 132.7 %forward.1 = (bf16[512,768]{1,0:T(8,128)(2,1)}, bf16[512,768]{1,0:T(8,128)(2,1)}, bf16[1536,768]{1,0:T(8,128)(2,1)}, bf16[512,768]{1,0:T(8,128)(2,1)}, bf16[1536...) custom-call(bf16[512,768]{1,0:T(8,128)(2,1)} %bitcast.69, ...), custom_call_target="tpu_custom_call" | custom-call | tf_op jit(solution)/shard_map/forward/pallas_call | solution.py:63
  222.8 78.9 %experts.1 = (bf16[4,512,768]{2,1,0:T(8,128)(2,1)}, bf16[4,528,768]{2,1,0:T(8,128)(2,1)}, bf16[768,12288]{1,0:T(8,128)(2,1)}) custom-call(s32[32]{0:T(128)} %reshape_squeeze.3.cnt_ref, bf16[4,528,768]{2,1,0:T(8,128)(2,1)} %get-tuple-element.53.h_refs, bf16[4,512,768]{2,1,0:T(8,128)(2,1)} %get-tuple-element.54.g_refs, ...), custom_call_target="tpu_custom_call" | custom-call | tf_op jit(solution)/shard_map/experts/pallas_call | solution.py:767
  301.6 145.9 %backward.1 = (f32[512,768]{1,0:T(8,128)}, bf16[512,768]{1,0:T(8,128)(2,1)}, f32[16,512]{1,0:T(8,128)}, f32[24,768]{1,0:T(8,128)}, bf16[512,768]{1,0:T(8,128)(2,...) custom-call(bf16[4,528,768]{2,1,0:T(8,128)(2,1)} %get-tuple-element.56.back_ref, ...), custom_call_target="tpu_custom_call" | custom-call | tf_op jit(solution)/shard_map/backward/pallas_call | solution.py:63
  447.6 45.0 %grads.1 = (bf16[768,3072]{1,0:T(8,128)(2,1)}, f32[8,768]{1,0:T(8,128)}, bf16[512,768]{1,0:T(8,128)(2,1)}) custom-call(bf16[512,768]{1,0:T(8,128)(2,1)} %bitcast.70, bf16[512,768]{1,0:T(8,128)(2,1)} %get-tuple-element.70.x1_ref, bf16[512,768]{1,0:T(8,128)(2,1)} %get-tuple-element.71.x2_ref, bf16[1536,768]{1,0:T(8,128)(2,1)} %get-tuple-element.72.h_ref, ...), custom_call_target="tpu_custom_call" | custom-call | tf_op jit(solution)/shard_map/grads/pallas_call | solution.py:63
  493.2 12.4 %all-to-all-start.2 = ((bf16[8,64,768]{2,1,0:T(8,128)(2,1)}), bf16[8,64,768]{2,1,0:T(8,128)(2,1)S(1)}, u32[]{:S(2)}, u32[]{:S(2)}) async-start(bf16[8,64,768]{2,1,0:T(8,128)(2,1)} %bitcast.25), calls=%async_computation.2 | async-start | bytes 1572864 | tf_op jit(solution)/shard_map/all_to_all | solution.py:878
  505.7 4.7 collective-permute-start.11
  516.6 3.3 collective-permute-done.12
  521.7 3.5 collective-permute-done.7
  533.3 4.2 all-to-all-start.3
  540.8 8.7 %collective-permute-done.15 = f32[24,768]{1,0:T(8,128)S(1)} collective-permute-done((f32[24,768]{1,0:T(8,128)S(1)}, f32[24,768]{1,0:T(8,128)S(1)}, u32[]{:S(2)}, u32[]{:S(2)}) %collective-permute-start.15) | collective-permute-done | bytes 73760 | tf_op jit(solution)/shard_map/ppermute | solution.py:894
  549.5 14.3 %reduce-scatter.3.cloned.1.call-done = bf16[96,3072]{1,0:T(8,128)(2,1)} async-done(((bf16[768,3072]{1,0:T(8,128)(2,1)}), bf16[96,3072]{1,0:T(8,128)(2,1)}) %reduce-scatter.3.cloned.1.call-update) | async-done | bytes 589840 | tf_op jit(solution)/shard_map/reduce_scatter | solution.py:900
  568.7 3.4 collective-permute-start.5
  576.5 3.6 restore.1
  580.1 8.8 %collective-permute-done.4 = bf16[96,4,192]{2,0,1:T(8,128)(2,1)} collective-permute-done((bf16[96,4,192]{2,0,1:T(8,128)(2,1)S(1)}, bf16[96,4,192]{2,0,1:T(8,128)(2,1)}, u32[]{:S(2)}, u32[]{:S(2)}) %collective-permute-start.4) | collective-permute-done | bytes 147488 | tf_op jit(solution)/shard_map/ppermute | solution.py:820
  591.8 102.1 %reduce-scatter.5.cloned.1.call-done = bf16[96,12288]{1,0:T(8,128)(2,1)} async-done(((bf16[768,12288]{1,0:T(8,128)(2,1)}), bf16[96,12288]{1,0:T(8,128)(2,1)}) %reduce-scatter.5.cloned.1.call-update) | async-done | bytes 2359312 | tf_op jit(solution)/shard_map/reduce_scatter | solution.py:864
  697.9 3.7 reshape.105
  (118 shorter events, 62.1 us)
Async XLA Ops:
  7.2 80.8 %all-gather.3.cloned.1.call-start = ((), (), s32[]{:S(2)}) async-start(), calls=%async_computation.6 | async-start | bytes 5308416 | tf_op jit(solution)/shard_map/all_gather | solution.py:828
  8.2 11.0 %collective-permute-start.2 = (bf16[96,4,192]{2,0,1:T(8,128)(2,1)S(1)}, bf16[96,4,192]{2,0,1:T(8,128)(2,1)S(1)}, u32[]{:S(2)}, u32[]{:S(2)}) collective-permute-start(bf16[96,4,192]{2,0,1:T(8,128)(2,1)S(1)} %get-tuple-element.97), channel_id=1, source_target_pairs={{0,3},{1,2},{2,1},{3,0},{4,7},{5,6},{6,5},{7,4},{8,11},{9,10},{10,... | collective-permute-start | bytes 442376 | tf_op jit(solution)/shard_map/ppermute | solution.py:820
  13.3 16.7 %collective-permute-start.1 = (bf16[96,4,192]{2,0,1:T(8,128)(2,1)S(1)}, bf16[96,4,192]{2,0,1:T(8,128)(2,1)S(1)}, u32[]{:S(2)}, u32[]{:S(2)}) collective-permute-start(bf16[96,4,192]{2,0,1:T(8,128)(2,1)S(1)} %get-tuple-element.97), channel_id=1, source_target_pairs={{0,2},{1,3},{2,0},{3,1},{4,6},{5,7},{6,4},{7,5},{8,10},{9,11},{10,... | collective-permute-start | bytes 442376 | tf_op jit(solution)/shard_map/ppermute | solution.py:820
  13.4 16.7 %collective-permute-start = (bf16[96,4,192]{2,0,1:T(8,128)(2,1)S(1)}, bf16[96,4,192]{2,0,1:T(8,128)(2,1)S(1)}, u32[]{:S(2)}, u32[]{:S(2)}) collective-permute-start(bf16[96,4,192]{2,0,1:T(8,128)(2,1)S(1)} %get-tuple-element.97), channel_id=1, source_target_pairs={{0,1},{1,0},{2,3},{3,2},{4,5},{5,4},{6,7},{7,6},{8,9},{9,8},{10,11... | collective-permute-start | bytes 442376 | tf_op jit(solution)/shard_map/ppermute | solution.py:820
  32.9 189.8 %all-gather.5.cloned.1.call-start = ((), (), s32[]{:S(2)}) async-start(), calls=%async_computation.7 | async-start | bytes 21233664 | tf_op jit(solution)/shard_map/all_gather | solution.py:830
  41.2 17.9 %all-to-all-start = ((bf16[8,64,768]{2,1,0:T(8,128)(2,1)}), bf16[8,64,768]{2,1,0:T(8,128)(2,1)S(1)}, u32[]{:S(2)}, u32[]{:S(2)}) async-start(bf16[8,64,768]{2,1,0:T(8,128)(2,1)} %bitcast.76), calls=%async_computation | async-start | bytes 1572864 | tf_op jit(solution)/shard_map/all_to_all | solution.py:842
  59.1 24.7 %all-to-all-start.1 = ((bf16[8,64,768]{2,1,0:T(8,128)(2,1)}), bf16[8,64,768]{2,1,0:T(8,128)(2,1)S(1)}, u32[]{:S(2)}, u32[]{:S(2)}) async-start(bf16[8,64,768]{2,1,0:T(8,128)(2,1)} %bitcast.75), calls=%async_computation.1 | async-start | bytes 1572864 | tf_op jit(solution)/shard_map/all_to_all | solution.py:843
  62.7 501.2 %reduce-scatter.3.cloned.1.call-start = ((), (), s32[]{:S(2)}) async-start(), calls=%async_computation.8 | async-start | bytes 5308416 | tf_op jit(solution)/shard_map/reduce_scatter | solution.py:900
  492.6 201.2 %reduce-scatter.5.cloned.1.call-start = ((), (), s32[]{:S(2)}) async-start(), calls=%async_computation.9 | async-start | bytes 21233664 | tf_op jit(solution)/shard_map/reduce_scatter | solution.py:864
  493.2 40.1 %all-to-all-start.2 = ((bf16[8,64,768]{2,1,0:T(8,128)(2,1)}), bf16[8,64,768]{2,1,0:T(8,128)(2,1)S(1)}, u32[]{:S(2)}, u32[]{:S(2)}) async-start(bf16[8,64,768]{2,1,0:T(8,128)(2,1)} %bitcast.25), calls=%async_computation.2 | async-start | bytes 1572864 | tf_op jit(solution)/shard_map/all_to_all | solution.py:878
  505.7 7.6 %collective-permute-start.11 = (f32[24,768]{1,0:T(8,128)S(1)}, f32[24,768]{1,0:T(8,128)S(1)}, u32[]{:S(2)}, u32[]{:S(2)}) collective-permute-start(f32[24,768]{1,0:T(8,128)S(1)} %copy-done.5), channel_id=1, source_target_pairs={{0,1},{1,0},{2,3},{3,2},{4,5},{5,4},{6,7},{7,6},{8,9},{9,8},{10,11... | collective-permute-start | bytes 221192 | tf_op jit(solution)/shard_map/ppermute | solution.py:894
  513.2 6.7 collective-permute-start.12
  516.3 3.7 collective-permute-start.6
  519.9 11.7 %collective-permute-start.13 = (f32[24,768]{1,0:T(8,128)S(1)}, f32[24,768]{1,0:T(8,128)S(1)}, u32[]{:S(2)}, u32[]{:S(2)}) collective-permute-start(f32[24,768]{1,0:T(8,128)S(1)} %add.104), channel_id=1, source_target_pairs={{0,4},{4,0},{8,12},{12,8},{16,20},{20,16},{24,28},{28,24},{1,5},{5... | collective-permute-start | bytes 221192 | tf_op jit(solution)/shard_map/ppermute | solution.py:894
  520.7 4.5 collective-permute-start.7
  525.2 1.2 collective-permute-start.8
  526.4 3.6 collective-permute-start.9
  530.0 10.2 %collective-permute-start.10 = (f32[1,768]{1,0:T(1,128)S(1)}, f32[1,768]{1,0:T(1,128)S(1)}, u32[]{:S(2)}, u32[]{:S(2)}) collective-permute-start(f32[1,768]{1,0:T(1,128)S(1)} %add.101), channel_id=1, source_target_pairs={{0,16},{4,20},{8,24},{12,28},{16,0},{20,4},{24,8},{28,12},{1,17},{... | collective-permute-start | bytes 9224 | tf_op jit(solution)/shard_map/ppermute | solution.py:894
  531.6 6.6 collective-permute-start.14
  533.3 43.1 %all-to-all-start.3 = ((bf16[8,64,768]{2,1,0:T(8,128)(2,1)}), bf16[8,64,768]{2,1,0:T(8,128)(2,1)}, u32[]{:S(2)}, u32[]{:S(2)}) async-start(bf16[8,64,768]{2,1,0:T(8,128)(2,1)} %bitcast.27), calls=%async_computation.3 | async-start | bytes 1572864 | tf_op jit(solution)/shard_map/all_to_all | solution.py:887
  538.2 11.3 %collective-permute-start.15 = (f32[24,768]{1,0:T(8,128)S(1)}, f32[24,768]{1,0:T(8,128)S(1)}, u32[]{:S(2)}, u32[]{:S(2)}) collective-permute-start(f32[24,768]{1,0:T(8,128)S(1)} %add.106), channel_id=1, source_target_pairs={{0,16},{4,20},{8,24},{12,28},{16,0},{20,4},{24,8},{28,12},{1,17},{... | collective-permute-start | bytes 221192 | tf_op jit(solution)/shard_map/ppermute | solution.py:894
  568.7 11.4 %collective-permute-start.5 = (bf16[96,4,192]{2,0,1:T(8,128)(2,1)S(1)}, bf16[96,4,192]{2,0,1:T(8,128)(2,1)}, u32[]{:S(2)}, u32[]{:S(2)}) collective-permute-start(bf16[96,4,192]{2,0,1:T(8,128)(2,1)S(1)} %bitcast.80), channel_id=1, source_target_pairs={{0,3},{1,2},{2,1},{3,0},{4,7},{5,6},{6,5},{7,4},{8,11},{9,10},{10,... | collective-permute-start | bytes 442376 | tf_op jit(solution)/shard_map/ppermute | solution.py:820
  572.2 16.7 %collective-permute-start.4 = (bf16[96,4,192]{2,0,1:T(8,128)(2,1)S(1)}, bf16[96,4,192]{2,0,1:T(8,128)(2,1)}, u32[]{:S(2)}, u32[]{:S(2)}) collective-permute-start(bf16[96,4,192]{2,0,1:T(8,128)(2,1)S(1)} %bitcast.81), channel_id=1, source_target_pairs={{0,2},{1,3},{2,0},{3,1},{4,6},{5,7},{6,4},{7,5},{8,10},{9,11},{10,... | collective-permute-start | bytes 442376 | tf_op jit(solution)/shard_map/ppermute | solution.py:820
  573.0 15.9 %collective-permute-start.3 = (bf16[96,4,192]{2,0,1:T(8,128)(2,1)}, bf16[96,4,192]{2,0,1:T(8,128)(2,1)}, u32[]{:S(2)}, u32[]{:S(2)}) collective-permute-start(bf16[96,4,192]{2,0,1:T(8,128)(2,1)} %bitcast.64), channel_id=1, source_target_pairs={{0,1},{1,0},{2,3},{3,2},{4,5},{5,4},{6,7},{7,6},{8,9},{9,8},{10,11... | collective-permute-start | bytes 442376 | tf_op jit(solution)/shard_map/ppermute | solution.py:820
  (14 other events, 193.9 us)
Sparse Core Ops, SparseCore 0:
  33.1 54.8 all-gather.2
  90.4 98.5 all-gather.4
  492.8 71.0 reduce-scatter.2
  567.3 126.4 reduce-scatter.4

commit v3 on v2

--- a/solution.py
+++ b/solution.py
@@ -157,7 +157,7 @@
         if dest <= k and dest < size - 1:
             events.append((0 if k == size - 1 else dest + size - 1 - k, -1, dest))
     drop = [(t, w, d) for t, w, d in events if (k == 0 and w == 1 and d == 0) or (k == size - 1 and w == -1 and d == k)]
-    return sorted(ev for ev in events if ev not in drop)
+    return sorted((ev for ev in events if ev not in drop), key=lambda ev: (ev[0], ev[1], -ev[1] * ev[2]))
 
 
 def turn(u):
@@ -895,8 +895,9 @@
                 bit *= 2
         return v
 
-    small_all = total(small)
-    gain_all = total(gain_part[0:1])[0]
+    small_all = total(jnp.concatenate([small, gain_part], axis=0))
+    gain_all = small_all[SPARE + 8]
+    gw_attn, ff_sum = lax.optimization_barrier((gw_attn, ff_sum))
     attn_sum = lax.psum_scatter(gw_attn, "dp", scatter_dimension=0, tiled=True).reshape(d_here, 4, n_t, D // n_t)
 
     def share(j):

time: 714 us -> 585 us (0.82)
  waiting for transfers between devices: 191 us -> 93.5 us
  Pallas kernels: 410 us -> 390 us
  starting transfers between devices: 49.6 us -> 40.5 us
    reduce_scatter x1, waiting for transfers between devices: 102 us -> 0.02 us  [body(): ff_sum = lax.psum_scatter(gw_ff, 'dp', scatter_dimension=0, tiled=True)]
    reduce_scatter x1, waiting for transfers between devices: 14.3 us -> 32.6 us  [body(): lax.psum_scatter(gw_attn, 'dp', scatter_dimension=0, tiled=True)]
    pallas_call x5, Pallas kernels: 331 us -> 316 us  [call(): pl.pallas_call(body, name=name, out_shape=[jax.ShapeDtypeStruct(*o) for o...]
    ppermute x10 -> x5, starting transfers between devices: 15.2 us -> 6.7 us  [total(): v = v + lax.ppermute(v, axis, [(i, i ^ bit) for i in range(count)])]
    ppermute x6, waiting for transfers between devices: 24.9 us -> 17 us  [swap(): return lax.ppermute(v, 'tensor', [(i, i ^ j) for i in range(n_t)])]
    ppermute x10 -> x5, waiting for transfers between devices: 21.6 us -> 15.9 us  [total(): v = v + lax.ppermute(v, axis, [(i, i ^ bit) for i in range(count)])]
  transfers between devices with their start and end apart: 24 -> 19, of which waited for: 14 -> 12; matrix products, arithmetic and copies ran while one was open for 4% -> 6% of each run, Pallas kernels for 20% -> 54%
where the time goes in v3:
time: 585 us; the launch traced here: 580 us
  Pallas kernels  390 us (67%)
  waiting for transfers between devices  93.5 us (16%)
  starting transfers between devices  40.5 us (7%)
  local copies, waits for them, and re-layouts  31.2 us (5%)
  between operations  14.6 us (2%)
  other arithmetic  10.6 us (2%)
    pallas_call x5, Pallas kernels, call(): pl.pallas_call(body, name=name, out_shape=[jax.ShapeDtypeStruct(*o) for o...  316 us
    pallas_call x1, Pallas kernels, experts_call(): pl.pallas_call(functools.partial(experts_body, ff, chunks), name='experts...  73.9 us
    reduce_scatter x1, waiting for transfers between devices, body(): lax.psum_scatter(gw_attn, 'dp', scatter_dimension=0, tiled=True)  32.6 us
    ppermute x6, waiting for transfers between devices, swap(): return lax.ppermute(v, 'tensor', [(i, i ^ j) for i in range(n_t)])  17 us
    ppermute x5, waiting for transfers between devices, total(): v = v + lax.ppermute(v, axis, [(i, i ^ bit) for i in range(count)])  15.9 us
    all_to_all x1, waiting for transfers between devices, body(): g0 = lax.all_to_all(gs, 'dp', split_axis=0, concat_axis=0, tiled=True)  15.8 us
    all_to_all x1, starting transfers between devices, body(): lax.all_to_all(result, 'dp', split_axis=0, concat_axis=0, tiled=True)  12 us
  transfers between devices with their start and end apart: 19, of which 12 were waited for; matrix products, arithmetic and copies ran while one was open for 6% of the time, Pallas kernels for 54%

profile of v3, /device:TPU:0, one launch (start us, length us, event | category | flops | bytes accessed | tf_op | source)
XLA Modules:
  0.0 580.1 jit_solution(4013136367849971823)
XLA Ops:
  8.2 5.1 collective-permute-start.2
  14.0 5.3 collective-permute-done.2
  19.2 10.8 %collective-permute-done.1 = bf16[96,4,192]{2,0,1:T(8,128)(2,1)S(1)} collective-permute-done((bf16[96,4,192]{2,0,1:T(8,128)(2,1)S(1)}, bf16[96,4,192]{2,0,1:T(8,128)(2,1)S(1)}, u32[]{:S(2)}, u32[]{:S(2)}) %collective-permute-start.1) | collective-permute-done | bytes 147488 | tf_op jit(solution)/shard_map/ppermute | solution.py:820
  37.7 3.5 deal.1
  41.2 3.7 all-to-all-start
  50.3 8.8 %all-to-all-done = bf16[8,64,768]{2,1,0:T(8,128)(2,1)S(1)} async-done(((bf16[8,64,768]{2,1,0:T(8,128)(2,1)}), bf16[8,64,768]{2,1,0:T(8,128)(2,1)S(1)}, u32[]{:S(2)}, u32[]{:S(2)}) %all-to-all-start) | async-done | bytes 786464 | tf_op jit(solution)/shard_map/all_to_all | solution.py:842
  59.1 3.5 all-to-all-start.1
  62.7 2.8 fusion.2
  68.0 15.8 %all-to-all-done.1 = bf16[8,64,768]{2,1,0:T(8,128)(2,1)S(1)} async-done(((bf16[8,64,768]{2,1,0:T(8,128)(2,1)}), bf16[8,64,768]{2,1,0:T(8,128)(2,1)S(1)}, u32[]{:S(2)}, u32[]{:S(2)}) %all-to-all-start.1) | async-done | bytes 786464 | tf_op jit(solution)/shard_map/all_to_all | solution.py:843
  84.7 3.3 all-gather.3.cloned.1.call-done.w_ref
  87.9 132.7 %forward.1 = (bf16[512,768]{1,0:T(8,128)(2,1)}, bf16[512,768]{1,0:T(8,128)(2,1)}, bf16[1536,768]{1,0:T(8,128)(2,1)}, bf16[512,768]{1,0:T(8,128)(2,1)}, bf16[1536...) custom-call(bf16[512,768]{1,0:T(8,128)(2,1)} %bitcast.69, ...), custom_call_target="tpu_custom_call" | custom-call | tf_op jit(solution)/shard_map/forward/pallas_call | solution.py:63
  220.7 73.9 %experts.1 = (bf16[4,512,768]{2,1,0:T(8,128)(2,1)}, bf16[4,528,768]{2,1,0:T(8,128)(2,1)}, bf16[768,12288]{1,0:T(8,128)(2,1)}) custom-call(s32[32]{0:T(128)} %reshape_squeeze.3.cnt_ref, bf16[4,528,768]{2,1,0:T(8,128)(2,1)} %get-tuple-element.55.h_refs, bf16[4,512,768]{2,1,0:T(8,128)(2,1)} %get-tuple-element.56.g_refs, ...), custom_call_target="tpu_custom_call" | custom-call | tf_op jit(solution)/shard_map/experts/pallas_call | solution.py:767
  296.8 133.6 %backward.1 = (f32[512,768]{1,0:T(8,128)}, bf16[512,768]{1,0:T(8,128)(2,1)}, f32[16,512]{1,0:T(8,128)}, f32[24,768]{1,0:T(8,128)}, bf16[512,768]{1,0:T(8,128)(2,...) custom-call(bf16[4,528,768]{2,1,0:T(8,128)(2,1)} %get-tuple-element.58.back_ref, ...), custom_call_target="tpu_custom_call" | custom-call | tf_op jit(solution)/shard_map/backward/pallas_call | solution.py:63
  430.4 42.7 %grads.1 = (bf16[768,3072]{1,0:T(8,128)(2,1)}, f32[8,768]{1,0:T(8,128)}, bf16[512,768]{1,0:T(8,128)(2,1)}) custom-call(bf16[512,768]{1,0:T(8,128)(2,1)} %bitcast.70, bf16[512,768]{1,0:T(8,128)(2,1)} %get-tuple-element.72.x1_ref, bf16[512,768]{1,0:T(8,128)(2,1)} %get-tuple-element.73.x2_ref, bf16[1536,768]{1,0:T(8,128)(2,1)} %get-tuple-element.74.h_ref, ...), custom_call_target="tpu_custom_call" | custom-call | tf_op jit(solution)/shard_map/grads/pallas_call | solution.py:63
  473.2 12.0 %all-to-all-start.2 = ((bf16[8,64,768]{2,1,0:T(8,128)(2,1)}), bf16[8,64,768]{2,1,0:T(8,128)(2,1)S(1)}, u32[]{:S(2)}, u32[]{:S(2)}) async-start(bf16[8,64,768]{2,1,0:T(8,128)(2,1)} %bitcast.25), calls=%async_computation.2 | async-start | bytes 1572864 | tf_op jit(solution)/shard_map/all_to_all | solution.py:878
  487.7 3.5 collective-permute-done.6
  491.7 7.1 %collective-permute-done.7 = f32[32,768]{1,0:T(8,128)S(1)} collective-permute-done((f32[32,768]{1,0:T(8,128)S(1)}, f32[32,768]{1,0:T(8,128)S(1)}, u32[]{:S(2)}, u32[]{:S(2)}) %collective-permute-start.7) | collective-permute-done | bytes 98336 | tf_op jit(solution)/shard_map/ppermute | solution.py:894
  501.6 3.6 collective-permute-done.9
  507.5 4.2 all-to-all-start.3
  512.8 32.6 %reduce-scatter.5.cloned.1.call-done = bf16[96,3072]{1,0:T(8,128)(2,1)} async-done(((bf16[768,3072]{1,0:T(8,128)(2,1)}), bf16[96,3072]{1,0:T(8,128)(2,1)}) %reduce-scatter.5.cloned.1.call-update) | async-done | bytes 589840 | tf_op jit(solution)/shard_map/reduce_scatter | solution.py:901
  550.2 3.3 collective-permute-start.5
  558.5 3.3 restore.1
  561.7 2.5 copy.49
  565.8 3.7 reshape.105
  (104 shorter events, 44.1 us)
Async XLA Ops:
  7.2 80.8 %all-gather.3.cloned.1.call-start = ((), (), s32[]{:S(2)}) async-start(), calls=%async_computation.6 | async-start | bytes 5308416 | tf_op jit(solution)/shard_map/all_gather | solution.py:828
  8.2 11.0 %collective-permute-start.2 = (bf16[96,4,192]{2,0,1:T(8,128)(2,1)S(1)}, bf16[96,4,192]{2,0,1:T(8,128)(2,1)S(1)}, u32[]{:S(2)}, u32[]{:S(2)}) collective-permute-start(bf16[96,4,192]{2,0,1:T(8,128)(2,1)S(1)} %get-tuple-element.103), channel_id=1, source_target_pairs={{0,3},{1,2},{2,1},{3,0},{4,7},{5,6},{6,5},{7,4},{8,11},{9,10},{10,... | collective-permute-start | bytes 442376 | tf_op jit(solution)/shard_map/ppermute | solution.py:820
  13.3 16.7 %collective-permute-start.1 = (bf16[96,4,192]{2,0,1:T(8,128)(2,1)S(1)}, bf16[96,4,192]{2,0,1:T(8,128)(2,1)S(1)}, u32[]{:S(2)}, u32[]{:S(2)}) collective-permute-start(bf16[96,4,192]{2,0,1:T(8,128)(2,1)S(1)} %get-tuple-element.103), channel_id=1, source_target_pairs={{0,2},{1,3},{2,0},{3,1},{4,6},{5,7},{6,4},{7,5},{8,10},{9,11},{10,... | collective-permute-start | bytes 442376 | tf_op jit(solution)/shard_map/ppermute | solution.py:820
  13.4 16.7 %collective-permute-start = (bf16[96,4,192]{2,0,1:T(8,128)(2,1)S(1)}, bf16[96,4,192]{2,0,1:T(8,128)(2,1)S(1)}, u32[]{:S(2)}, u32[]{:S(2)}) collective-permute-start(bf16[96,4,192]{2,0,1:T(8,128)(2,1)S(1)} %get-tuple-element.103), channel_id=1, source_target_pairs={{0,1},{1,0},{2,3},{3,2},{4,5},{5,4},{6,7},{7,6},{8,9},{9,8},{10,11... | collective-permute-start | bytes 442376 | tf_op jit(solution)/shard_map/ppermute | solution.py:820
  32.9 187.7 %all-gather.5.cloned.1.call-start = ((), (), s32[]{:S(2)}) async-start(), calls=%async_computation.7 | async-start | bytes 21233664 | tf_op jit(solution)/shard_map/all_gather | solution.py:830
  37.7 11.3 %copy-start.5 = (f32[768,12]{0,1:T(8,128)S(1)}, f32[768,12]{0,1:T(8,128)}, u32[]{:S(2)}) copy-start(f32[768,12]{0,1:T(8,128)} %param.27) | copy-start | bytes 110596
  41.2 17.9 %all-to-all-start = ((bf16[8,64,768]{2,1,0:T(8,128)(2,1)}), bf16[8,64,768]{2,1,0:T(8,128)(2,1)S(1)}, u32[]{:S(2)}, u32[]{:S(2)}) async-start(bf16[8,64,768]{2,1,0:T(8,128)(2,1)} %bitcast.76), calls=%async_computation | async-start | bytes 1572864 | tf_op jit(solution)/shard_map/all_to_all | solution.py:842
  59.1 24.7 %all-to-all-start.1 = ((bf16[8,64,768]{2,1,0:T(8,128)(2,1)}), bf16[8,64,768]{2,1,0:T(8,128)(2,1)S(1)}, u32[]{:S(2)}, u32[]{:S(2)}) async-start(bf16[8,64,768]{2,1,0:T(8,128)(2,1)} %bitcast.75), calls=%async_computation.1 | async-start | bytes 1572864 | tf_op jit(solution)/shard_map/all_to_all | solution.py:843
  62.7 410.5 %reduce-scatter.3.cloned.1.call-start = ((), (), s32[]{:S(2)}) async-start(), calls=%async_computation.8 | async-start | bytes 21233664 | tf_op jit(solution)/shard_map/reduce_scatter | solution.py:864
  294.7 250.7 %reduce-scatter.5.cloned.1.call-start = ((), (), s32[]{:S(2)}) async-start(), calls=%async_computation.9 | async-start | bytes 5308416 | tf_op jit(solution)/shard_map/reduce_scatter | solution.py:901
  473.2 12.0 %copy-start.4 = (f32[24,768]{1,0:T(8,128)S(1)}, f32[24,768]{1,0:T(8,128)}, u32[]{:S(2)}) copy-start(f32[24,768]{1,0:T(8,128)} %get-tuple-element.88) | copy-start | bytes 221188
  473.2 12.0 %copy-start.8 = (f32[8,768]{1,0:T(8,128)S(1)}, f32[8,768]{1,0:T(8,128)}, u32[]{:S(2)}) copy-start(f32[8,768]{1,0:T(8,128)} %get-tuple-element.89) | copy-start | bytes 73732
  473.2 38.5 %copy-start.7 = (f32[16,512]{1,0:T(8,128)S(1)}, f32[16,512]{1,0:T(8,128)}, u32[]{:S(2)}) copy-start(f32[16,512]{1,0:T(8,128)} %get-tuple-element.83) | copy-start | bytes 98308
  473.2 34.3 %all-to-all-start.2 = ((bf16[8,64,768]{2,1,0:T(8,128)(2,1)}), bf16[8,64,768]{2,1,0:T(8,128)(2,1)S(1)}, u32[]{:S(2)}, u32[]{:S(2)}) async-start(bf16[8,64,768]{2,1,0:T(8,128)(2,1)} %bitcast.25), calls=%async_computation.2 | async-start | bytes 1572864 | tf_op jit(solution)/shard_map/all_to_all | solution.py:878
  485.2 5.9 %collective-permute-start.6 = (f32[32,768]{1,0:T(8,128)S(1)}, f32[32,768]{1,0:T(8,128)S(1)}, u32[]{:S(2)}, u32[]{:S(2)}) collective-permute-start(f32[32,768]{1,0:T(8,128)S(1)} %constant_dynamic-update-slice_fusion), channel_id=1, source_target_pairs={{0,1},{1,0},{2,3},{3,2},{4,5},{5,4},{6,7},{7,6},{8,9},{9,8},{10,11... | collective-permute-start | bytes 294920 | tf_op jit(solution)/shard_map/ppermute | solution.py:894
  491.1 7.7 %collective-permute-start.7 = (f32[32,768]{1,0:T(8,128)S(1)}, f32[32,768]{1,0:T(8,128)S(1)}, u32[]{:S(2)}, u32[]{:S(2)}) collective-permute-start(f32[32,768]{1,0:T(8,128)S(1)} %add.83), channel_id=1, source_target_pairs={{0,2},{1,3},{2,0},{3,1},{4,6},{5,7},{6,4},{7,5},{8,10},{9,11},{10,... | collective-permute-start | bytes 294920 | tf_op jit(solution)/shard_map/ppermute | solution.py:894
  498.9 1.4 collective-permute-start.8
  500.2 4.9 collective-permute-start.9
  505.2 7.6 %collective-permute-start.10 = (f32[32,768]{1,0:T(8,128)S(1)}, f32[32,768]{1,0:T(8,128)S(1)}, u32[]{:S(2)}, u32[]{:S(2)}) collective-permute-start(f32[32,768]{1,0:T(8,128)S(1)} %add.86), channel_id=1, source_target_pairs={{0,16},{4,20},{8,24},{12,28},{16,0},{20,4},{24,8},{28,12},{1,17},{... | collective-permute-start | bytes 294920 | tf_op jit(solution)/shard_map/ppermute | solution.py:894
  507.5 41.9 %copy-start.2 = (bf16[8,64,768]{2,1,0:T(8,128)(2,1)}, bf16[8,64,768]{2,1,0:T(8,128)(2,1)S(1)}, u32[]{:S(2)}) copy-start(bf16[8,64,768]{2,1,0:T(8,128)(2,1)S(1)} %all-to-all-done.2) | copy-start | bytes 2359300
  507.5 51.0 %all-to-all-start.3 = ((bf16[8,64,768]{2,1,0:T(8,128)(2,1)}), bf16[8,64,768]{2,1,0:T(8,128)(2,1)}, u32[]{:S(2)}, u32[]{:S(2)}) async-start(bf16[8,64,768]{2,1,0:T(8,128)(2,1)} %bitcast.27), calls=%async_computation.3 | async-start | bytes 1572864 | tf_op jit(solution)/shard_map/all_to_all | solution.py:887
  550.2 19.3 %collective-permute-start.5 = (bf16[96,4,192]{2,0,1:T(8,128)(2,1)}, bf16[96,4,192]{2,0,1:T(8,128)(2,1)}, u32[]{:S(2)}, u32[]{:S(2)}) collective-permute-start(bf16[96,4,192]{2,0,1:T(8,128)(2,1)} %bitcast.62), channel_id=1, source_target_pairs={{0,3},{1,2},{2,1},{3,0},{4,7},{5,6},{6,5},{7,4},{8,11},{9,10},{10,... | collective-permute-start | bytes 442376 | tf_op jit(solution)/shard_map/ppermute | solution.py:820
  554.2 16.3 %collective-permute-start.4 = (bf16[96,4,192]{2,0,1:T(8,128)(2,1)}, bf16[96,4,192]{2,0,1:T(8,128)(2,1)}, u32[]{:S(2)}, u32[]{:S(2)}) collective-permute-start(bf16[96,4,192]{2,0,1:T(8,128)(2,1)} %bitcast.63), channel_id=1, source_target_pairs={{0,2},{1,3},{2,0},{3,1},{4,6},{5,7},{6,4},{7,5},{8,10},{9,11},{10,... | collective-permute-start | bytes 442376 | tf_op jit(solution)/shard_map/ppermute | solution.py:820
  554.9 15.6 %collective-permute-start.3 = (bf16[96,4,192]{2,0,1:T(8,128)(2,1)}, bf16[96,4,192]{2,0,1:T(8,128)(2,1)}, u32[]{:S(2)}, u32[]{:S(2)}) collective-permute-start(bf16[96,4,192]{2,0,1:T(8,128)(2,1)} %bitcast.64), channel_id=1, source_target_pairs={{0,1},{1,0},{2,3},{3,2},{4,5},{5,4},{6,7},{7,6},{8,9},{9,8},{10,11... | collective-permute-start | bytes 442376 | tf_op jit(solution)/shard_map/ppermute | solution.py:820
  (9 other events, 69.7 us)
Sparse Core Ops, SparseCore 0:
  33.1 54.8 all-gather.2
  90.4 98.5 all-gather.4
  294.8 146.9 reduce-scatter.2
  473.3 71.9 reduce-scatter.4

commit v4 on v3

--- a/solution.py
+++ b/solution.py
@@ -617,6 +617,237 @@
     line.leave()
 
 
+class Peers:
+    def __init__(self):
+        self.d, self.t = lax.axis_index("dp"), lax.axis_index("tensor")
+        self.sent = []
+
+    def enter(self, targets):
+        sem = pltpu.get_barrier_semaphore()
+        for where in targets:
+            pl.semaphore_signal(sem, 1, device_id=where, device_id_type=pl.DeviceIdType.MESH)
+        pl.semaphore_wait(sem, len(targets))
+
+    def copy(self, where, src, dst, sems):
+        return pltpu.make_async_remote_copy(
+            src_ref=src,
+            dst_ref=dst,
+            send_sem=sems[0],
+            recv_sem=sems[1],
+            device_id=where,
+            device_id_type=pl.DeviceIdType.MESH,
+        )
+
+    def send(self, where, src, dst, sems):
+        copy = self.copy(where, src, dst, sems)
+        copy.start()
+        self.sent.append(copy)
+
+    def leave(self):
+        for copy in self.sent:
+            copy.wait_send()
+
+
+def flip(index, bit):
+    return index + bit * (1 - 2 * ((index // bit) % 2))
+
+
+def finish_body(n_dp, size, x0_ref, x1_ref, x2_ref, h_ref, dq_ref, dk_ref, dv_ref, da_ref, o_ref, w_ref, dx_ref, gain_ref,
+                y_ref, small_ref, pos_ref,
+                yo_ref, go_ref, gw_ref, sum_ref,
+                d0_ref, d1_ref, d2_ref, ra_ref, rb_ref, out_ref, yr_ref, gr_ref, part_ref, r1_ref, r2_ref, r3_ref,
+                zs_ref, zr_ref, cur_ref, got_ref,
+                sems_s, sems_r, sy, ry, sg, rg, s1, r1, s2, r2, s3, r3, sz, rz, sb, rb):
+    rows = x0_ref.shape[0]
+    share = rows // n_dp
+    line = Line(size)
+    last = size - 1
+    block = 256
+    net = Peers()
+    d, t = net.d, net.t
+    place = pick(iota((rows, rows), 0) == pos_ref[...])
+    around = [(j, lax.rem(d + j, n_dp), lax.rem(d + n_dp - j, n_dp)) for j in range(1, n_dp)]
+    along = [(j, lax.rem(t + j, size), lax.rem(t + size - j, size)) for j in range(1, size)]
+    net.enter([{"dp": to} for _, to, _ in around] + [{"tensor": to} for _, to, _ in along])
+
+    def scatter(src_ref, dst_ref, sems):
+        for j, to, _ in around:
+            net.send({"dp": to}, src_ref.at[to], dst_ref.at[d], (sems[0].at[j - 1], sems[1].at[j - 1]))
+        dst_ref[d] = src_ref[d]
+
+    def gathered(dst_ref, sems):
+        for j, _, source in around:
+            held = dst_ref.at[source]
+            net.copy({"dp": source}, held, held, (sems[0].at[j - 1], sems[1].at[j - 1])).wait_recv()
+
+    scatter(y_ref, yr_ref, (sy, ry))
+
+    def hidden(c, d_ref):
+        def one(i, _):
+            at = pl.ds(pl.multiple_of(i * block, block), block)
+            to = pl.ds(pl.multiple_of(c * rows + i * block, block), block)
+            total = mm(dk_ref[to, :], w_ref[:, D : 2 * D], NT) + mm(dv_ref[to, :], w_ref[:, 2 * D : 3 * D], NT)
+            if c == 2:
+                total = total + mm(dq_ref[at, :], w_ref[:, 0:D], NT)
+            d_ref[at, :] = total.astype(d_ref.dtype)
+            return 0
+
+        lax.fori_loop(0, rows // block, one, 0)
+
+    def gain_of(x_ref, d_ref):
+        x = x_ref[...].astype(F32)
+        r = lax.rsqrt(jnp.mean(x * x, axis=1, keepdims=True) + EPSILON)
+        return jnp.sum(d_ref[...].astype(F32) * x * r, axis=0, keepdims=True)
+
+    core, x, y = lax.rem(d, 2), lax.rem(d // 2, 2), d // 4
+    there = ({"dp": flip(d, 2)}, {"dp": flip(d, 4)})
+    deep = D // n_dp
+
+    def weight(u, left, right_ref):
+        for c in range(D // 256):
+            cols = slice(c * 256, (c + 1) * 256)
+            value = mm(left, right_ref[:, cols], TN).astype(BF16)
+            part_ref[u, :, :, cols] = value.reshape(n_dp, deep, 256)
+        for j in range(4):
+            net.send({"dp": flip(d, 1)}, part_ref.at[u, 2 * j + 1 - core], r1_ref.at[u, j], (s1.at[u, j], r1.at[u, j]))
+
+    def add(u, j, arrived):
+        spot = 2 * j + core
+        part_ref[u, spot] = (part_ref[u, spot].astype(F32) + arrived[...].astype(F32)).astype(BF16)
+
+    def chips(u):
+        if u % 2 == 0:
+            first = (there[0], [2 * i + 1 - x for i in range(2)], [2 * i + x for i in range(2)])
+            return first, (there[1], 2 * (1 - y) + x)
+        first = (there[1], [2 * (1 - y) + i for i in range(2)], [2 * y + i for i in range(2)])
+        return first, (there[0], 2 * y + 1 - x)
+
+    def halve(u):
+        for j in range(4):
+            held = r1_ref.at[u, j]
+            net.copy({"dp": flip(d, 1)}, held, held, (s1.at[u, j], r1.at[u, j])).wait_recv()
+            add(u, j, held)
+        where, theirs, _ = chips(u)[0]
+        for i in range(2):
+            net.send(where, part_ref.at[u, 2 * theirs[i] + core], r2_ref.at[u, i], (s2.at[u, i], r2.at[u, i]))
+
+    def quarter(u):
+        (where, _, mine), (after, spot) = chips(u)
+        for i in range(2):
+            held = r2_ref.at[u, i]
+            net.copy(where, held, held, (s2.at[u, i], r2.at[u, i])).wait_recv()
+            add(u, mine[i], held)
+        net.send(after, part_ref.at[u, 2 * spot + core], r3_ref.at[u], (s3.at[u], r3.at[u]))
+
+    def own(u):
+        after = chips(u)[1][0]
+        held = r3_ref.at[u]
+        net.copy(after, held, held, (s3.at[u], r3.at[u])).wait_recv()
+        value = part_ref[u, d].astype(F32) + held[...].astype(F32)
+        wide_share = D // size
+        for p in range(size):
+            zs_ref[u, p] = value[:, p * wide_share : (p + 1) * wide_share].astype(BF16)
+        for j, to, _ in along:
+            net.send({"tensor": to}, zs_ref.at[u, to], zr_ref.at[u, j - 1], (sz.at[u, j - 1], rz.at[u, j - 1]))
+
+    def whole(u):
+        total = zs_ref[u, t].astype(F32)
+        for j, _, source in along:
+            held = zr_ref.at[u, j - 1]
+            net.copy({"tensor": source}, held, held, (sz.at[u, j - 1], rz.at[u, j - 1])).wait_recv()
+            total = total + held[...].astype(F32)
+        gw_ref[u] = total
+
+    steps = [("tensor", bit) for bit in (1, 2, 4, 8) if bit < size] + [("dp", bit) for bit in (1, 2, 4, 8) if bit < n_dp]
+
+    def small_out(i):
+        axis, bit = steps[i]
+        mine = t if axis == "tensor" else d
+        net.send({axis: flip(mine, bit)}, cur_ref.at[i], got_ref.at[i], (sb.at[i], rb.at[i]))
+
+    def small_in(i):
+        axis, bit = steps[i]
+        mine = t if axis == "tensor" else d
+        held = got_ref.at[i]
+        net.copy({axis: flip(mine, bit)}, held, held, (sb.at[i], rb.at[i])).wait_recv()
+        total = cur_ref[i] + held[...]
+        if i + 1 < len(steps):
+            cur_ref[i + 1] = total
+            small_out(i + 1)
+        else:
+            sum_ref[...] = total
+
+    hidden(0, d2_ref)
+
+    def first(k):
+        if k > 1:
+            line.send(k, k - 1, lambda: (d2_ref, ra_ref, (sems_s.at[0], sems_r.at[0])))
+
+    line.each(first)
+    h = h_ref[...]
+    weight(0, h, dk_ref)
+    hidden(1, d1_ref)
+    gain = gain_of(x2_ref, d2_ref) + gain_of(x1_ref, d1_ref)
+
+    def second(k):
+        if 0 < k < last:
+            line.arrived(k, ra_ref, (sems_s.at[0], sems_r.at[0]))
+            d1_ref[...] = (d1_ref[...].astype(F32) + ra_ref[...].astype(F32)).astype(BF16)
+        if k > 0:
+            line.send(k, k - 1, lambda: (d1_ref, rb_ref, (sems_s.at[1], sems_r.at[1])))
+
+    line.each(second)
+    weight(1, h, dv_ref)
+    halve(0)
+    hidden(2, d0_ref)
+    gain = gain + gain_of(x0_ref, d0_ref)
+    rest = small_ref.shape[0]
+    cur_ref[0, 0:rest, :] = small_ref[...]
+    cur_ref[0, rest : rest + 8, :] = jnp.broadcast_to(gain, (8, D))
+    small_out(0)
+    weight(2, h[2 * rows :], dq_ref)
+    halve(1)
+    quarter(0)
+    small_in(0)
+    weight(3, da_ref[...], o_ref)
+    halve(2)
+    quarter(1)
+    own(0)
+    small_in(1)
+    gathered(yr_ref, (sy, ry))
+    yo_ref[...] = mm(place, yr_ref[...].reshape(rows, D), TN).astype(BF16)
+
+    def third(k):
+        if k < last:
+            line.arrived(k, rb_ref, (sems_s.at[1], sems_r.at[1]))
+            d0_ref[...] += rb_ref[...].astype(F32)
+
+    line.each(third)
+    xv = x0_ref[...].astype(F32)
+    r = lax.rsqrt(jnp.mean(xv * xv, axis=1, keepdims=True) + EPSILON)
+    xr = xv * r
+    scaled = d0_ref[...] * gain_ref[...]
+    value = dx_ref[...] + r * (scaled - xr * jnp.mean(xr * scaled, axis=1, keepdims=True))
+    out_ref[...] = value.astype(BF16).reshape(n_dp, share, D)
+    scatter(out_ref, gr_ref, (sg, rg))
+    halve(3)
+    quarter(2)
+    own(1)
+    small_in(2)
+    quarter(3)
+    own(2)
+    small_in(3)
+    own(3)
+    for i in range(4, len(steps)):
+        small_in(i)
+    gathered(gr_ref, (sg, rg))
+    go_ref[...] = mm(place, gr_ref[...].reshape(rows, D), TN).astype(BF16)
+    for u in range(4):
+        whole(u)
+    line.leave()
+    net.leave()
+
+
 def experts_body(ff, chunks, cnt_ref, h_refs, g_refs, slot_ref, w_ref, o_refs, d_refs, gw_ref,
                  xbuf, gbuf, cbuf, onehot, fbuf, dbuf, gacc, gates, dgrow, off_ref, base_ref, nt_ref):
     rows = slot_ref.shape[2]
@@ -875,37 +1106,58 @@
         + [dma(n_t - 1, 2)] * 4 + [dma(n_t - 1, 1)] * 4,
         meet=1,
     )
-    back_out = lax.all_to_all(result, "dp", split_axis=0, concat_axis=0, tiled=True)
-    gw_attn, gain_part, d_start = call(
-        functools.partial(grads_body, n_t),
-        "grads",
-        [((D, 4 * D), BF16), ((8, D), F32), (row, BF16)],
-        [x0, x1, x2, h, dq, dk, dv, da, o, w_attn, dx, gain_attn],
-        scratch=[pltpu.VMEM(row, F32)] + [pltpu.VMEM(row, BF16)] * 4 + [dma(2), dma(2)],
-        meet=2,
-    )
-    back_grad = lax.all_to_all(d_start, "dp", split_axis=0, concat_axis=0, tiled=True)
-    output, grad_tokens = call(restore_body, "restore", [(row, BF16)] * 2, [pos, back_out, back_grad])
-
-    def total(v):
-        for axis, count in (("tensor", n_t), ("dp", n_dp)):
-            bit = 1
-            while bit < count:
-                v = v + lax.ppermute(v, axis, [(i, i ^ bit) for i in range(count)])
-                bit *= 2
-        return v
-
-    small_all = total(jnp.concatenate([small, gain_part], axis=0))
-    gain_all = small_all[SPARE + 8]
-    gw_attn, ff_sum = lax.optimization_barrier((gw_attn, ff_sum))
-    attn_sum = lax.psum_scatter(gw_attn, "dp", scatter_dimension=0, tiled=True).reshape(d_here, 4, n_t, D // n_t)
-
-    def share(j):
-        return lax.dynamic_index_in_dim(attn_sum, t ^ j, 2, keepdims=False)
-
-    attn_own = share(0).astype(F32)
-    for j in range(1, n_t):
-        attn_own = attn_own + swap(share(j), j).astype(F32)
+    if n_dp == 8 and d_here % 16 == 0 and rows % 128 == 0:
+        units, share = 4, rows // n_dp
+        piece = (d_here, D)
+        hops = 3 + (n_t - 1).bit_length()
+        output, grad_tokens, attn_parts, small_all = call(
+            functools.partial(finish_body, n_dp, n_t),
+            "finish",
+            [(row, BF16), (row, BF16), ((units, d_here, D // n_t), F32), ((SPARE + 16, D), F32)],
+            [x0, x1, x2, h, dq, dk, dv, da, o, w_attn, dx, gain_attn, result.reshape(n_dp, share, D), small, pos],
+            scratch=[pltpu.VMEM(row, F32)] + [pltpu.VMEM(row, BF16)] * 4 + [pltpu.VMEM((n_dp, share, D), BF16)] * 3
+            + [pltpu.VMEM((units, n_dp) + piece, BF16), pltpu.VMEM((units, 4) + piece, BF16), pltpu.VMEM((units, 2) + piece, BF16),
+               pltpu.VMEM((units,) + piece, BF16), pltpu.VMEM((units, n_t, d_here, D // n_t), BF16),
+               pltpu.VMEM((units, n_t - 1, d_here, D // n_t), BF16)]
+            + [pltpu.VMEM((hops, SPARE + 16, D), F32)] * 2
+            + [dma(2)] * 2 + [dma(n_dp - 1)] * 4 + [dma(units, 4)] * 2 + [dma(units, 2)] * 2 + [dma(units)] * 2
+            + [dma(units, n_t - 1)] * 2 + [dma(hops)] * 2,
+            meet=2,
+        )
+        gain_all = small_all[SPARE + 8]
+        attn_own = jnp.stack([attn_parts[2], attn_parts[0], attn_parts[1], attn_parts[3]], axis=1)
+    else:
+        back_out = lax.all_to_all(result, "dp", split_axis=0, concat_axis=0, tiled=True)
+        gw_attn, gain_part, d_start = call(
+            functools.partial(grads_body, n_t),
+            "grads",
+            [((D, 4 * D), BF16), ((8, D), F32), (row, BF16)],
+            [x0, x1, x2, h, dq, dk, dv, da, o, w_attn, dx, gain_attn],
+            scratch=[pltpu.VMEM(row, F32)] + [pltpu.VMEM(row, BF16)] * 4 + [dma(2), dma(2)],
+            meet=2,
+        )
+        back_grad = lax.all_to_all(d_start, "dp", split_axis=0, concat_axis=0, tiled=True)
+        output, grad_tokens = call(restore_body, "restore", [(row, BF16)] * 2, [pos, back_out, back_grad])
+
+        def total(v):
+            for axis, count in (("tensor", n_t), ("dp", n_dp)):
+                bit = 1
+                while bit < count:
+                    v = v + lax.ppermute(v, axis, [(i, i ^ bit) for i in range(count)])
+                    bit *= 2
+            return v
+
+        small_all = total(jnp.concatenate([small, gain_part], axis=0))
+        gain_all = small_all[SPARE + 8]
+        gw_attn, ff_sum = lax.optimization_barrier((gw_attn, ff_sum))
+        attn_sum = lax.psum_scatter(gw_attn, "dp", scatter_dimension=0, tiled=True).reshape(d_here, 4, n_t, D // n_t)
+
+        def share(j):
+            return lax.dynamic_index_in_dim(attn_sum, t ^ j, 2, keepdims=False)
+
+        attn_own = share(0).astype(F32)
+        for j in range(1, n_t):
+            attn_own = attn_own + swap(share(j), j).astype(F32)
     ff_own = ff_sum.reshape(d_here, EXPERTS, 3 * ff).astype(F32)
     return (
         output,

time: 585 us -> 559 us (0.956)
  waiting for transfers between devices: 93.5 us -> 44.7 us
  Pallas kernels: 390 us -> 434 us
  starting transfers between devices: 40.5 us -> 13.1 us
    pallas_call x5 -> x4, Pallas kernels: 316 us -> 355 us  [call(): pl.pallas_call(body, name=name, out_shape=[jax.ShapeDtypeStruct(*o) for o...]
    reduce_scatter x1 -> x0, waiting for transfers between devices: 32.6 us -> none  [body(): lax.psum_scatter(gw_attn, 'dp', scatter_dimension=0, tiled=True)]
    all_to_all x2 -> x0, starting transfers between devices: 16.2 us -> none  [the longest x1 12 us: body(): lax.all_to_all(result, 'dp', split_axis=0, concat_axis=0, tiled=True)]
    ppermute x5 -> x0, waiting for transfers between devices: 15.9 us -> none  [total(): v = v + lax.ppermute(v, axis, [(i, i ^ bit) for i in range(count)])]
    ppermute x5 -> x0, starting transfers between devices: 6.7 us -> none  [total(): v = v + lax.ppermute(v, axis, [(i, i ^ bit) for i in range(count)])]
    ppermute x6 -> x3, waiting for transfers between devices: 17 us -> 13.1 us  [swap(): return lax.ppermute(v, 'tensor', [(i, i ^ j) for i in range(n_t)])]
  transfers between devices with their start and end apart: 19 -> 8, of which waited for: 12 -> 5; matrix products, arithmetic and copies ran while one was open for 6% -> 5% of each run, Pallas kernels for 54% -> 65%
where the time goes in v4:
time: 559 us; the launch traced here: 548 us
  Pallas kernels  434 us (78%)
  waiting for transfers between devices  44.7 us (8%)
  local copies, waits for them, and re-layouts  32.4 us (6%)
  between operations  14.4 us (3%)
  starting transfers between devices  13.1 us (2%)
  other arithmetic  10 us (2%)
    pallas_call x4, Pallas kernels, call(): pl.pallas_call(body, name=name, out_shape=[jax.ShapeDtypeStruct(*o) for o...  355 us
    pallas_call x1, Pallas kernels, experts_call(): pl.pallas_call(functools.partial(experts_body, ff, chunks), name='experts...  78.9 us
    all_to_all x1, waiting for transfers between devices, body(): g0 = lax.all_to_all(gs, 'dp', split_axis=0, concat_axis=0, tiled=True)  15.5 us
    ppermute x3, waiting for transfers between devices, swap(): return lax.ppermute(v, 'tensor', [(i, i ^ j) for i in range(n_t)])  13.1 us
    all_to_all x1, waiting for transfers between devices, body(): x0 = lax.all_to_all(xs, 'dp', split_axis=0, concat_axis=0, tiled=True)  11.7 us
  transfers between devices with their start and end apart: 8, of which 5 were waited for; matrix products, arithmetic and copies ran while one was open for 5% of the time, Pallas kernels for 65%

profile of v4, /device:TPU:0, one launch (start us, length us, event | category | flops | bytes accessed | tf_op | source)
XLA Modules:
  0.0 548.5 jit_solution(9910199216291269174)
XLA Ops:
  8.2 4.1 collective-permute-start.1
  13.9 12.6 %collective-permute-done.1 = bf16[96,4,192]{2,0,1:T(8,128)(2,1)S(1)} collective-permute-done((bf16[96,4,192]{2,0,1:T(8,128)(2,1)S(1)}, bf16[96,4,192]{2,0,1:T(8,128)(2,1)S(1)}, u32[]{:S(2)}, u32[]{:S(2)}) %collective-permute-start.1) | collective-permute-done | bytes 147488 | tf_op jit(solution)/shard_map/ppermute | solution.py:1051
  28.1 1.8 reshape.91
  32.5 2.2 copy.31
  34.7 3.5 deal.1
  38.3 3.8 all-to-all-start
  47.4 11.7 %all-to-all-done = bf16[8,64,768]{2,1,0:T(8,128)(2,1)S(1)} async-done(((bf16[8,64,768]{2,1,0:T(8,128)(2,1)}), bf16[8,64,768]{2,1,0:T(8,128)(2,1)S(1)}, u32[]{:S(2)}, u32[]{:S(2)}) %all-to-all-start) | async-done | bytes 786464 | tf_op jit(solution)/shard_map/all_to_all | solution.py:1073
  59.1 3.5 all-to-all-start.1
  62.7 2.8 fusion
  65.6 2.4 pad_maximum_fusion.3
  68.0 15.5 %all-to-all-done.1 = bf16[8,64,768]{2,1,0:T(8,128)(2,1)S(1)} async-done(((bf16[8,64,768]{2,1,0:T(8,128)(2,1)}), bf16[8,64,768]{2,1,0:T(8,128)(2,1)S(1)}, u32[]{:S(2)}, u32[]{:S(2)}) %all-to-all-start.1) | async-done | bytes 786464 | tf_op jit(solution)/shard_map/all_to_all | solution.py:1074
  84.4 4.2 all-gather.3.cloned.1.call-done.w_ref
  88.6 132.7 %forward.1 = (bf16[512,768]{1,0:T(8,128)(2,1)}, bf16[512,768]{1,0:T(8,128)(2,1)}, bf16[1536,768]{1,0:T(8,128)(2,1)}, bf16[512,768]{1,0:T(8,128)(2,1)}, bf16[1536...) custom-call(bf16[512,768]{1,0:T(8,128)(2,1)} %bitcast.58, ...), custom_call_target="tpu_custom_call" | custom-call | tf_op jit(solution)/shard_map/forward/pallas_call | solution.py:63
  221.4 78.9 %experts.1 = (bf16[4,512,768]{2,1,0:T(8,128)(2,1)}, bf16[4,528,768]{2,1,0:T(8,128)(2,1)}, bf16[768,12288]{1,0:T(8,128)(2,1)}) custom-call(s32[32]{0:T(128)} %reshape_squeeze.3.cnt_ref, bf16[4,528,768]{2,1,0:T(8,128)(2,1)} %get-tuple-element.54.h_refs, bf16[4,512,768]{2,1,0:T(8,128)(2,1)} %get-tuple-element.55.g_refs, ...), custom_call_target="tpu_custom_call" | custom-call | tf_op jit(solution)/shard_map/experts/pallas_call | solution.py:998
  300.3 2.1 dynamic-slice_bitcast_fusion.h2_ref
  302.3 129.2 %backward.1 = (f32[512,768]{1,0:T(8,128)}, bf16[512,768]{1,0:T(8,128)(2,1)}, f32[16,512]{1,0:T(8,128)}, f32[24,768]{1,0:T(8,128)}, bf16[512,768]{1,0:T(8,128)(2,...) custom-call(bf16[4,528,768]{2,1,0:T(8,128)(2,1)} %get-tuple-element.57.back_ref, ...), custom_call_target="tpu_custom_call" | custom-call | tf_op jit(solution)/shard_map/backward/pallas_call | solution.py:63
  431.6 89.5 %finish.1 = (bf16[512,768]{1,0:T(8,128)(2,1)}, bf16[512,768]{1,0:T(8,128)(2,1)}, f32[4,96,192]{2,1,0:T(8,128)}, f32[32,768]{1,0:T(8,128)}) custom-call(bf16[512,768]{1,0:T(8,128)(2,1)} %bitcast.59, bf16[512,768]{1,0:T(8,128)(2,1)} %get-tuple-element.50.x1_ref, bf16[512,768]{1,0:T(8,128)(2,1)} %get-tuple-element.51.x2_ref, ...), custom_call_target="tpu_custom_call" | custom-call | tf_op jit(solution)/shard_map/finish/pallas_call | solution.py:63
  523.8 1.4 slice_reduce_fusion.1
  525.1 1.7 slice_bitcast_fusion
  528.2 1.4 slice_bitcast_fusion.4
  529.6 2.5 copy.32
  533.7 3.7 reshape.99
  537.4 2.1 copy.35
  539.5 2.1 copy.36
  (63 shorter events, 18.6 us)
Async XLA Ops:
  7.2 81.4 %all-gather.3.cloned.1.call-start = ((), (), s32[]{:S(2)}) async-start(), calls=%async_computation.3 | async-start | bytes 5308416 | tf_op jit(solution)/shard_map/all_gather | solution.py:1059
  8.2 18.4 %collective-permute-start.1 = (bf16[96,4,192]{2,0,1:T(8,128)(2,1)S(1)}, bf16[96,4,192]{2,0,1:T(8,128)(2,1)S(1)}, u32[]{:S(2)}, u32[]{:S(2)}) collective-permute-start(bf16[96,4,192]{2,0,1:T(8,128)(2,1)S(1)} %get-tuple-element.97), channel_id=1, source_target_pairs={{0,2},{1,3},{2,0},{3,1},{4,6},{5,7},{6,4},{7,5},{8,10},{9,11},{10,... | collective-permute-start | bytes 442376 | tf_op jit(solution)/shard_map/ppermute | solution.py:1051
  12.3 14.2 %collective-permute-start.2 = (bf16[96,4,192]{2,0,1:T(8,128)(2,1)S(1)}, bf16[96,4,192]{2,0,1:T(8,128)(2,1)S(1)}, u32[]{:S(2)}, u32[]{:S(2)}) collective-permute-start(bf16[96,4,192]{2,0,1:T(8,128)(2,1)S(1)} %get-tuple-element.97), channel_id=1, source_target_pairs={{0,3},{1,2},{2,1},{3,0},{4,7},{5,6},{6,5},{7,4},{8,11},{9,10},{10,... | collective-permute-start | bytes 442376 | tf_op jit(solution)/shard_map/ppermute | solution.py:1051
  13.7 13.4 %collective-permute-start = (bf16[96,4,192]{2,0,1:T(8,128)(2,1)S(1)}, bf16[96,4,192]{2,0,1:T(8,128)(2,1)S(1)}, u32[]{:S(2)}, u32[]{:S(2)}) collective-permute-start(bf16[96,4,192]{2,0,1:T(8,128)(2,1)S(1)} %get-tuple-element.97), channel_id=1, source_target_pairs={{0,1},{1,0},{2,3},{3,2},{4,5},{5,4},{6,7},{7,6},{8,9},{9,8},{10,11... | collective-permute-start | bytes 442376 | tf_op jit(solution)/shard_map/ppermute | solution.py:1051
  27.3 2.7 copy-start.2
  30.0 191.4 %all-gather.5.cloned.1.call-start = ((), (), s32[]{:S(2)}) async-start(), calls=%async_computation.4 | async-start | bytes 21233664 | tf_op jit(solution)/shard_map/all_gather | solution.py:1061
  34.7 8.2 %copy-start.10 = (s32[1,8]{1,0:T(1,128)S(1)}, s32[1,8]{1,0:T(1,128)}, u32[]{:S(2)}) copy-start(s32[1,8]{1,0:T(1,128)} %param.18) | copy-start | bytes 100
  34.7 8.3 %copy-start.6 = (f32[2,768,2]{1,2,0:T(2,128)S(1)}, f32[2,768,2]{1,2,0:T(2,128)}, u32[]{:S(2)}) copy-start(f32[2,768,2]{1,2,0:T(2,128)} %param.28) | copy-start | bytes 36868
  34.7 8.4 %copy-start.8 = (f32[768]{0:T(1024)S(1)}, f32[768]{0:T(1024)}, u32[]{:S(2)}) copy-start(f32[768]{0:T(1024)} %param.25) | copy-start | bytes 9220
  34.7 9.0 %copy-start.9 = (f32[768]{0:T(1024)S(1)}, f32[768]{0:T(1024)}, u32[]{:S(2)}) copy-start(f32[768]{0:T(1024)} %param.26) | copy-start | bytes 9220
  34.7 9.5 %copy-start.4 = (f32[512,12]{0,1:T(8,128)S(1)}, f32[512,12]{0,1:T(8,128)}, u32[]{:S(2)}) copy-start(f32[512,12]{0,1:T(8,128)} %param.20) | copy-start | bytes 73732
  34.7 10.1 %copy-start.7 = (f32[2,768]{1,0:T(2,128)S(1)}, f32[2,768]{1,0:T(2,128)}, u32[]{:S(2)}) copy-start(f32[2,768]{1,0:T(2,128)} %param.29) | copy-start | bytes 18436
  34.7 11.4 %copy-start.3 = (f32[768,12]{0,1:T(8,128)S(1)}, f32[768,12]{0,1:T(8,128)}, u32[]{:S(2)}) copy-start(f32[768,12]{0,1:T(8,128)} %param.27) | copy-start | bytes 110596
  38.3 20.9 %all-to-all-start = ((bf16[8,64,768]{2,1,0:T(8,128)(2,1)}), bf16[8,64,768]{2,1,0:T(8,128)(2,1)S(1)}, u32[]{:S(2)}, u32[]{:S(2)}) async-start(bf16[8,64,768]{2,1,0:T(8,128)(2,1)} %bitcast.65), calls=%async_computation | async-start | bytes 1572864 | tf_op jit(solution)/shard_map/all_to_all | solution.py:1073
  59.1 8.9 %copy-start = (bf16[8,64,768]{2,1,0:T(8,128)(2,1)}, bf16[8,64,768]{2,1,0:T(8,128)(2,1)S(1)}, u32[]{:S(2)}) copy-start(bf16[8,64,768]{2,1,0:T(8,128)(2,1)S(1)} %all-to-all-done) | copy-start | bytes 2359300
  59.1 24.4 %all-to-all-start.1 = ((bf16[8,64,768]{2,1,0:T(8,128)(2,1)}), bf16[8,64,768]{2,1,0:T(8,128)(2,1)S(1)}, u32[]{:S(2)}, u32[]{:S(2)}) async-start(bf16[8,64,768]{2,1,0:T(8,128)(2,1)} %bitcast.64), calls=%async_computation.1 | async-start | bytes 1572864 | tf_op jit(solution)/shard_map/all_to_all | solution.py:1074
  62.7 466.9 %reduce-scatter.2.cloned.1.call-start = ((), (), s32[]{:S(2)}) async-start(), calls=%async_computation.5 | async-start | bytes 21233664 | tf_op jit(solution)/shard_map/reduce_scatter | solution.py:1095
  83.5 0.9 copy-start.1
  431.6 96.0 %copy-start.5 = (f32[16,512]{1,0:T(8,128)S(1)}, f32[16,512]{1,0:T(8,128)}, u32[]{:S(2)}) copy-start(f32[16,512]{1,0:T(8,128)} %get-tuple-element.80) | copy-start | bytes 98308
Sparse Core Ops, SparseCore 0:
  30.1 58.4 all-gather.2
  91.1 98.5 all-gather.4
  300.4 144.2 reduce-scatter.1

commit v5 on v4

--- a/solution.py
+++ b/solution.py
@@ -22,7 +22,7 @@
 SCORE_SCALE = HEAD_DIM**-0.5
 LOG2E = 1.4426950408889634
 TILE = 160
-ROWS = 256
+ROWS = 192
 SPARE = 16
 VMEM_CAP = 66_000_000
 
@@ -758,7 +758,7 @@
             total = total + held[...].astype(F32)
         gw_ref[u] = total
 
-    steps = [("tensor", bit) for bit in (1, 2, 4, 8) if bit < size] + [("dp", bit) for bit in (1, 2, 4, 8) if bit < n_dp]
+    steps = [("dp", bit) for bit in (1, 2, 4, 8) if bit < n_dp] + [("tensor", bit) for bit in (1, 2, 4, 8) if bit < size]
 
     def small_out(i):
         axis, bit = steps[i]
@@ -784,19 +784,16 @@
             line.send(k, k - 1, lambda: (d2_ref, ra_ref, (sems_s.at[0], sems_r.at[0])))
 
     line.each(first)
+    hidden(1, d1_ref)
+
+    def second(k):
+        if k == last:
+            line.send(k, k - 1, lambda: (d1_ref, rb_ref, (sems_s.at[1], sems_r.at[1])))
+
+    line.each(second)
     h = h_ref[...]
     weight(0, h, dk_ref)
-    hidden(1, d1_ref)
     gain = gain_of(x2_ref, d2_ref) + gain_of(x1_ref, d1_ref)
-
-    def second(k):
-        if 0 < k < last:
-            line.arrived(k, ra_ref, (sems_s.at[0], sems_r.at[0]))
-            d1_ref[...] = (d1_ref[...].astype(F32) + ra_ref[...].astype(F32)).astype(BF16)
-        if k > 0:
-            line.send(k, k - 1, lambda: (d1_ref, rb_ref, (sems_s.at[1], sems_r.at[1])))
-
-    line.each(second)
     weight(1, h, dv_ref)
     halve(0)
     hidden(2, d0_ref)
@@ -805,24 +802,39 @@
     cur_ref[0, 0:rest, :] = small_ref[...]
     cur_ref[0, rest : rest + 8, :] = jnp.broadcast_to(gain, (8, D))
     small_out(0)
+    halve(1)
+
+    def third(k):
+        if 0 < k < last:
+            line.arrived(k, ra_ref, (sems_s.at[0], sems_r.at[0]))
+            d1_ref[...] = (d1_ref[...].astype(F32) + ra_ref[...].astype(F32)).astype(BF16)
+            line.send(k, k - 1, lambda: (d1_ref, rb_ref, (sems_s.at[1], sems_r.at[1])))
+
+    line.each(third)
     weight(2, h[2 * rows :], dq_ref)
-    halve(1)
-    quarter(0)
     small_in(0)
     weight(3, da_ref[...], o_ref)
+    quarter(0)
+    quarter(1)
     halve(2)
-    quarter(1)
+    small_in(1)
+    halve(3)
     own(0)
-    small_in(1)
+    own(1)
     gathered(yr_ref, (sy, ry))
     yo_ref[...] = mm(place, yr_ref[...].reshape(rows, D), TN).astype(BF16)
-
-    def third(k):
+    quarter(2)
+    quarter(3)
+    small_in(2)
+    own(2)
+    own(3)
+
+    def fourth(k):
         if k < last:
             line.arrived(k, rb_ref, (sems_s.at[1], sems_r.at[1]))
             d0_ref[...] += rb_ref[...].astype(F32)
 
-    line.each(third)
+    line.each(fourth)
     xv = x0_ref[...].astype(F32)
     r = lax.rsqrt(jnp.mean(xv * xv, axis=1, keepdims=True) + EPSILON)
     xr = xv * r
@@ -830,20 +842,12 @@
     value = dx_ref[...] + r * (scaled - xr * jnp.mean(xr * scaled, axis=1, keepdims=True))
     out_ref[...] = value.astype(BF16).reshape(n_dp, share, D)
     scatter(out_ref, gr_ref, (sg, rg))
-    halve(3)
-    quarter(2)
-    own(1)
-    small_in(2)
-    quarter(3)
-    own(2)
-    small_in(3)
-    own(3)
-    for i in range(4, len(steps)):
+    for i in range(3, len(steps)):
         small_in(i)
+    for u in range(4):
+        whole(u)
     gathered(gr_ref, (sg, rg))
     go_ref[...] = mm(place, gr_ref[...].reshape(rows, D), TN).astype(BF16)
-    for u in range(4):
-        whole(u)
     line.leave()
     net.leave()
 

time: 559 us -> 550 us (0.984)
    pallas_call x4, Pallas kernels: 355 us -> 348 us  [call(): pl.pallas_call(body, name=name, out_shape=[jax.ShapeDtypeStruct(*o) for o...]
  transfers between devices with their start and end apart: 8 -> 8, of which waited for: 5 -> 5; matrix products, arithmetic and copies ran while one was open for 5% -> 5% of each run, Pallas kernels for 65% -> 64%
where the time goes in v5:
time: 550 us; the launch traced here: 545 us
  Pallas kernels  430 us (78%)
  waiting for transfers between devices  44.7 us (8%)
  local copies, waits for them, and re-layouts  32.4 us (6%)
  between operations  14.4 us (3%)
  starting transfers between devices  13.1 us (2%)
  other arithmetic  10 us (2%)
    pallas_call x4, Pallas kernels, call(): pl.pallas_call(body, name=name, out_shape=[jax.ShapeDtypeStruct(*o) for o...  348 us
    pallas_call x1, Pallas kernels, experts_call(): pl.pallas_call(functools.partial(experts_body, ff, chunks), name='experts...  81.8 us
    all_to_all x1, waiting for transfers between devices, body(): g0 = lax.all_to_all(gs, 'dp', split_axis=0, concat_axis=0, tiled=True)  15.5 us
    ppermute x3, waiting for transfers between devices, swap(): return lax.ppermute(v, 'tensor', [(i, i ^ j) for i in range(n_t)])  13.1 us
    all_to_all x1, waiting for transfers between devices, body(): x0 = lax.all_to_all(xs, 'dp', split_axis=0, concat_axis=0, tiled=True)  11.7 us
  transfers between devices with their start and end apart: 8, of which 5 were waited for; matrix products, arithmetic and copies ran while one was open for 5% of the time, Pallas kernels for 64%

profile of v5, /device:TPU:0, one launch (start us, length us, event | category | flops | bytes accessed | tf_op | source)
XLA Modules:
  0.0 544.8 jit_solution(7100340020286336931)
XLA Ops:
  8.2 4.1 collective-permute-start.1
  13.9 12.6 %collective-permute-done.1 = bf16[96,4,192]{2,0,1:T(8,128)(2,1)S(1)} collective-permute-done((bf16[96,4,192]{2,0,1:T(8,128)(2,1)S(1)}, bf16[96,4,192]{2,0,1:T(8,128)(2,1)S(1)}, u32[]{:S(2)}, u32[]{:S(2)}) %collective-permute-start.1) | collective-permute-done | bytes 147488 | tf_op jit(solution)/shard_map/ppermute | solution.py:1055
  28.1 1.8 reshape.91
  32.5 2.2 copy.31
  34.7 3.5 deal.1
  38.3 3.8 all-to-all-start
  47.4 11.7 %all-to-all-done = bf16[8,64,768]{2,1,0:T(8,128)(2,1)S(1)} async-done(((bf16[8,64,768]{2,1,0:T(8,128)(2,1)}), bf16[8,64,768]{2,1,0:T(8,128)(2,1)S(1)}, u32[]{:S(2)}, u32[]{:S(2)}) %all-to-all-start) | async-done | bytes 786464 | tf_op jit(solution)/shard_map/all_to_all | solution.py:1077
  59.1 3.5 all-to-all-start.1
  62.7 2.8 fusion
  65.6 2.4 pad_maximum_fusion.3
  68.0 15.5 %all-to-all-done.1 = bf16[8,64,768]{2,1,0:T(8,128)(2,1)S(1)} async-done(((bf16[8,64,768]{2,1,0:T(8,128)(2,1)}), bf16[8,64,768]{2,1,0:T(8,128)(2,1)S(1)}, u32[]{:S(2)}, u32[]{:S(2)}) %all-to-all-start.1) | async-done | bytes 786464 | tf_op jit(solution)/shard_map/all_to_all | solution.py:1078
  84.4 4.2 all-gather.3.cloned.1.call-done.w_ref
  88.6 132.7 %forward.1 = (bf16[512,768]{1,0:T(8,128)(2,1)}, bf16[512,768]{1,0:T(8,128)(2,1)}, bf16[1536,768]{1,0:T(8,128)(2,1)}, bf16[512,768]{1,0:T(8,128)(2,1)}, bf16[1536...) custom-call(bf16[512,768]{1,0:T(8,128)(2,1)} %bitcast.58, ...), custom_call_target="tpu_custom_call" | custom-call | tf_op jit(solution)/shard_map/forward/pallas_call | solution.py:63
  221.4 81.8 %experts.1 = (bf16[4,512,768]{2,1,0:T(8,128)(2,1)}, bf16[4,528,768]{2,1,0:T(8,128)(2,1)}, bf16[768,12288]{1,0:T(8,128)(2,1)}) custom-call(s32[32]{0:T(128)} %reshape_squeeze.3.cnt_ref, bf16[4,528,768]{2,1,0:T(8,128)(2,1)} %get-tuple-element.54.h_refs, bf16[4,512,768]{2,1,0:T(8,128)(2,1)} %get-tuple-element.55.g_refs, ...), custom_call_target="tpu_custom_call" | custom-call | tf_op jit(solution)/shard_map/experts/pallas_call | solution.py:1002
  303.2 2.1 dynamic-slice_bitcast_fusion.h2_ref
  305.3 133.5 %backward.1 = (f32[512,768]{1,0:T(8,128)}, bf16[512,768]{1,0:T(8,128)(2,1)}, f32[16,512]{1,0:T(8,128)}, f32[24,768]{1,0:T(8,128)}, bf16[512,768]{1,0:T(8,128)(2,...) custom-call(bf16[4,528,768]{2,1,0:T(8,128)(2,1)} %get-tuple-element.57.back_ref, ...), custom_call_target="tpu_custom_call" | custom-call | tf_op jit(solution)/shard_map/backward/pallas_call | solution.py:63
  438.8 78.6 %finish.1 = (bf16[512,768]{1,0:T(8,128)(2,1)}, bf16[512,768]{1,0:T(8,128)(2,1)}, f32[4,96,192]{2,1,0:T(8,128)}, f32[32,768]{1,0:T(8,128)}) custom-call(bf16[512,768]{1,0:T(8,128)(2,1)} %bitcast.59, bf16[512,768]{1,0:T(8,128)(2,1)} %get-tuple-element.50.x1_ref, bf16[512,768]{1,0:T(8,128)(2,1)} %get-tuple-element.51.x2_ref, ...), custom_call_target="tpu_custom_call" | custom-call | tf_op jit(solution)/shard_map/finish/pallas_call | solution.py:63
  520.1 1.4 slice_reduce_fusion.1
  521.5 1.7 slice_bitcast_fusion
  524.5 1.4 slice_bitcast_fusion.4
  526.0 2.5 copy.32
  530.0 3.7 reshape.99
  533.7 2.1 copy.35
  535.8 2.1 copy.36
  (63 shorter events, 18.6 us)
Async XLA Ops:
  7.2 81.4 %all-gather.3.cloned.1.call-start = ((), (), s32[]{:S(2)}) async-start(), calls=%async_computation.3 | async-start | bytes 5308416 | tf_op jit(solution)/shard_map/all_gather | solution.py:1063
  8.2 18.4 %collective-permute-start.1 = (bf16[96,4,192]{2,0,1:T(8,128)(2,1)S(1)}, bf16[96,4,192]{2,0,1:T(8,128)(2,1)S(1)}, u32[]{:S(2)}, u32[]{:S(2)}) collective-permute-start(bf16[96,4,192]{2,0,1:T(8,128)(2,1)S(1)} %get-tuple-element.97), channel_id=1, source_target_pairs={{0,2},{1,3},{2,0},{3,1},{4,6},{5,7},{6,4},{7,5},{8,10},{9,11},{10,... | collective-permute-start | bytes 442376 | tf_op jit(solution)/shard_map/ppermute | solution.py:1055
  12.3 14.2 %collective-permute-start.2 = (bf16[96,4,192]{2,0,1:T(8,128)(2,1)S(1)}, bf16[96,4,192]{2,0,1:T(8,128)(2,1)S(1)}, u32[]{:S(2)}, u32[]{:S(2)}) collective-permute-start(bf16[96,4,192]{2,0,1:T(8,128)(2,1)S(1)} %get-tuple-element.97), channel_id=1, source_target_pairs={{0,3},{1,2},{2,1},{3,0},{4,7},{5,6},{6,5},{7,4},{8,11},{9,10},{10,... | collective-permute-start | bytes 442376 | tf_op jit(solution)/shard_map/ppermute | solution.py:1055
  13.7 13.4 %collective-permute-start = (bf16[96,4,192]{2,0,1:T(8,128)(2,1)S(1)}, bf16[96,4,192]{2,0,1:T(8,128)(2,1)S(1)}, u32[]{:S(2)}, u32[]{:S(2)}) collective-permute-start(bf16[96,4,192]{2,0,1:T(8,128)(2,1)S(1)} %get-tuple-element.97), channel_id=1, source_target_pairs={{0,1},{1,0},{2,3},{3,2},{4,5},{5,4},{6,7},{7,6},{8,9},{9,8},{10,11... | collective-permute-start | bytes 442376 | tf_op jit(solution)/shard_map/ppermute | solution.py:1055
  27.3 2.7 copy-start.2
  30.0 191.4 %all-gather.5.cloned.1.call-start = ((), (), s32[]{:S(2)}) async-start(), calls=%async_computation.4 | async-start | bytes 21233664 | tf_op jit(solution)/shard_map/all_gather | solution.py:1065
  34.7 8.2 %copy-start.10 = (s32[1,8]{1,0:T(1,128)S(1)}, s32[1,8]{1,0:T(1,128)}, u32[]{:S(2)}) copy-start(s32[1,8]{1,0:T(1,128)} %param.18) | copy-start | bytes 100
  34.7 8.3 %copy-start.6 = (f32[2,768,2]{1,2,0:T(2,128)S(1)}, f32[2,768,2]{1,2,0:T(2,128)}, u32[]{:S(2)}) copy-start(f32[2,768,2]{1,2,0:T(2,128)} %param.28) | copy-start | bytes 36868
  34.7 8.4 %copy-start.8 = (f32[768]{0:T(1024)S(1)}, f32[768]{0:T(1024)}, u32[]{:S(2)}) copy-start(f32[768]{0:T(1024)} %param.25) | copy-start | bytes 9220
  34.7 9.0 %copy-start.9 = (f32[768]{0:T(1024)S(1)}, f32[768]{0:T(1024)}, u32[]{:S(2)}) copy-start(f32[768]{0:T(1024)} %param.26) | copy-start | bytes 9220
  34.7 9.5 %copy-start.4 = (f32[512,12]{0,1:T(8,128)S(1)}, f32[512,12]{0,1:T(8,128)}, u32[]{:S(2)}) copy-start(f32[512,12]{0,1:T(8,128)} %param.20) | copy-start | bytes 73732
  34.7 10.1 %copy-start.7 = (f32[2,768]{1,0:T(2,128)S(1)}, f32[2,768]{1,0:T(2,128)}, u32[]{:S(2)}) copy-start(f32[2,768]{1,0:T(2,128)} %param.29) | copy-start | bytes 18436
  34.7 11.4 %copy-start.3 = (f32[768,12]{0,1:T(8,128)S(1)}, f32[768,12]{0,1:T(8,128)}, u32[]{:S(2)}) copy-start(f32[768,12]{0,1:T(8,128)} %param.27) | copy-start | bytes 110596
  38.3 20.9 %all-to-all-start = ((bf16[8,64,768]{2,1,0:T(8,128)(2,1)}), bf16[8,64,768]{2,1,0:T(8,128)(2,1)S(1)}, u32[]{:S(2)}, u32[]{:S(2)}) async-start(bf16[8,64,768]{2,1,0:T(8,128)(2,1)} %bitcast.65), calls=%async_computation | async-start | bytes 1572864 | tf_op jit(solution)/shard_map/all_to_all | solution.py:1077
  59.1 8.9 %copy-start = (bf16[8,64,768]{2,1,0:T(8,128)(2,1)}, bf16[8,64,768]{2,1,0:T(8,128)(2,1)S(1)}, u32[]{:S(2)}) copy-start(bf16[8,64,768]{2,1,0:T(8,128)(2,1)S(1)} %all-to-all-done) | copy-start | bytes 2359300
  59.1 24.4 %all-to-all-start.1 = ((bf16[8,64,768]{2,1,0:T(8,128)(2,1)}), bf16[8,64,768]{2,1,0:T(8,128)(2,1)S(1)}, u32[]{:S(2)}, u32[]{:S(2)}) async-start(bf16[8,64,768]{2,1,0:T(8,128)(2,1)} %bitcast.64), calls=%async_computation.1 | async-start | bytes 1572864 | tf_op jit(solution)/shard_map/all_to_all | solution.py:1078
  62.7 463.3 %reduce-scatter.2.cloned.1.call-start = ((), (), s32[]{:S(2)}) async-start(), calls=%async_computation.5 | async-start | bytes 21233664 | tf_op jit(solution)/shard_map/reduce_scatter | solution.py:1099
  83.5 0.9 copy-start.1
  438.8 85.1 %copy-start.5 = (f32[16,512]{1,0:T(8,128)S(1)}, f32[16,512]{1,0:T(8,128)}, u32[]{:S(2)}) copy-start(f32[16,512]{1,0:T(8,128)} %get-tuple-element.80) | copy-start | bytes 98308
Sparse Core Ops, SparseCore 0:
  30.1 58.4 all-gather.2
  91.1 98.5 all-gather.4
  303.3 144.2 reduce-scatter.1
